TPU v7x, 512 devices: a whole 4x4x16 slice. The times are simulated.
512 devices in a mesh: member: 8 (over z_lo, core), grid: 64 (over z_hi, y, x).
Axes of the slice: x: 4, y: 4, z: 16 (z_hi: 4, z_lo: 4; z = z_hi * 4 + z_lo), core: 2. Of those that a mesh axis runs over, the one named last changes fastest.
Arguments:
- states: bfloat16 [8, 8192, 1024], P('member', 'grid'), may hold values from -16 to 16
- norm_scale_vector: float32 [1024], replicated, may hold values from 0.1 to 1.9
- query_weight: bfloat16 [1024, 512], P('grid'), may hold values from -2 to 2
- key_weight: bfloat16 [1024, 512], P('grid'), may hold values from -2 to 2
- value_weight: bfloat16 [1024, 512], P('grid'), may hold values from -0.1875 to 0.1875
- output_weight: bfloat16 [512, 1024], P('grid'), may hold values from -0.25 to 0.25
- head_weight: bfloat16 [1024, 128], P('grid'), may hold values from -0.5 to 0.5
- neighbours: int32 [8192, 8], P('grid'), may hold values from 0 to 8191, as said below
- observed: float32 [8192, 128], P('grid'), may hold values from -16 to 16
Outputs:
- grad_input: bfloat16 [8, 8192, 1024], P('member', 'grid')
- grad_mixing: float32 [512, 1024], P('grid')
- grad_head: float32 [1024, 128], P('grid')
- grad_key_value: float32 [8, 8192, 1024], P('member', 'grid')
Inputs may be any that keep to these rules, and one draw needn't show every extreme that they name: `neighbours`: the first neighbour of every point is the point itself; every neighbour index lies within 32 positions of the point's own index, and that distance occurs.
All inputs are finite; a program needn't handle non-finite values.
Results may differ from a plain program's by a relative error of at most 0.035.
Values may be sent and summed in bfloat16 or wider, within the bound.
No kernel may reach another device: no remote copies, remote signals or barrier semaphores. Data moves between devices by JAX's collectives and lax.ppermute only.
A program may use at most 64 MiB of HBM per device.

v0:
```python
import math

import jax
import jax.numpy as jnp
from jax import lax
from jax.sharding import PartitionSpec as P

HEADS = 8
HDIM = 64
KNB = 8
HALO = 32


epsilon = 1e-05
smooth = 0.1


def in_order(blocks, dim):
    blocks = jnp.moveaxis(blocks, 0, dim)
    dims = blocks.shape
    return blocks.reshape(*dims[:dim], dims[dim] * dims[dim + 1], *dims[dim + 2 :])


def gather_together(arrays, axis, dims):
    ravelled = jnp.concatenate([a.reshape(-1) for a in arrays])
    lines, at, done = (lax.all_gather(ravelled, axis), 0, [])
    for a, dim in zip(arrays, dims):
        blocks = lines[:, at : at + a.size].reshape(-1, *a.shape)
        done.append(in_order(blocks, dim))
        at += a.size
    return tuple(done)


def extended_2(x, sides, width):
    for axis, dim in sides:
        devices, length = (lax.axis_size(axis), x.shape[dim])
        up = [(i, (i + 1) % devices) for i in range(devices - 1)]
        down = [(j, i) for i, j in up]
        last = lax.slice_in_dim(x, length - width, length, axis=dim)
        leading = lax.slice_in_dim(x, 0, width, axis=dim)
        before = lax.ppermute(last, axis, up)
        after = lax.ppermute(leading, axis, down)
        x = jnp.concatenate([before, x, after], axis=dim)
    return x


def sent_to_all(x, axis):
    devices = lax.axis_size(axis)
    return lax.all_to_all(jnp.broadcast_to(x[None], (devices, *x.shape)), axis, 0, 0, tiled=True)


def gather_directly(x, axis, dim):
    blocks = sent_to_all(x, axis)
    return in_order(blocks, dim)


def passed_along(block, axis, distance):
    devices = range(lax.axis_size(axis))
    route = [(i - distance, i) for i in devices if i - distance in devices]
    return lax.ppermute(block, axis, route)


def cut_along(x, dim, devices):
    before, after = (x.shape[:dim], x.shape[dim + 1 :])
    return jnp.moveaxis(x.reshape(*before, devices, -1, *after), dim, 0)


def sum_at_owner(x, axis, dim):
    blocks = cut_along(x, dim, lax.axis_size(axis))
    arrived = lax.all_to_all(blocks, axis, split_axis=0, concat_axis=0, tiled=True)
    return arrived.sum(axis=0)


def taken_together(x, axis):
    return sent_to_all(x, axis).astype(jnp.float32).sum(axis=0)


def layer_norm(states):
    values = states.astype(jnp.float32)
    center = values - jnp.mean(values, axis=-1, keepdims=True)
    inverse_spread = lax.rsqrt(jnp.mean(center * center, axis=-1, keepdims=True) + epsilon)
    return (center * inverse_spread, inverse_spread)


def gradient_of(spread):
    return spread / jnp.sqrt(spread * spread + smooth * smooth)


def attend(query_rows, gathered):
    number = query_rows.shape[0]
    inner_width = query_rows.shape[1]
    query_heads = query_rows.reshape(number, HEADS, HDIM)
    key_heads = gathered[:, :, :inner_width].reshape(number, KNB, HEADS, HDIM)
    value_heads = gathered[:, :, inner_width:].reshape(number, KNB, HEADS, HDIM)
    scores = jnp.einsum(
        "rhe,rkhe->rhk", query_heads, key_heads, preferred_element_type=jnp.float32
    ) * (1.0 / math.sqrt(HDIM))
    highest = jnp.max(scores, axis=-1, keepdims=True)
    exponent = jnp.exp(scores - highest)
    attention = exponent / jnp.sum(exponent, axis=-1, keepdims=True)
    attention_cast = attention.astype(jnp.bfloat16)
    attended_rows = jnp.einsum(
        "rhk,rkhe->rhe", attention_cast, value_heads, preferred_element_type=jnp.float32
    )
    return (
        attended_rows.reshape(number, inner_width).astype(jnp.bfloat16),
        attention,
        attention_cast,
    )


def attend_back(query_rows, gathered, attention, attention_cast, grad_mixed):
    number = query_rows.shape[0]
    inner_width = query_rows.shape[1]
    query_heads = query_rows.reshape(number, HEADS, HDIM)
    key_heads = gathered[:, :, :inner_width].reshape(number, KNB, HEADS, HDIM)
    value_heads = gathered[:, :, inner_width:].reshape(number, KNB, HEADS, HDIM)
    grad_heads = grad_mixed.reshape(number, HEADS, HDIM)
    grad_prob = jnp.einsum(
        "rhe,rkhe->rhk", grad_heads, value_heads, preferred_element_type=jnp.float32
    )
    grad_score = (
        attention
        * (grad_prob - jnp.sum(attention * grad_prob, axis=-1, keepdims=True))
        * (1.0 / math.sqrt(HDIM))
    )
    grad_query = jnp.einsum(
        "rhk,rkhe->rhe", grad_score, key_heads, preferred_element_type=jnp.float32
    )
    grad_keys = jnp.einsum(
        "rhk,rhe->rkhe", grad_score, query_heads, preferred_element_type=jnp.float32
    )
    grad_values = jnp.einsum(
        "rhk,rhe->rkhe", attention_cast, grad_heads, preferred_element_type=jnp.float32
    )
    returned = jnp.concatenate(
        [
            grad_keys.reshape(number, KNB, inner_width),
            grad_values.reshape(number, KNB, inner_width),
        ],
        axis=-1,
    )
    return (grad_query.reshape(number, inner_width).astype(jnp.bfloat16), returned)


def transposed(left, right):
    return lax.dot_general(
        left, right, (((1,), (1,)), ((), ())), preferred_element_type=jnp.float32
    )


def shards(
    states,
    norm_scale_vector,
    query_weight,
    key_weight,
    value_weight,
    output_weight,
    head_weight,
    neighbours,
    observed,
):
    points = states.shape[1]
    inner_width = query_weight.shape[1]
    inputs = states[0]
    centred_rows, inverse_spread = layer_norm(inputs)
    normed = (centred_rows * norm_scale_vector).astype(jnp.bfloat16)
    full_query, full_key, full_value, full_out, complete_head = gather_together(
        (query_weight, key_weight, value_weight, output_weight, head_weight),
        "grid",
        (0, 0, 0, 0, 0),
    )
    query_rows = jnp.dot(normed, full_query, preferred_element_type=jnp.float32).astype(
        jnp.bfloat16
    )
    key_part = jnp.dot(normed, full_key, preferred_element_type=jnp.float32)
    value_part = jnp.dot(normed, full_value, preferred_element_type=jnp.float32)
    key_value_pair = jnp.concatenate(
        [key_part.astype(jnp.bfloat16), value_part.astype(jnp.bfloat16)], axis=1
    )
    extended = extended_2(key_value_pair, (("grid", 0),), HALO)
    local_rows = neighbours - (lax.axis_index("grid") * points - HALO)
    gathered = jnp.take(extended, local_rows, axis=0)
    attended_rows, attention, attention_cast = attend(query_rows, gathered)
    residual = inputs.astype(jnp.float32)
    layer_output = (
        residual + jnp.dot(attended_rows, full_out, preferred_element_type=jnp.float32)
    ).astype(jnp.bfloat16)
    member_prediction = jnp.dot(layer_output, complete_head, preferred_element_type=jnp.float32)
    member_list = lax.axis_size("member")
    every_member = gather_directly(member_prediction[None], "member", 0)
    pairwise_total = jnp.sum(gradient_of(member_prediction[None] - every_member), axis=0)
    prediction_gradient = (
        gradient_of(member_prediction - observed) - pairwise_total / (member_list - 1)
    ).astype(jnp.bfloat16)
    grad_output = transposed(prediction_gradient, complete_head)
    output_cast = grad_output.astype(jnp.bfloat16)
    grad_mixed = transposed(output_cast, full_out).astype(jnp.bfloat16)
    grad_query, returned = attend_back(query_rows, gathered, attention, attention_cast, grad_mixed)
    margin = HALO
    summed = jax.ops.segment_sum(
        returned.reshape(points * KNB, 2 * inner_width),
        local_rows.reshape(points * KNB),
        num_segments=points + 2 * margin,
    )
    lower = summed[:margin]
    upper = summed[points + margin :]
    middle = summed[margin : points + margin]
    from_after = passed_along(lower.astype(jnp.bfloat16), "grid", -1).astype(lower.dtype)
    from_before = passed_along(upper.astype(jnp.bfloat16), "grid", 1).astype(upper.dtype)
    middle = middle.at[:margin].add(from_before)
    middle = middle.at[points - margin :].add(from_after)
    grad_keys = middle[:, :inner_width].astype(jnp.bfloat16)
    grad_values = middle[:, inner_width:].astype(jnp.bfloat16)
    back_query, back_key, back_value = (full_query, full_key, full_value)
    grad_normed = transposed(grad_query, back_query)
    grad_normed = grad_normed + transposed(grad_keys, back_key)
    grad_normed = grad_normed + transposed(grad_values, back_value)
    grad_centred = grad_normed * norm_scale_vector
    grad_states = inverse_spread * (
        grad_centred
        - jnp.mean(grad_centred, axis=-1, keepdims=True)
        - centred_rows * jnp.mean(grad_centred * centred_rows, axis=-1, keepdims=True)
    )
    grad_input = (grad_output + grad_states).astype(jnp.bfloat16)[None]
    columns = attended_rows
    factor_share = sum_at_owner(
        lax.dot_general(
            columns,
            prediction_gradient,
            (((0,), (0,)), ((), ())),
            preferred_element_type=jnp.float32,
        ),
        "grid",
        0,
    )
    mixing_share = lax.dot_general(
        factor_share,
        complete_head.astype(jnp.float32),
        (((1,), (1,)), ((), ())),
        precision=lax.Precision.HIGHEST,
    )
    columns = layer_output
    head_share = sum_at_owner(
        lax.dot_general(
            columns,
            prediction_gradient,
            (((0,), (0,)), ((), ())),
            preferred_element_type=jnp.float32,
        ),
        "grid",
        0,
    )
    mixing_total, head_total = (
        taken_together(mixing_share.astype(jnp.bfloat16), "member").astype(jnp.float32),
        taken_together(head_share.astype(jnp.bfloat16), "member").astype(jnp.float32),
    )
    scaling = 1.0 / math.sqrt(member_list * lax.axis_size("grid") * points)
    return (grad_input, mixing_total * scaling, head_total * scaling, middle[None])


def solution(mesh):
    return jax.shard_map(
        shards,
        mesh=mesh,
        in_specs=(
            P("member", "grid", None),
            P(),
            P("grid", None),
            P("grid", None),
            P("grid", None),
            P("grid", None),
            P("grid", None),
            P("grid", None),
            P("grid", None),
        ),
        out_specs=(
            P("member", "grid", None),
            P("grid", None),
            P("grid", None),
            P("member", "grid", None),
        ),
        check_vma=False,
    )
```

profile of v0, /device:TPU:1, one launch (start us, length us, event | category | flops | bytes accessed | tf_op | source)
XLA Modules:
  0.0 364.5 jit_solution(17949907621889207882)
XLA Ops:
  15.8 143.7 %all-gather.3.cloned.1.call-done = bf16[2228224]{0:T(1024)(128)(2,1)} async-done(((bf16[34816]{0:T(1024)(128)(2,1)}), bf16[2228224]{0:T(1024)(128)(2,1)}) %all-gather.3.cloned.1.call-update) | async-done | bytes 4456464 | tf_op jit(solution)/shard_map/all_gather | solution.py:26
  159.5 7.5 %reshape.233 = bf16[64,34816]{1,0:T(8,128)(2,1)} reshape(bf16[2228224]{0:T(1024)(128)(2,1)} %all-gather.3.cloned.1.call-done) | data formatting | bytes 8912896 | tf_op jit(solution)/shard_map/all_gather | solution.py:26
  166.9 4.0 %fusion.51 = (bf16[64,8192]{1,0:T(8,128)(2,1)}, bf16[64,8192]{1,0:T(8,128)(2,1)S(1)}, bf16[64,8192]{1,0:T(8,128)(2,1)S(1)}, bf16[64,8192]{1,0:T(8,128)(2,1)}) fusion(bf16[64,34816]{1,0:T(8,128)(2,1)} %reshape.233), kind=kLoop, calls=%fused_computation.95 | loop fusion | bytes 8388608 | tf_op jit(solution)/shard_map/slice | solution.py:28
  174.8 4.3 %collective-permute-start = (bf16[32,1024]{1,0:T(8,128)(2,1)}, bf16[32,1024]{1,0:T(8,128)(2,1)}, u32[]{:S(2)}, u32[]{:S(2)}) collective-permute-start(bf16[32,1024]{1,0:T(8,128)(2,1)} %get-tuple-element.40), channel_id=1, source_target_pairs={{0,1},{1,2},{2,3},{3,4},{4,5},{5,6},{6,7},{7,8},{8,9},{9,10},{10,1... | collective-permute-start | bytes 196616 | tf_op jit(solution)/shard_map/ppermute | solution.py:41
  187.9 5.4 %gather_fusion = bf16[1024,1024]{1,0:T(8,128)(2,1)} fusion(bf16[192,1024]{1,0:T(8,128)(2,1)S(1)} %pad_maximum_fusion, s32[1024]{0:T(1024)S(1)} %broadcast_clamp_fusion), kind=kCustom, calls=%fused_computation | custom fusion | bytes 4198400 | tf_op jit(solution)/shard_map/jit(_take)/gather | solution.py:183
  193.2 4.2 %copy.30 = bf16[128,8,1024]{0,2,1:T(8,128)(2,1)} copy(bf16[128,8,1024]{2,1,0:T(8,128)(2,1)} %bitcast.106) | data formatting | bytes 4194304 | tf_op jit(solution)/shard_map/jit(_take)/gather | solution.py:183
  202.8 2.2 convert_convert_fusion
  207.5 4.6 %all-to-all-start = ((f32[8,1,128,128]{3,2,1,0:T(8,128)}), f32[8,1,128,128]{3,2,1,0:T(8,128)S(1)}, u32[]{:S(2)}, u32[]{:S(2)}) async-start(f32[8,1,128,128]{3,2,1,0:T(8,128)} %broadcast_in_dim.27), calls=%async_computation | async-start | bytes 1048576 | tf_op jit(solution)/shard_map/all_to_all | solution.py:49
  213.4 13.1 %all-to-all-done = f32[8,1,128,128]{3,2,1,0:T(8,128)S(1)} async-done(((f32[8,1,128,128]{3,2,1,0:T(8,128)}), f32[8,1,128,128]{3,2,1,0:T(8,128)S(1)}, u32[]{:S(2)}, u32[]{:S(2)}) %all-to-all-start) | async-done | bytes 524320 | tf_op jit(solution)/shard_map/all_to_all | solution.py:49
  226.7 2.1 fusion.56
  229.7 20.2 %all-to-all-start.1 = ((f32[64,8,128]{2,1,0:T(8,128)}), f32[64,8,128]{2,1,0:T(8,128)}, u32[]{:S(2)}, u32[]{:S(2)}) async-start(f32[64,8,128]{2,1,0:T(8,128)} %fusion.40), calls=%async_computation.1 | async-start | bytes 524288 | tf_op jit(solution)/shard_map/all_to_all | solution.py:70
  254.8 3.2 multiply_bitcast_fusion.1
  258.0 3.5 concatenate.24
  261.5 3.2 multiply_bitcast_fusion
  264.7 4.8 %concatenate.25 = f32[1024,512]{1,0:T(8,128)} reshape(f32[128,8,8,64]{3,2,1,0:T(8,128)} %multiply_bitcast_fusion) | data formatting | bytes 4194304 | tf_op jit(solution)/shard_map/concatenate | solution.py:136
  269.5 9.9 %scatter_custom_fusion = f32[192,1024]{1,0:T(8,128)S(1)} fusion(s32[1024]{0:T(1024)S(1)} %reshape.227, f32[1024,512]{1,0:T(8,128)} %concatenate.25, f32[]{:T(128)} %constant.99.clone.1, f32[1024,512]{1,0:T(8,128)S(1)} %concatenate.24, f32[]{:T(128)} %constant.88.clone.1), kind=kCustom, calls=%fused_computation.5 | custom fusion | flops 2097152 | bytes 4980744 | tf_op jit(solution)/shard_map/scatter-add | solution.py:201
  282.3 4.5 %all-to-all-start.2 = ((bf16[8,8,1024]{2,1,0:T(8,128)(2,1)}), bf16[8,8,1024]{2,1,0:T(8,128)(2,1)S(1)}, u32[]{:S(2)}, u32[]{:S(2)}) async-start(bf16[8,8,1024]{2,1,0:T(8,128)(2,1)} %broadcast_in_dim.54), calls=%async_computation.2 | async-start | bytes 262144 | tf_op jit(solution)/shard_map/all_to_all | solution.py:49
  288.4 2.9 collective-permute-start.2
  291.3 2.0 fusion.58
  293.3 17.1 %all-to-all-start.3 = ((f32[64,16,128]{2,1,0:T(8,128)}), f32[64,16,128]{2,1,0:T(8,128)}, u32[]{:S(2)}, u32[]{:S(2)}) async-start(f32[64,16,128]{2,1,0:T(8,128)} %bitcast.109), calls=%async_computation.3 | async-start | bytes 1048576 | tf_op jit(solution)/shard_map/all_to_all | solution.py:70
  312.8 4.1 %collective-permute-done.3 = bf16[32,1024]{1,0:T(8,128)(2,1)S(1)} collective-permute-done((bf16[32,1024]{1,0:T(8,128)(2,1)S(1)}, bf16[32,1024]{1,0:T(8,128)(2,1)S(1)}, u32[]{:S(2)}, u32[]{:S(2)}) %collective-permute-start.3) | collective-permute-done | bytes 65568 | tf_op jit(solution)/shard_map/ppermute | solution.py:60
  319.1 12.9 %all-to-all-done.3 = f32[64,16,128]{2,1,0:T(8,128)} async-done(((f32[64,16,128]{2,1,0:T(8,128)}), f32[64,16,128]{2,1,0:T(8,128)}, u32[]{:S(2)}, u32[]{:S(2)}) %all-to-all-start.3) | async-done | bytes 524320 | tf_op jit(solution)/shard_map/all_to_all | solution.py:70
  333.7 18.3 %all-to-all-start.4 = ((bf16[8,16,128]{2,1,0:T(8,128)(2,1)}), bf16[8,16,128]{2,1,0:T(8,128)(2,1)S(1)}, u32[]{:S(2)}, u32[]{:S(2)}) async-start(bf16[8,16,128]{2,1,0:T(8,128)(2,1)} %broadcast_in_dim.55), calls=%async_computation.4 | async-start | bytes 65536 | tf_op jit(solution)/shard_map/all_to_all | solution.py:49
  352.7 4.4 %all-to-all-done.4 = bf16[8,16,128]{2,1,0:T(8,128)(2,1)S(1)} async-done(((bf16[8,16,128]{2,1,0:T(8,128)(2,1)}), bf16[8,16,128]{2,1,0:T(8,128)(2,1)S(1)}, u32[]{:S(2)}, u32[]{:S(2)}) %all-to-all-start.4) | async-done | bytes 32800 | tf_op jit(solution)/shard_map/all_to_all | solution.py:49
  (149 shorter events, 47.8 us)
Async XLA Ops:
  7.2 152.3 %all-gather.3.cloned.1.call-start = ((), (), s32[]{:S(2)}) async-start(), calls=%async_computation.5 | async-start | bytes 4526080 | tf_op jit(solution)/shard_map/all_gather | solution.py:26
  172.0 9.9 %copy-start.9 = (bf16[1024,512]{1,0:T(8,128)(2,1)}, bf16[1024,512]{1,0:T(8,128)(2,1)S(1)}, u32[]{:S(2)}) copy-start(bf16[1024,512]{1,0:T(8,128)(2,1)S(1)} %reshape_reshape.16) | copy-start | bytes 3145732
  174.1 6.3 %copy-start.22 = (bf16[128,512]{1,0:T(8,128)(2,1)}, bf16[128,512]{1,0:T(8,128)(2,1)S(1)}, u32[]{:S(2)}) copy-start(bf16[128,512]{1,0:T(8,128)(2,1)S(1)} %convolution_convert_fusion.2) | copy-start | bytes 393220
  174.8 12.1 %collective-permute-start = (bf16[32,1024]{1,0:T(8,128)(2,1)}, bf16[32,1024]{1,0:T(8,128)(2,1)}, u32[]{:S(2)}, u32[]{:S(2)}) collective-permute-start(bf16[32,1024]{1,0:T(8,128)(2,1)} %get-tuple-element.40), channel_id=1, source_target_pairs={{0,1},{1,2},{2,3},{3,4},{4,5},{5,6},{6,7},{7,8},{8,9},{9,10},{10,1... | collective-permute-start | bytes 196616 | tf_op jit(solution)/shard_map/ppermute | solution.py:41
  179.1 7.9 %collective-permute-start.1 = (bf16[32,1024]{1,0:T(8,128)(2,1)}, bf16[32,1024]{1,0:T(8,128)(2,1)}, u32[]{:S(2)}, u32[]{:S(2)}) collective-permute-start(bf16[32,1024]{1,0:T(8,128)(2,1)} %get-tuple-element.41), channel_id=1, source_target_pairs={{1,0},{2,1},{3,2},{4,3},{5,4},{6,5},{7,6},{8,7},{9,8},{10,9},{11,1... | collective-permute-start | bytes 196616 | tf_op jit(solution)/shard_map/ppermute | solution.py:42
  180.4 5.2 %slice-start = ((bf16[64,34816]{1,0:T(8,128)(2,1)}), bf16[64,2048]{1,0:T(8,128)(2,1)S(1)}, s32[]{:S(2)}) async-start(bf16[64,34816]{1,0:T(8,128)(2,1)} %reshape.233), calls=%async_computation.6 | async-start | bytes 524288 | tf_op jit(solution)/shard_map/slice | solution.py:28
  206.1 6.2 %copy-start.16 = (f32[128,8,64]{0,2,1:T(8,128)S(1)}, f32[128,8,64]{0,2,1:T(8,128)}, u32[]{:S(2)}) copy-start(f32[128,8,64]{0,2,1:T(8,128)} %bitcast_convert_fusion.1) | copy-start | bytes 786436
  206.5 20.2 %copy-start.17 = (bf16[128,1024]{1,0:T(8,128)(2,1)}, bf16[128,1024]{1,0:T(8,128)(2,1)S(1)}, u32[]{:S(2)}) copy-start(bf16[128,1024]{1,0:T(8,128)(2,1)S(1)} %fusion.14) | copy-start | bytes 786436
  206.5 20.2 %copy-start.27 = (f32[128,128]{1,0:T(8,128)S(1)}, f32[128,128]{1,0:T(8,128)}, u32[]{:S(2)}) copy-start(f32[128,128]{1,0:T(8,128)} %param.21) | copy-start | bytes 196612
  207.5 19.0 %all-to-all-start = ((f32[8,1,128,128]{3,2,1,0:T(8,128)}), f32[8,1,128,128]{3,2,1,0:T(8,128)S(1)}, u32[]{:S(2)}, u32[]{:S(2)}) async-start(f32[8,1,128,128]{3,2,1,0:T(8,128)} %broadcast_in_dim.27), calls=%async_computation | async-start | bytes 1048576 | tf_op jit(solution)/shard_map/all_to_all | solution.py:49
  226.7 24.9 %copy-start.1 = (bf16[128,8,1024]{0,2,1:T(8,128)(2,1)S(1)}, bf16[128,8,1024]{0,2,1:T(8,128)(2,1)}, u32[]{:S(2)}) copy-start(bf16[128,8,1024]{0,2,1:T(8,128)(2,1)} %copy-done) | copy-start | bytes 6291460
  229.7 50.5 %all-to-all-start.1 = ((f32[64,8,128]{2,1,0:T(8,128)}), f32[64,8,128]{2,1,0:T(8,128)}, u32[]{:S(2)}, u32[]{:S(2)}) async-start(f32[64,8,128]{2,1,0:T(8,128)} %fusion.40), calls=%async_computation.1 | async-start | bytes 524288 | tf_op jit(solution)/shard_map/all_to_all | solution.py:70
  269.5 11.9 %copy-start.6 = (bf16[1024,128]{1,0:T(8,128)(2,1)S(1)}, bf16[1024,128]{1,0:T(8,128)(2,1)}, u32[]{:S(2)}) copy-start(bf16[1024,128]{1,0:T(8,128)(2,1)} %reshape_reshape.19) | copy-start | bytes 786436
  279.4 11.9 %copy-start.25 = (bf16[128,128]{1,0:T(8,128)(2,1)S(1)}, bf16[128,128]{1,0:T(8,128)(2,1)}, u32[]{:S(2)}) copy-start(bf16[128,128]{1,0:T(8,128)(2,1)} %copy-done.24) | copy-start | bytes 98308
  279.4 31.1 %copy-start.4 = (bf16[128,8,512]{0,2,1:T(8,128)(2,1)S(1)}, bf16[128,8,512]{0,2,1:T(8,128)(2,1)}, u32[]{:S(2)}) copy-start(bf16[128,8,512]{0,2,1:T(8,128)(2,1)} %get-tuple-element.31) | copy-start | bytes 3145732
  280.2 30.6 %copy-start.12 = (bf16[1024,512]{1,0:T(8,128)(2,1)S(1)}, bf16[1024,512]{1,0:T(8,128)(2,1)}, u32[]{:S(2)}) copy-start(bf16[1024,512]{1,0:T(8,128)(2,1)} %copy-done.11) | copy-start | bytes 3145732
  282.3 11.0 %all-to-all-start.2 = ((bf16[8,8,1024]{2,1,0:T(8,128)(2,1)}), bf16[8,8,1024]{2,1,0:T(8,128)(2,1)S(1)}, u32[]{:S(2)}, u32[]{:S(2)}) async-start(bf16[8,8,1024]{2,1,0:T(8,128)(2,1)} %broadcast_in_dim.54), calls=%async_computation.2 | async-start | bytes 262144 | tf_op jit(solution)/shard_map/all_to_all | solution.py:49
  288.4 24.4 %collective-permute-start.2 = (bf16[32,1024]{1,0:T(8,128)(2,1)}, bf16[32,1024]{1,0:T(8,128)(2,1)S(1)}, u32[]{:S(2)}, u32[]{:S(2)}) collective-permute-start(bf16[32,1024]{1,0:T(8,128)(2,1)} %get-tuple-element.39), channel_id=1, source_target_pairs={{0,1},{1,2},{2,3},{3,4},{4,5},{5,6},{6,7},{7,8},{8,9},{9,10},{10,1... | collective-permute-start | bytes 196616 | tf_op jit(solution)/shard_map/ppermute | solution.py:60
  293.3 38.7 %all-to-all-start.3 = ((f32[64,16,128]{2,1,0:T(8,128)}), f32[64,16,128]{2,1,0:T(8,128)}, u32[]{:S(2)}, u32[]{:S(2)}) async-start(f32[64,16,128]{2,1,0:T(8,128)} %bitcast.109), calls=%async_computation.3 | async-start | bytes 1048576 | tf_op jit(solution)/shard_map/all_to_all | solution.py:70
  310.8 6.2 %copy-start.10 = (bf16[1024,512]{1,0:T(8,128)(2,1)S(1)}, bf16[1024,512]{1,0:T(8,128)(2,1)}, u32[]{:S(2)}) copy-start(bf16[1024,512]{1,0:T(8,128)(2,1)} %copy-done.9) | copy-start | bytes 3145732
  311.3 6.2 %copy-start.8 = (bf16[1024,512]{1,0:T(8,128)(2,1)S(1)}, bf16[1024,512]{1,0:T(8,128)(2,1)}, u32[]{:S(2)}) copy-start(bf16[1024,512]{1,0:T(8,128)(2,1)} %copy-done.7) | copy-start | bytes 3145732
  311.3 6.2 %copy-start.31 = (f32[128]{0:T(128)S(1)}, f32[128]{0:T(128)}, u32[]{:S(2)}) copy-start(f32[128]{0:T(128)} %add_rsqrt_fusion) | copy-start | bytes 1540
  311.4 5.5 %collective-permute-start.3 = (bf16[32,1024]{1,0:T(8,128)(2,1)S(1)}, bf16[32,1024]{1,0:T(8,128)(2,1)S(1)}, u32[]{:S(2)}, u32[]{:S(2)}) collective-permute-start(bf16[32,1024]{1,0:T(8,128)(2,1)S(1)} %copy-done.28), channel_id=1, source_target_pairs={{1,0},{2,1},{3,2},{4,3},{5,4},{6,5},{7,6},{8,7},{9,8},{10,9},{11,1... | collective-permute-start | bytes 196616 | tf_op jit(solution)/shard_map/ppermute | solution.py:60
  333.7 23.3 %all-to-all-start.4 = ((bf16[8,16,128]{2,1,0:T(8,128)(2,1)}), bf16[8,16,128]{2,1,0:T(8,128)(2,1)S(1)}, u32[]{:S(2)}, u32[]{:S(2)}) async-start(bf16[8,16,128]{2,1,0:T(8,128)(2,1)} %broadcast_in_dim.55), calls=%async_computation.4 | async-start | bytes 65536 | tf_op jit(solution)/shard_map/all_to_all | solution.py:49
  (20 other events, 45.6 us)
Sparse Core Ops, SparseCore 0:
  12.7 146.7 all-gather.2
where the time goes:
time: 366 us; the launch traced here: 365 us
  waiting for transfers between devices  178 us (49%)
  starting transfers between devices  74.7 us (20%)
  local copies, waits for them, and re-layouts  48.5 us (13%)
  other arithmetic  35.8 us (10%)
  between operations  14.7 us (4%)
  matrix products  12.6 us (3%)
    all_gather x1, waiting for transfers between devices, gather_together(): lines, at, done = (lax.all_gather(ravelled, axis), 0, [])  144 us
    all_to_all x2, starting transfers between devices, sum_at_owner(): lax.all_to_all(blocks, axis, split_axis=0, concat_axis=0, tiled=True)  37.4 us
    all_to_all x3, starting transfers between devices, sent_to_all(): lax.all_to_all(jnp.broadcast_to(x[None], (devices, *x.shape)), axis, 0, 0...  27.4 us
    all_to_all x3, waiting for transfers between devices, sent_to_all(): lax.all_to_all(jnp.broadcast_to(x[None], (devices, *x.shape)), axis, 0, 0...  17.5 us
    all_to_all x2, waiting for transfers between devices, sum_at_owner(): lax.all_to_all(blocks, axis, split_axis=0, concat_axis=0, tiled=True)  12.9 us
    scatter-add x1, other arithmetic, shards(): jax.ops.segment_sum(returned.reshape(points * KNB, 2 * inner_width), loca...  9.9 us
    gather x2, local copies, waits for them, and re-layouts, shards(): gathered = jnp.take(extended, local_rows, axis=0)  9.54 us
    concatenate x2, local copies, waits for them, and re-layouts, attend_back(): jnp.concatenate([grad_keys.reshape(number, KNB, inner_width), grad_values...  8.29 us
  transfers between devices with their start and end apart: 10, of which 5 were waited for; matrix products, arithmetic and copies ran while one was open for 13% of the time, Pallas kernels for 0%

commit v1 on v0

v1 whole, which is shorter than its diff:
```python
import functools
import math

import jax
import jax.numpy as jnp
from jax import lax
from jax.experimental import pallas as pl
from jax.experimental.pallas import tpu as pltpu
from jax.sharding import Mesh, PartitionSpec as P

HEADS = 8
HDIM = 64
KNB = 8
HALO = 32
PTS = 128
EXT = PTS + 2 * HALO
D = 1024
HD = 512
NVAR = 128
LANE = 128

epsilon = 1e-05
smooth = 0.1

MEMBER = ("zl", "core")
GRID = ("zh", "y", "x")
PLANE = ("y", "x")
COLUMN = ("zl", "core", "zh")

BF = jnp.bfloat16
F32 = jnp.float32
VM = pl.BlockSpec(memory_space=pltpu.VMEM)
SM = pl.BlockSpec(memory_space=pltpu.SMEM)
HB = pl.BlockSpec(memory_space=pl.ANY)


def nn(a, b):
    return lax.dot_general(a, b, (((1,), (0,)), ((), ())), preferred_element_type=F32)


def nt(a, b):
    return lax.dot_general(a, b, (((1,), (1,)), ((), ())), preferred_element_type=F32)


def tn(a, b):
    return lax.dot_general(a, b, (((0,), (0,)), ((), ())), preferred_element_type=F32)


def call(body, outs, args, specs=None, scratch=(), cost=(1e9, 4e6), limit=40 << 20):
    return pl.pallas_call(
        body,
        out_shape=tuple(jax.ShapeDtypeStruct(s, d) for s, d in outs),
        in_specs=list(specs) if specs is not None else [VM] * len(args),
        out_specs=tuple(VM for _ in outs),
        scratch_shapes=list(scratch),
        compiler_params=pltpu.CompilerParams(vmem_limit_bytes=limit),
        cost_estimate=pl.CostEstimate(
            flops=int(cost[0]), bytes_accessed=int(cost[1]), transcendentals=0
        ),
    )(*args)


def normalised(rows):
    values = rows.astype(F32)
    center = values - jnp.mean(values, axis=-1, keepdims=True)
    inverse = lax.rsqrt(jnp.mean(center * center, axis=-1, keepdims=True) + epsilon)
    return center * inverse, inverse


def prepare_body(before, own, after, scale, rel, normed, count):
    for part, at in ((before, 0), (own, HALO), (after, HALO + PTS)):
        centred, _ = normalised(part[...])
        normed[at : at + part.shape[0], :] = (centred * scale[...]).astype(BF)
    place = lax.broadcasted_iota(jnp.int32, (PTS, EXT), 1)
    total = jnp.zeros((PTS, EXT), F32)
    for k in range(KNB):
        total = total + (place == rel[:, k : k + 1]).astype(F32)
    count[...] = total


def halves(tile_shape, head):
    lane = lax.broadcasted_iota(jnp.int32, tile_shape, 1)
    return (lane < HDIM) if head == 0 else (lane >= HDIM)


def forward_body(
    zh_n, rs, ro, core, normed, states, count, own, other,
    wqkv, wout, whead, q, kv, probs, mixed, out, fore, sq, so, sh,
):
    pn = wqkv.shape[0] // zh_n
    qrows = 6 * rs
    orows = 4 * ro

    def pieces(buf, c):
        for zh in range(zh_n):
            at = pl.ds(zh * pn, pn)
            for t in range(6):
                yield (
                    buf.at[:, zh, pl.ds(t * rs, rs), :],
                    wqkv.at[at, :, pl.ds((6 * c + t) * LANE, LANE)],
                    sq.at[c, zh, t],
                )
            for t in range(4):
                yield (
                    buf.at[:, zh, pl.ds(qrows + t * ro, ro), :],
                    wout.at[at, :, pl.ds((4 * c + t) * LANE, LANE)],
                    so.at[c, zh, t],
                )
            yield (
                buf.at[:, zh, pl.ds(qrows + orows, rs // 2), :],
                whead.at[at, c],
                sh.at[c, zh],
            )

    def begin(a, b):
        for src, dst, sem in pieces(a, 0):
            pltpu.make_async_copy(src, dst, sem).start()
        for src, dst, sem in pieces(b, 1):
            pltpu.make_async_copy(src, dst, sem).start()

    @pl.when(core[0] == 0)
    def _():
        begin(own, other)

    @pl.when(core[0] != 0)
    def _():
        begin(other, own)

    for c in range(2):
        for src, dst, sem in pieces(own, c):
            pltpu.make_async_copy(src, dst, sem).wait()

    rows = normed[...]
    weights = wqkv[...].reshape(D, 3 * HD)
    q[...] = nn(rows[HALO : HALO + PTS], weights[:, :HD]).astype(BF)
    kv[...] = nn(rows, weights[:, HD:]).astype(BF)
    times = count[...]
    here = times > 0
    for pair in range(HEADS // 2):
        at = pl.ds(pair * LANE, LANE)
        q2, k2, v2 = q[:, at], kv[:, at], kv[:, pl.ds(HD + pair * LANE, LANE)]
        got = []
        for side in range(2):
            chosen = jnp.where(halves((PTS, LANE), side), q2, jnp.zeros_like(q2))
            score = nt(chosen, k2) * (1.0 / math.sqrt(HDIM))
            score = jnp.where(here, score, -1e30)
            highest = jnp.max(score, axis=-1, keepdims=True)
            power = jnp.exp(score - highest)
            prob = power / jnp.sum(times * power, axis=-1, keepdims=True)
            prob = prob.astype(BF)
            probs[2 * pair + side] = prob
            got.append(nn((times * prob.astype(F32)).astype(BF), v2))
        mixed[:, at] = jnp.where(halves((PTS, LANE), 0), got[0], got[1]).astype(BF)
    flat_out = wout[...].astype(F32).reshape(HD, D).astype(BF)
    flat_head = whead[...].astype(F32).reshape(D, NVAR).astype(BF)
    layer = (states[...].astype(F32) + nn(mixed[...], flat_out)).astype(BF)
    out[...] = layer
    fore[...] = nn(layer, flat_head)


def slope(z):
    return z * lax.rsqrt(z * z + smooth * smooth)


def score_body(members, zh_n, every, fore, observed, mixed, out, gf, wg):
    mine = fore[...]
    total = jnp.zeros_like(mine)
    for m in range(members):
        total = total + slope(mine - every[m])
    grad = (slope(mine - observed[...]) - total * (1.0 / (members - 1))).astype(BF)
    gf[...] = grad
    pn = wg.shape[0]
    heads = tn(out[...], grad)
    factor = tn(mixed[...], grad)
    rb, ra = D // (zh_n * pn), HD // (zh_n * pn)
    for zh in range(zh_n):
        wg[:, zh, 0:rb, :] = (
            heads[zh * pn * rb : (zh + 1) * pn * rb].reshape(pn, rb, NVAR).astype(BF)
        )
        wg[:, zh, rb : rb + ra, :] = (
            factor[zh * pn * ra : (zh + 1) * pn * ra].reshape(pn, ra, NVAR).astype(BF)
        )


def backward_body(gf, whead, wout, q, kv, probs, count, gq, mid, lower, upper):
    flat_out = wout[...].astype(F32).reshape(HD, D).astype(BF)
    flat_head = whead[...].astype(F32).reshape(D, NVAR).astype(BF)
    go = nt(gf[...], flat_head).astype(BF)
    gm = nt(go, flat_out).astype(BF)
    times = count[...]
    for pair in range(HEADS // 2):
        at = pl.ds(pair * LANE, LANE)
        vat = pl.ds(HD + pair * LANE, LANE)
        q2, k2, v2 = q[:, at], kv[:, at], kv[:, vat]
        g2 = gm[:, pair * LANE : (pair + 1) * LANE]
        gqs, gks, gvs = [], [], []
        for side in range(2):
            chosen = jnp.where(halves((PTS, LANE), side), g2, jnp.zeros_like(g2))
            gp = nt(chosen, v2)
            weight = times * probs[2 * pair + side].astype(F32)
            centre = jnp.sum(weight * gp, axis=-1, keepdims=True)
            gs = (weight * (gp - centre) * (1.0 / math.sqrt(HDIM))).astype(BF)
            gqs.append(nn(gs, k2))
            gks.append(tn(gs, q2))
            gvs.append(tn(weight.astype(BF), g2))
        gq[:, at] = jnp.where(halves((PTS, LANE), 0), gqs[0], gqs[1]).astype(BF)
        pick = halves((EXT, LANE), 0)
        for where_at, parts in ((at, gks), (vat, gvs)):
            total = jnp.where(pick, parts[0], parts[1])
            lower[:, where_at] = total[:HALO].astype(BF)
            mid[:, where_at] = total[HALO : HALO + PTS]
            upper[:, where_at] = total[HALO + PTS :].astype(BF)


def final_body(states, scale, gf, whead, wqkv, gq, mid, first, last, total, grad):
    flat_head = whead[...].astype(F32).reshape(D, NVAR).astype(BF)
    total[...] = mid[...]
    total[:HALO, :] += first[...].astype(F32)
    total[PTS - HALO :, :] += last[...].astype(F32)
    kvs = total[...].astype(BF)
    weights = wqkv[...].reshape(D, 3 * HD)
    gn = nt(gq[...], weights[:, :HD]) + nt(kvs, weights[:, HD:])
    centred, inverse = normalised(states[...])
    g = gn * scale[...]
    back = inverse * (
        g
        - jnp.mean(g, axis=-1, keepdims=True)
        - centred * jnp.mean(g * centred, axis=-1, keepdims=True)
    )
    grad[...] = (nt(gf[...], flat_head) + back).astype(BF)


def weights_body(scaling, parts, whead, mixing, head):
    flat_head = whead[...].astype(F32).reshape(D, NVAR).astype(BF)
    rb = head.shape[0]
    total = jnp.zeros(parts.shape[1:], F32)
    for i in range(parts.shape[0]):
        total = total + parts[i].astype(F32)
    total = total * scaling
    head[...] = total[:rb]
    factor = total[rb:]
    high = factor.astype(BF)
    low = (factor - high.astype(F32)).astype(BF)
    mixing[...] = nt(high, flat_head) + nt(low, flat_head)


def to_all(x, axes):
    n = lax.axis_size(axes)
    return lax.all_to_all(
        jnp.broadcast_to(x[None], (n, *x.shape)), axes, 0, 0, tiled=True
    )


def packed_half(query, key, value, out, head, core):
    qkv = jnp.concatenate([query, key, value], axis=1)
    rs, ro = qkv.shape[0], out.shape[0]

    def half(c):
        cols = [qkv[:, (6 * c + t) * LANE : (6 * c + t + 1) * LANE] for t in range(6)]
        cols += [out[:, (4 * c + t) * LANE : (4 * c + t + 1) * LANE] for t in range(4)]
        cols += [head[c * rs // 2 : (c + 1) * rs // 2]]
        return jnp.concatenate(cols, axis=0)

    return jnp.where(core == 0, half(0), half(1))


def gathered_halves(mine):
    column = to_all(mine, "zh")
    plane = to_all(column, PLANE)
    return plane, lax.ppermute(plane, "core", [(0, 1), (1, 0)])


def shards(
    states, norm_scale, query, key, value, out_w, head_w, neighbours, observed
):
    members = lax.axis_size(MEMBER)
    devices = lax.axis_size(GRID)
    zh_n = lax.axis_size("zh")
    pn = lax.axis_size(PLANE)
    core = lax.axis_index("core")
    inputs = states[0]
    rs, ro = query.shape[0], out_w.shape[0]

    up = [(i, i + 1) for i in range(devices - 1)]
    down = [(j, i) for i, j in up]
    own, other = gathered_halves(
        packed_half(query, key, value, out_w, head_w, core)
    )
    before = lax.ppermute(inputs[PTS - HALO :], GRID, up)
    after = lax.ppermute(inputs[:HALO], GRID, down)
    rel = neighbours - (lax.axis_index(GRID) * PTS - HALO)
    scale = norm_scale.reshape(1, D)
    normed, count = call(
        prepare_body,
        [((EXT, D), BF), ((PTS, EXT), F32)],
        (before, inputs, after, scale, rel),
        cost=(4e6, 1e6),
    )
    wqkv, wout, whead, q, kv, probs, mixed, out, fore = call(
        functools.partial(forward_body, zh_n, rs, ro),
        [
            ((devices, rs, 3 * HD), BF),
            ((devices, ro, D), BF),
            ((devices, 2, rs // 2, NVAR), BF),
            ((PTS, HD), BF),
            ((EXT, D), BF),
            ((HEADS, PTS, EXT), BF),
            ((PTS, HD), BF),
            ((PTS, D), BF),
            ((PTS, NVAR), F32),
        ],
        (core.reshape(1).astype(jnp.int32), normed, inputs, count, own, other),
        specs=(SM, VM, VM, VM, HB, HB),
        scratch=(
            pltpu.SemaphoreType.DMA((2, zh_n, 6)),
            pltpu.SemaphoreType.DMA((2, zh_n, 4)),
            pltpu.SemaphoreType.DMA((2, zh_n)),
        ),
        cost=(2e9, 1e7),
    )
    every = to_all(fore, MEMBER)
    gf, wg = call(
        functools.partial(score_body, members, zh_n),
        [
            ((PTS, NVAR), BF),
            ((pn, zh_n, (D + HD) // devices, NVAR), BF),
        ],
        (every, fore, observed, mixed, out),
        cost=(1e8, 2e6),
    )
    plane = lax.all_to_all(wg, PLANE, 0, 0, tiled=True)
    gq, mid, lower, upper = call(
        backward_body,
        [((PTS, HD), BF), ((PTS, D), F32), ((HALO, D), BF), ((HALO, D), BF)],
        (gf, whead, wout, q, kv, probs, count),
        cost=(1e9, 4e6),
    )
    last = lax.ppermute(lower, GRID, down)
    first = lax.ppermute(upper, GRID, up)
    total, grad_input = call(
        final_body,
        [((PTS, D), F32), ((PTS, D), BF)],
        (inputs, scale, gf, whead, wqkv, gq, mid, first, last),
        cost=(1e9, 4e6),
    )
    partial = jnp.sum(plane.astype(F32), axis=0).astype(BF)
    spread = jnp.broadcast_to(partial[None], (members, *partial.shape))
    parts = lax.all_to_all(
        spread.reshape(members * zh_n, *partial.shape[1:]), COLUMN, 0, 0, tiled=True
    )
    scaling = 1.0 / math.sqrt(members * devices * PTS)
    mixing, head = call(
        functools.partial(weights_body, scaling),
        [((HD // devices, D), F32), ((D // devices, NVAR), F32)],
        (parts, whead),
        cost=(1e8, 1e6),
    )
    return grad_input[None], mixing, head, total[None]


def refined(mesh):
    members, devices = mesh.shape["member"], mesh.shape["grid"]
    cut = {64: (4, 4, 4), 4: (1, 2, 2), 8: (2, 2, 2)}[devices]
    return Mesh(
        mesh.devices.reshape(members // 2, 2, *cut), ("zl", "core", "zh", "y", "x")
    )


def solution(mesh):
    rows = P(GRID, None)
    return jax.shard_map(
        shards,
        mesh=refined(mesh),
        in_specs=(
            P(MEMBER, GRID, None),
            P(),
            rows,
            rows,
            rows,
            rows,
            rows,
            rows,
            rows,
        ),
        out_specs=(P(MEMBER, GRID, None), rows, rows, P(MEMBER, GRID, None)),
        check_vma=False,
    )
```

time: 366 us -> 194 us (0.53)
  the two profiles are of different devices: /device:TPU:1 before, /device:TPU:30 now
where the time goes in v1:
time: 194 us; the launch traced here: 193 us
  blocking collectives  94.2 us (49%)
  starting transfers between devices  41.1 us (21%)
  local copies, waits for them, and re-layouts  23.1 us (12%)
  waiting for transfers between devices  18.1 us (9%)
  Pallas kernels  14.3 us (7%)
    all_to_all x3, blocking collectives, to_all(): lax.all_to_all(jnp.broadcast_to(x[None], (n, *x.shape)), axes, 0, 0, tile...  82 us
    unnamed x53, local copies, waits for them, and re-layouts  21.4 us
    ppermute x1, waiting for transfers between devices, shards(): last = lax.ppermute(lower, GRID, down)  16.3 us
    pallas_call x6, Pallas kernels, call(): pl.pallas_call(body, out_shape=tuple((jax.ShapeDtypeStruct(s, d) for s, d...  14.3 us
    all_to_all x1, starting transfers between devices, shards(): lax.all_to_all(spread.reshape(members * zh_n, *partial.shape[1:]), COLUMN...  12.2 us
    all_to_all x1, blocking collectives, shards(): plane = lax.all_to_all(wg, PLANE, 0, 0, tiled=True)  12.2 us
    ppermute x1, starting transfers between devices, shards(): before = lax.ppermute(inputs[PTS - HALO:], GRID, up)  11.2 us
    ppermute x1, starting transfers between devices, shards(): first = lax.ppermute(upper, GRID, up)  11.2 us
  transfers between devices with their start and end apart: 6, of which 3 were waited for; matrix products, arithmetic and copies ran while one was open for 0% of the time, Pallas kernels for 3%

profile of v1, /device:TPU:30, one launch (start us, length us, event | category | flops | bytes accessed | tf_op | source)
XLA Modules:
  0.0 192.8 jit_solution(10256265771211691164)
XLA Ops:
  11.2 29.9 %all_to_all.25 = bf16[4,136,128]{2,1,0:T(8,128)(2,1)S(1)} all-to-all(bf16[4,136,128]{2,1,0:T(8,128)(2,1)S(1)} %broadcast_in_dim.12), channel_id=1, replica_groups=mesh['zl'=4,'core'=2,'zh'=4,'y'=4,'x'=4] {'zh'}, dimensions={0} | all-to-all | bytes 278528 | tf_op jit(solution)/shard_map/all_to_all | solution.py:249
  41.4 30.7 %all_to_all.26.own = bf16[16,4,136,128]{3,2,1,0:T(8,128)(2,1)S(1)} all-to-all(bf16[16,4,136,128]{3,2,1,0:T(8,128)(2,1)S(1)} %broadcast_in_dim.13), channel_id=1, replica_groups=mesh['zl'=4,'core'=2,'zh'=4,'y'=4,'x'=4] {'y','x'}, dimensions={0} | all-to-all | bytes 4456448 | tf_op jit(solution)/shard_map/all_to_all | solution.py:249
  72.1 1.9 collective-permute-start.2
  74.0 1.4 copy-done
  75.4 2.8 %collective-permute-start.1 = (bf16[32,1024]{1,0:T(8,128)(2,1)S(1)}, bf16[32,1024]{1,0:T(8,128)(2,1)S(1)}, u32[]{:S(2)}, u32[]{:S(2)}) collective-permute-start(bf16[32,1024]{1,0:T(8,128)(2,1)S(1)} %get-tuple-element.46), channel_id=1, source_target_pairs={{1,0},{2,1},{3,2},{4,3},{5,4},{6,5},{7,6},{8,7},{9,8},{10,9},{11,1... | collective-permute-start | bytes 196616 | tf_op jit(solution)/shard_map/ppermute | solution.py:290
  78.2 11.2 %collective-permute-start = (bf16[32,1024]{1,0:T(8,128)(2,1)S(1)}, bf16[32,1024]{1,0:T(8,128)(2,1)S(1)}, u32[]{:S(2)}, u32[]{:S(2)}) collective-permute-start(bf16[32,1024]{1,0:T(8,128)(2,1)S(1)} %get-tuple-element.47), channel_id=1, source_target_pairs={{0,1},{1,2},{2,3},{3,4},{4,5},{5,6},{6,7},{7,8},{8,9},{9,10},{10,1... | collective-permute-start | bytes 196616 | tf_op jit(solution)/shard_map/ppermute | solution.py:289
  89.9 1.3 collective-permute-done.before
  91.7 1.7 copy-done.1
  93.4 6.4 %shard_map.121 = (bf16[64,16,1536]{2,1,0:T(8,128)(2,1)S(1)}, bf16[64,8,1024]{2,1,0:T(8,128)(2,1)S(1)}, bf16[64,2,8,128]{3,2,1,0:T(8,128)(2,1)S(1)}, bf16[128,512...) custom-call(s32[1]{0:T(128)} %bitcast.2.core, ...), custom_call_target="tpu_custom_call" | custom-call | flops 2000000000 | bytes 10000000 | tf_op jit(solution)/shard_map/pallas_call | solution.py:50
  101.3 21.5 %all_to_all.27.every = f32[8,128,128]{2,1,0:T(8,128)S(1)} all-to-all(f32[8,128,128]{2,1,0:T(8,128)S(1)} %broadcast_in_dim.14), channel_id=1, replica_groups=mesh['zl'=4,'core'=2,'zh'=4,'y'=4,'x'=4] {'zl','core'}, dimensions={0} | all-to-all | bytes 1048576 | tf_op jit(solution)/shard_map/all_to_all | solution.py:249
  123.2 12.2 %all_to_all.28 = bf16[16,4,24,128]{3,2,1,0:T(8,128)(2,1)} all-to-all(bf16[16,4,24,128]{3,2,1,0:T(8,128)(2,1)S(1)} %get-tuple-element.42), channel_id=1, replica_groups=mesh['zl'=4,'core'=2,'zh'=4,'y'=4,'x'=4] {'y','x'}, dimensions={0} | all-to-all | bytes 786432 | tf_op jit(solution)/shard_map/all_to_all | solution.py:331
  135.4 1.1 reduce_sum.12
  137.1 12.2 %all-to-all-start.4 = ((bf16[32,24,128]{2,1,0:T(8,128)(2,1)}), bf16[32,24,128]{2,1,0:T(8,128)(2,1)}, u32[]{:S(2)}, u32[]{:S(2)}) async-start(bf16[32,24,128]{2,1,0:T(8,128)(2,1)} %bitcast.15), calls=%async_computation.4 | async-start | bytes 393216 | tf_op jit(solution)/shard_map/all_to_all | solution.py:348
  149.3 0.9 copy-done.4
  151.1 1.2 copy-done.11
  152.4 1.0 copy-done.13
  153.4 1.0 copy-done.15
  155.3 3.2 %shard_map.123 = (bf16[128,512]{1,0:T(8,128)(2,1)S(1)}, f32[128,1024]{1,0:T(8,128)S(1)}, bf16[32,1024]{1,0:T(8,128)(2,1)S(1)}, bf16[32,1024]{1,0:T(8,128)(2,1)S(1)}) custom-call(bf16[128,128]{1,0:T(8,128)(2,1)S(1)} %get-tuple-element.30.gf, bf16[64,2,8,128]{3,2,1,0:T(8,128)(2,1)S(1)} %copy-done.4, bf16[64,8,1024]{2,1,0:T(8,128)(2,1)S(1)} %copy-done.11, ...), custom_call_target="tpu_custom_call" | custom-call | flops 1000000000 | bytes 4000000 | tf_op jit(solution)/shard_map/pallas_call | solution.py:50
  158.5 11.2 %collective-permute-start.3 = (bf16[32,1024]{1,0:T(8,128)(2,1)S(1)}, bf16[32,1024]{1,0:T(8,128)(2,1)S(1)}, u32[]{:S(2)}, u32[]{:S(2)}) collective-permute-start(bf16[32,1024]{1,0:T(8,128)(2,1)S(1)} %get-tuple-element.39), channel_id=1, source_target_pairs={{0,1},{1,2},{2,3},{3,4},{4,5},{5,6},{6,7},{7,8},{8,9},{9,10},{10,1... | collective-permute-start | bytes 196616 | tf_op jit(solution)/shard_map/ppermute | solution.py:339
  169.7 1.9 collective-permute-start.4
  171.7 16.3 %collective-permute-done.4.last = bf16[32,1024]{1,0:T(8,128)(2,1)S(1)} collective-permute-done((bf16[32,1024]{1,0:T(8,128)(2,1)S(1)}, bf16[32,1024]{1,0:T(8,128)(2,1)S(1)}, u32[]{:S(2)}, u32[]{:S(2)}) %collective-permute-start.4) | collective-permute-done | bytes 65568 | tf_op jit(solution)/shard_map/ppermute | solution.py:338
  188.0 2.1 %shard_map.124 = (f32[128,1024]{1,0:T(8,128)}, bf16[128,1024]{1,0:T(8,128)(2,1)}) custom-call(bf16[128,1024]{1,0:T(8,128)(2,1)S(1)} %bitcast.12, f32[1,1024]{1,0:T(1,128)S(1)} %bitcast.14, bf16[128,128]{1,0:T(8,128)(2,1)S(1)} %get-tuple-element.30.gf, bf16[64,2,8,128]{3,2,1,0:T(8,128)(2,1)S(1)} %copy-done.4, ...), custom_call_target="tpu_custom_call" | custom-call | flops 1000000000 | bytes 4000000 | tf_op jit(solution)/shard_map/pallas_call | solution.py:50
  190.0 0.9 copy-done.5
  191.0 1.8 shard_map.125
  (60 shorter events, 16.2 us)
Async XLA Ops:
  41.4 34.0 %copy-start.2 = (bf16[1,128,1024]{2,1,0:T(8,128)(2,1)S(1)}, bf16[1,128,1024]{2,1,0:T(8,128)(2,1)}, u32[]{:S(2)}) copy-start(bf16[1,128,1024]{2,1,0:T(8,128)(2,1)} %param.9) | copy-start | bytes 786436
  41.4 48.0 %copy-start.18 = (s32[128,8]{0,1:T(8,128)S(1)}, s32[128,8]{0,1:T(8,128)}, u32[]{:S(2)}) copy-start(s32[128,8]{0,1:T(8,128)} %param.16) | copy-start | bytes 12292
  41.4 49.9 %copy-start.7 = (f32[1024]{0:T(1024)S(1)}, f32[1024]{0:T(1024)}, u32[]{:S(2)}) copy-start(f32[1024]{0:T(1024)} %param.10) | copy-start | bytes 12292
  72.1 19.6 %collective-permute-start.2 = (bf16[16,4,136,128]{3,2,1,0:T(8,128)(2,1)S(1)}, bf16[16,4,136,128]{3,2,1,0:T(8,128)(2,1)}, u32[]{:S(2)}, u32[]{:S(2)}) collective-permute-start(bf16[16,4,136,128]{3,2,1,0:T(8,128)(2,1)S(1)} %all_to_all.26.own), channel_id=1, source_target_pairs={{0,64},{64,0},{1,65},{65,1},{2,66},{66,2},{3,67},{67,3},{4,68},{68... | collective-permute-start | bytes 6684680 | tf_op jit(solution)/shard_map/ppermute | solution.py:270
  74.0 1.4 copy-start
  75.4 14.5 %collective-permute-start.1 = (bf16[32,1024]{1,0:T(8,128)(2,1)S(1)}, bf16[32,1024]{1,0:T(8,128)(2,1)S(1)}, u32[]{:S(2)}, u32[]{:S(2)}) collective-permute-start(bf16[32,1024]{1,0:T(8,128)(2,1)S(1)} %get-tuple-element.46), channel_id=1, source_target_pairs={{1,0},{2,1},{3,2},{4,3},{5,4},{6,5},{7,6},{8,7},{9,8},{10,9},{11,1... | collective-permute-start | bytes 196616 | tf_op jit(solution)/shard_map/ppermute | solution.py:290
  78.2 13.1 %collective-permute-start = (bf16[32,1024]{1,0:T(8,128)(2,1)S(1)}, bf16[32,1024]{1,0:T(8,128)(2,1)S(1)}, u32[]{:S(2)}, u32[]{:S(2)}) collective-permute-start(bf16[32,1024]{1,0:T(8,128)(2,1)S(1)} %get-tuple-element.47), channel_id=1, source_target_pairs={{0,1},{1,2},{2,3},{3,4},{4,5},{5,6},{6,7},{7,8},{8,9},{9,10},{10,1... | collective-permute-start | bytes 196616 | tf_op jit(solution)/shard_map/ppermute | solution.py:289
  91.7 8.1 %copy-start.8 = (f32[128,192]{1,0:T(8,128)}, f32[128,192]{1,0:T(8,128)S(1)}, u32[]{:S(2)}) copy-start(f32[128,192]{1,0:T(8,128)S(1)} %get-tuple-element.26.count) | copy-start | bytes 294916
  91.7 1.7 copy-start.1
  93.4 29.4 %copy-start.6 = (f32[128,128]{1,0:T(8,128)S(1)}, f32[128,128]{1,0:T(8,128)}, u32[]{:S(2)}) copy-start(f32[128,128]{1,0:T(8,128)} %observed.1) | copy-start | bytes 196612
  100.5 0.7 copy-start.14
  101.3 21.9 %copy-start.10 = (bf16[64,8,1024]{2,1,0:T(8,128)(2,1)}, bf16[64,8,1024]{2,1,0:T(8,128)(2,1)S(1)}, u32[]{:S(2)}) copy-start(bf16[64,8,1024]{2,1,0:T(8,128)(2,1)S(1)} %get-tuple-element.33.wout) | copy-start | bytes 3145732
  101.3 21.9 %copy-start.12 = (bf16[8,128,192]{2,1,0:T(8,128)(2,1)}, bf16[8,128,192]{2,1,0:T(8,128)(2,1)S(1)}, u32[]{:S(2)}) copy-start(bf16[8,128,192]{2,1,0:T(8,128)(2,1)S(1)} %get-tuple-element.36.probs) | copy-start | bytes 1179652
  101.3 21.9 %copy-start.16 = (bf16[128,512]{1,0:T(8,128)(2,1)}, bf16[128,512]{1,0:T(8,128)(2,1)S(1)}, u32[]{:S(2)}) copy-start(bf16[128,512]{1,0:T(8,128)(2,1)S(1)} %get-tuple-element.34.q) | copy-start | bytes 393220
  137.1 52.9 %all-to-all-start.4 = ((bf16[32,24,128]{2,1,0:T(8,128)(2,1)}), bf16[32,24,128]{2,1,0:T(8,128)(2,1)}, u32[]{:S(2)}, u32[]{:S(2)}) async-start(bf16[32,24,128]{2,1,0:T(8,128)(2,1)} %bitcast.15), calls=%async_computation.4 | async-start | bytes 393216 | tf_op jit(solution)/shard_map/all_to_all | solution.py:348
  149.3 1.0 copy-start.4
  150.2 0.9 copy-start.9
  151.1 1.2 copy-start.11
  152.4 1.0 copy-start.13
  153.4 1.0 copy-start.15
  154.4 0.9 copy-start.17
  158.5 13.1 %collective-permute-start.3 = (bf16[32,1024]{1,0:T(8,128)(2,1)S(1)}, bf16[32,1024]{1,0:T(8,128)(2,1)S(1)}, u32[]{:S(2)}, u32[]{:S(2)}) collective-permute-start(bf16[32,1024]{1,0:T(8,128)(2,1)S(1)} %get-tuple-element.39), channel_id=1, source_target_pairs={{0,1},{1,2},{2,3},{3,4},{4,5},{5,6},{6,7},{7,8},{8,9},{9,10},{10,1... | collective-permute-start | bytes 196616 | tf_op jit(solution)/shard_map/ppermute | solution.py:339
  169.7 18.3 %collective-permute-start.4 = (bf16[32,1024]{1,0:T(8,128)(2,1)S(1)}, bf16[32,1024]{1,0:T(8,128)(2,1)S(1)}, u32[]{:S(2)}, u32[]{:S(2)}) collective-permute-start(bf16[32,1024]{1,0:T(8,128)(2,1)S(1)} %get-tuple-element.40), channel_id=1, source_target_pairs={{1,0},{2,1},{3,2},{4,3},{5,4},{6,5},{7,6},{8,7},{9,8},{10,9},{11,1... | collective-permute-start | bytes 196616 | tf_op jit(solution)/shard_map/ppermute | solution.py:338
  190.0 1.0 copy-start.5
  (1 other events, 0.7 us)

commit v2 on v1

v2 whole, which is shorter than its diff:
```python
import functools
import math

import jax
import jax.numpy as jnp
from jax import lax
from jax.experimental import pallas as pl
from jax.experimental.pallas import tpu as pltpu
from jax.sharding import Mesh, PartitionSpec as P


HEADS = 8
HDIM = 64
KNB = 8
HALO = 32
PTS = 128
EXT = PTS + 2 * HALO
D = 1024
HD = 512
NVAR = 128
LANE = 128

epsilon = 1e-05
smooth = 0.1

MEMBER = ("zl", "core")
GRID = ("zh", "y", "x")
PLANE = ("y", "x")
COLUMN = ("zl", "core", "zh")

BF = jnp.bfloat16
F32 = jnp.float32


def nn(a, b):
    return lax.dot_general(a, b, (((1,), (0,)), ((), ())), preferred_element_type=F32)


def nt(a, b):
    return lax.dot_general(a, b, (((1,), (1,)), ((), ())), preferred_element_type=F32)


def tn(a, b):
    return lax.dot_general(a, b, (((0,), (0,)), ((), ())), preferred_element_type=F32)


SPECS = {
    "V": pl.BlockSpec(memory_space=pltpu.VMEM),
    "A": pl.BlockSpec(),
    "H": pl.BlockSpec(memory_space=pltpu.HBM),
}


def call(body, outs, args, places, scratch=(), cost=(1e9, 4e6), limit=16):
    taken, given = places.split(">")
    shapes = [
        jax.ShapeDtypeStruct(s, d) if at == "V" else pltpu.HBM(s, d)
        for (s, d), at in zip(outs, given, strict=True)
    ]
    args = [
        x if at == "V" else pltpu.with_memory_space_constraint(x, pltpu.HBM)
        for x, at in zip(args, taken, strict=True)
    ]
    return pl.pallas_call(
        body,
        out_shape=tuple(shapes),
        in_specs=[SPECS[at] for at in taken],
        out_specs=tuple(SPECS[at] for at in given),
        scratch_shapes=list(scratch),
        compiler_params=pltpu.CompilerParams(vmem_limit_bytes=limit << 20),
        cost_estimate=pl.CostEstimate(
            flops=int(cost[0]), bytes_accessed=int(cost[1]), transcendentals=0
        ),
    )(*args)


def normalised(rows):
    values = rows.astype(F32)
    center = values - jnp.mean(values, axis=-1, keepdims=True)
    inverse = lax.rsqrt(jnp.mean(center * center, axis=-1, keepdims=True) + epsilon)
    return center * inverse, inverse


def prepare_body(before, own, after, scale, rel, normed, count):
    for part, at in ((before, 0), (own, HALO), (after, HALO + PTS)):
        centred, _ = normalised(part[...])
        normed[at : at + part.shape[0], :] = (centred * scale[...]).astype(BF)
    place = lax.broadcasted_iota(jnp.int32, (PTS, EXT), 1)
    total = jnp.zeros((PTS, EXT), F32)
    for k in range(KNB):
        total = total + (place == rel[:, k : k + 1]).astype(F32)
    count[...] = total


def halves(tile_shape, head):
    lane = lax.broadcasted_iota(jnp.int32, tile_shape, 1)
    return (lane < HDIM) if head == 0 else (lane >= HDIM)


def fetched(pairs, sems):
    return [pltpu.make_async_copy(s, d, sems.at[i]) for i, (s, d) in enumerate(pairs)]


def send_out(pairs, sems):
    copies = fetched(pairs, sems)
    for copy in copies:
        copy.start()
    for copy in copies:
        copy.wait()


def pack_body(query, key, value, out, head, mine, plane, sems):
    rs, ro = query.shape[0], out.shape[0]

    def put(row, tile):
        size = tile.shape[0]
        mine[row : row + size, :] = tile

    for c in range(2):

        @pl.when(lax.axis_index("core") == c)
        def _():
            for t in range(6):
                weight = (query, key, value)[(6 * c + t) // 4]
                lane = (6 * c + t) % 4 * LANE
                put(t * rs, weight[:, lane : lane + LANE])
            for t in range(4):
                lane = (4 * c + t) * LANE
                put(6 * rs + t * ro, out[:, lane : lane + LANE])
            put(6 * rs + 4 * ro, head[c * rs // 2 : (c + 1) * rs // 2, :])

    send_out([(mine, plane.at[i]) for i in range(plane.shape[0])], sems)


def rest_body(*refs):
    *blocks, rest, sems = refs
    send_out(
        [
            (block, rest.at[i, k])
            for k, block in enumerate(blocks)
            for i in range(rest.shape[0])
        ],
        sems,
    )


def forward_body(
    zh_n, rs, ro, normed, states, count, own0, other0, own1, other1,
    wqkv_out, wout_out, whead_out, q_out, kv_out, probs_out, mixed, out, fore,
    wqkv, wout, whead, q, kv, probs, sq, so, sh, sems,
):
    core, zh = lax.axis_index("core"), lax.axis_index("zh")

    def leaving(i):
        src, dst = (
            (wqkv, wqkv_out),
            (wout, wout_out),
            (whead, whead_out),
            (q, q_out),
            (kv, kv_out),
            (probs, probs_out),
        )[i]
        return pltpu.make_async_copy(src, dst, sems.at[i])

    pn = wqkv.shape[0] // zh_n
    qrows = 6 * rs
    orows = 4 * ro

    def pieces(first, rest, c):
        for k in range(zh_n):
            at = pl.ds(lax.rem(zh + k, zh_n) * pn, pn)

            def rows(start, size):
                if k == 0:
                    return first.at[:, pl.ds(start, size), :]
                return rest.at[:, k - 1, pl.ds(start, size), :]

            for t in range(6):
                yield (
                    rows(t * rs, rs),
                    wqkv.at[at, :, pl.ds((6 * c + t) * LANE, LANE)],
                    sq.at[c, k, t],
                )
            for t in range(4):
                yield (
                    rows(qrows + t * ro, ro),
                    wout.at[at, :, pl.ds((4 * c + t) * LANE, LANE)],
                    so.at[c, k, t],
                )
            yield rows(qrows + orows, rs // 2), whead.at[at, c], sh.at[c, k]

    def begin(a, b):
        for c, pair in enumerate((a, b)):
            for src, dst, sem in pieces(*pair, c):
                pltpu.make_async_copy(src, dst, sem).start()

    @pl.when(core == 0)
    def _():
        begin((own0, own1), (other0, other1))

    @pl.when(core != 0)
    def _():
        begin((other0, other1), (own0, own1))

    for c in range(2):
        for src, dst, sem in pieces(own0, own1, c):
            pltpu.make_async_copy(src, dst, sem).wait()

    for i in range(3):
        leaving(i).start()
    rows = normed[...]
    weights = wqkv[...].reshape(D, 3 * HD)
    q[...] = nn(rows[HALO : HALO + PTS], weights[:, :HD]).astype(BF)
    kv[...] = nn(rows, weights[:, HD:]).astype(BF)
    for i in range(3, 5):
        leaving(i).start()
    times = count[...]
    here = times > 0
    for pair in range(HEADS // 2):
        at = pl.ds(pair * LANE, LANE)
        q2, k2, v2 = q[:, at], kv[:, at], kv[:, pl.ds(HD + pair * LANE, LANE)]
        got = []
        for side in range(2):
            chosen = jnp.where(halves((PTS, LANE), side), q2, jnp.zeros_like(q2))
            score = nt(chosen, k2) * (1.0 / math.sqrt(HDIM))
            score = jnp.where(here, score, -1e30)
            highest = jnp.max(score, axis=-1, keepdims=True)
            power = jnp.exp(score - highest)
            prob = power / jnp.sum(times * power, axis=-1, keepdims=True)
            weight = (times * prob.astype(BF).astype(F32)).astype(BF)
            probs[2 * pair + side] = weight
            got.append(nn(weight, v2))
        mixed[:, at] = jnp.where(halves((PTS, LANE), 0), got[0], got[1]).astype(BF)
    leaving(5).start()
    flat_out = wout[...].astype(F32).reshape(HD, D).astype(BF)
    flat_head = whead[...].astype(F32).reshape(D, NVAR).astype(BF)
    layer = (states[...].astype(F32) + nn(mixed[...], flat_out)).astype(BF)
    out[...] = layer
    mine = nn(layer, flat_head)
    for i in range(fore.shape[0]):
        fore[i] = mine
    for i in range(6):
        leaving(i).wait()


def slope(z):
    return z * lax.rsqrt(z * z + smooth * smooth)


def score_body(members, zh_n, every, fore, observed, mixed, out, gf, wg):
    mine = fore[0]
    total = jnp.zeros_like(mine)
    for m in range(members):
        total = total + slope(mine - every[m])
    grad = (slope(mine - observed[...]) - total * (1.0 / (members - 1))).astype(BF)
    gf[...] = grad
    pn = wg.shape[0]
    heads = tn(out[...], grad)
    factor = tn(mixed[...], grad)
    rb, ra = D // (zh_n * pn), HD // (zh_n * pn)
    for zh in range(zh_n):
        wg[:, zh, 0:rb, :] = (
            heads[zh * pn * rb : (zh + 1) * pn * rb].reshape(pn, rb, NVAR).astype(BF)
        )
        wg[:, zh, rb : rb + ra, :] = (
            factor[zh * pn * ra : (zh + 1) * pn * ra].reshape(pn, ra, NVAR).astype(BF)
        )


def backward_body(
    gf, whead_in, wout_in, q_in, kv_in, probs_in, gq, mid, lower, upper,
    whead, wout, q, kv, probs, sems,
):
    copies = fetched(
        (
            (whead_in, whead),
            (wout_in, wout),
            (kv_in, kv),
            (probs_in, probs),
            (q_in, q),
        ),
        sems,
    )
    for copy in copies:
        copy.start()
    copies[0].wait()
    flat_head = whead[...].astype(F32).reshape(D, NVAR).astype(BF)
    go = nt(gf[...], flat_head).astype(BF)
    copies[1].wait()
    flat_out = wout[...].astype(F32).reshape(HD, D).astype(BF)
    gm = nt(go, flat_out).astype(BF)
    for copy in copies[2:]:
        copy.wait()
    for pair in range(HEADS // 2):
        at = pl.ds(pair * LANE, LANE)
        vat = pl.ds(HD + pair * LANE, LANE)
        q2, k2, v2 = q[:, at], kv[:, at], kv[:, vat]
        g2 = gm[:, pair * LANE : (pair + 1) * LANE]
        gqs, gks, gvs = [], [], []
        for side in range(2):
            chosen = jnp.where(halves((PTS, LANE), side), g2, jnp.zeros_like(g2))
            gp = nt(chosen, v2)
            held = probs[2 * pair + side]
            weight = held.astype(F32)
            centre = jnp.sum(weight * gp, axis=-1, keepdims=True)
            gs = (weight * (gp - centre) * (1.0 / math.sqrt(HDIM))).astype(BF)
            gqs.append(nn(gs, k2))
            gks.append(tn(gs, q2))
            gvs.append(tn(held, g2))
        gq[:, at] = jnp.where(halves((PTS, LANE), 0), gqs[0], gqs[1]).astype(BF)
        pick = halves((EXT, LANE), 0)
        for where_at, parts in ((at, gks), (vat, gvs)):
            total = jnp.where(pick, parts[0], parts[1])
            lower[:, where_at] = total[:HALO].astype(BF)
            mid[:, where_at] = total[HALO : HALO + PTS]
            upper[:, where_at] = total[HALO + PTS :].astype(BF)


def final_body(
    states, scale, gf, whead_in, wqkv_in, gq, mid, first, last, total, grad,
    whead, wqkv, sems,
):
    copies = fetched(((wqkv_in, wqkv), (whead_in, whead)), sems)
    for copy in copies:
        copy.start()
    centred, inverse = normalised(states[...])
    copies[1].wait()
    flat_head = whead[...].astype(F32).reshape(D, NVAR).astype(BF)
    total[...] = mid[...]
    total[:HALO, :] += first[...].astype(F32)
    total[PTS - HALO :, :] += last[...].astype(F32)
    kvs = total[...].astype(BF)
    copies[0].wait()
    weights = wqkv[...].reshape(D, 3 * HD)
    gn = nt(gq[...], weights[:, :HD]) + nt(kvs, weights[:, HD:])
    g = gn * scale[...]
    back = inverse * (
        g
        - jnp.mean(g, axis=-1, keepdims=True)
        - centred * jnp.mean(g * centred, axis=-1, keepdims=True)
    )
    grad[...] = (nt(gf[...], flat_head) + back).astype(BF)


def spread_body(plane, spread):
    total = plane[0].astype(F32)
    for i in range(1, plane.shape[0]):
        total = total + plane[i].astype(F32)
    total = total.astype(BF)
    for i in range(spread.shape[0]):
        spread[i] = total


def weights_body(scaling, parts, whead, mixing, head):
    flat_head = whead[...].astype(F32).reshape(D, NVAR).astype(BF)
    rb = head.shape[0]
    total = jnp.zeros(parts.shape[1:], F32)
    for i in range(parts.shape[0]):
        total = total + parts[i].astype(F32)
    total = total * scaling
    head[...] = total[:rb]
    factor = total[rb:]
    high = factor.astype(BF)
    low = (factor - high.astype(F32)).astype(BF)
    mixing[...] = nt(high, flat_head) + nt(low, flat_head)


def shards(
    states, norm_scale, query, key, value, out_w, head_w, neighbours, observed
):
    members = lax.axis_size(MEMBER)
    devices = lax.axis_size(GRID)
    zh_n = lax.axis_size("zh")
    pn = lax.axis_size(PLANE)
    inputs = states[0]
    rs, ro = query.shape[0], out_w.shape[0]
    packed = 6 * rs + 4 * ro + rs // 2
    swap = [(0, 1), (1, 0)]
    up = [(i, i + 1) for i in range(devices - 1)]
    down = [(j, i) for i, j in up]

    mine, plane = call(
        pack_body,
        [((packed, LANE), BF), ((pn, packed, LANE), BF)],
        (query, key, value, out_w, head_w),
        "AAAAA>VH",
        scratch=(pltpu.SemaphoreType.DMA((pn,)),),
        cost=(1e6, 1e6),
        limit=4,
    )
    own0 = lax.all_to_all(plane, PLANE, 0, 0, tiled=True)
    blocks = []
    for k in range(1, zh_n):
        turn = [((i + k) % zh_n, i) for i in range(zh_n)]
        blocks.append(lax.ppermute(mine, "zh", turn))
    before = lax.ppermute(inputs[PTS - HALO :], GRID, up)
    after = lax.ppermute(inputs[:HALO], GRID, down)
    rel = neighbours - (lax.axis_index(GRID) * PTS - HALO)
    scale = norm_scale.reshape(1, D)
    normed, count = call(
        prepare_body,
        [((EXT, D), BF), ((PTS, EXT), F32)],
        (before, inputs, after, scale, rel),
        "VAVAA>AA",
        cost=(4e6, 1e6),
        limit=8,
    )
    (rest,) = call(
        rest_body,
        [((pn, zh_n - 1, packed, LANE), BF)],
        blocks,
        "V" * (zh_n - 1) + ">H",
        scratch=(pltpu.SemaphoreType.DMA((pn * (zh_n - 1),)),),
        cost=(1e6, 2e6),
        limit=4,
    )
    own1 = lax.all_to_all(rest, PLANE, 0, 0, tiled=True)
    other0 = lax.ppermute(own0, "core", swap)
    other1 = lax.ppermute(own1, "core", swap)
    wqkv, wout, whead, q, kv, probs, mixed, out, fore = call(
        functools.partial(forward_body, zh_n, rs, ro),
        [
            ((devices, rs, 3 * HD), BF),
            ((devices, ro, D), BF),
            ((devices, 2, rs // 2, NVAR), BF),
            ((PTS, HD), BF),
            ((EXT, D), BF),
            ((HEADS, PTS, EXT), BF),
            ((PTS, HD), BF),
            ((PTS, D), BF),
            ((members, PTS, NVAR), F32),
        ],
        (normed, inputs, count, own0, other0, own1, other1),
        "AAAVVVV>HHHHHHVVV",
        scratch=(
            pltpu.VMEM((devices, rs, 3 * HD), BF),
            pltpu.VMEM((devices, ro, D), BF),
            pltpu.VMEM((devices, 2, rs // 2, NVAR), BF),
            pltpu.VMEM((PTS, HD), BF),
            pltpu.VMEM((EXT, D), BF),
            pltpu.VMEM((HEADS, PTS, EXT), BF),
            pltpu.SemaphoreType.DMA((2, zh_n, 6)),
            pltpu.SemaphoreType.DMA((2, zh_n, 4)),
            pltpu.SemaphoreType.DMA((2, zh_n)),
            pltpu.SemaphoreType.DMA((6,)),
        ),
        cost=(2e9, 1e7),
        limit=24,
    )
    every = lax.all_to_all(fore, MEMBER, 0, 0, tiled=True)
    gf, wg = call(
        functools.partial(score_body, members, zh_n),
        [
            ((PTS, NVAR), BF),
            ((pn, zh_n, (D + HD) // devices, NVAR), BF),
        ],
        (every, fore, observed, mixed, out),
        "VVAVV>AA",
        cost=(1e8, 2e6),
        limit=8,
    )
    plane = lax.all_to_all(wg, PLANE, 0, 0, tiled=True)
    gq, mid, lower, upper = call(
        backward_body,
        [((PTS, HD), BF), ((PTS, D), F32), ((HALO, D), BF), ((HALO, D), BF)],
        (gf, whead, wout, q, kv, probs),
        "AHHHHH>AAAA",
        scratch=(
            pltpu.VMEM(whead.shape, BF),
            pltpu.VMEM(wout.shape, BF),
            pltpu.VMEM(q.shape, BF),
            pltpu.VMEM(kv.shape, BF),
            pltpu.VMEM(probs.shape, BF),
            pltpu.SemaphoreType.DMA((5,)),
        ),
        cost=(1e9, 4e6),
        limit=16,
    )
    last = lax.ppermute(lower, GRID, down)
    first = lax.ppermute(upper, GRID, up)
    (spread,) = call(
        spread_body,
        [((members, *wg.shape[1:]), BF)],
        (plane,),
        "V>A",
        cost=(1e6, 1e6),
        limit=4,
    )
    parts = lax.all_to_all(
        spread.reshape(members * zh_n, *wg.shape[2:]), COLUMN, 0, 0, tiled=True
    )
    total, grad_input = call(
        final_body,
        [((PTS, D), F32), ((PTS, D), BF)],
        (inputs, scale, gf, whead, wqkv, gq, mid, first, last),
        "AAAHHAAVV>AA",
        scratch=(
            pltpu.VMEM(whead.shape, BF),
            pltpu.VMEM(wqkv.shape, BF),
            pltpu.SemaphoreType.DMA((2,)),
        ),
        cost=(1e9, 4e6),
        limit=16,
    )
    scaling = 1.0 / math.sqrt(members * devices * PTS)
    mixing, head = call(
        functools.partial(weights_body, scaling),
        [((HD // devices, D), F32), ((D // devices, NVAR), F32)],
        (parts, whead),
        "VA>AA",
        cost=(1e8, 1e6),
        limit=8,
    )
    return grad_input[None], mixing, head, total[None]


def refined(mesh):
    members, devices = mesh.shape["member"], mesh.shape["grid"]
    cut = {64: (4, 4, 4), 4: (1, 2, 2), 8: (2, 2, 2)}[devices]
    return Mesh(
        mesh.devices.reshape(members // 2, 2, *cut), ("zl", "core", "zh", "y", "x")
    )


def solution(mesh):
    rows = P(GRID, None)

    return jax.shard_map(
        shards,
        mesh=refined(mesh),
        in_specs=(
            P(MEMBER, GRID, None),
            P(),
            rows,
            rows,
            rows,
            rows,
            rows,
            rows,
            rows,
        ),
        out_specs=(P(MEMBER, GRID, None), rows, rows, P(MEMBER, GRID, None)),
        check_vma=False,
    )
```

time: 194 us -> 200 us (1.031)
  starting transfers between devices: 41.1 us -> 67.6 us
  local copies, waits for them, and re-layouts: 23.1 us -> 0.13 us
  blocking collectives: 94.2 us -> 74.2 us
  Pallas kernels: 14.3 us -> 30.8 us
  waiting for transfers between devices: 18.1 us -> 25.2 us
    ppermute x1 -> x5, starting transfers between devices: 1.91 us -> 29.3 us  [the longest x3 25.5 us: shards(): blocks.append(lax.ppermute(mine, 'zh', turn))]
    unnamed x53 -> x7, local copies, waits for them, and re-layouts: 21.4 us -> 0.12 us
    all_to_all x3, blocking collectives: 82 us -> 61.9 us  [the longest x1 24.9 us: shards(): own1 = lax.all_to_all(rest, PLANE, 0, 0, tiled=True)]
    pallas_call x6 -> x9, Pallas kernels: 14.3 us -> 30.8 us  [call(): pl.pallas_call(body, out_shape=tuple(shapes), in_specs=[SPECS[at] for at...]
    ppermute x1 -> x5, waiting for transfers between devices: 0.01 us -> 5.16 us  [the longest x3 5.15 us: shards(): blocks.append(lax.ppermute(mine, 'zh', turn))]
    ppermute x1, waiting for transfers between devices: 0.4 us -> 3.45 us  [shards(): after = lax.ppermute(inputs[:HALO], GRID, down)]
  transfers between devices with their start and end apart: 6 -> 10, of which waited for: 3 -> 4; matrix products, arithmetic and copies ran while one was open for 0% -> 0% of each run, Pallas kernels for 3% -> 7%
where the time goes in v2:
time: 200 us; the launch traced here: 199 us
  blocking collectives  74.2 us (37%)
  starting transfers between devices  67.6 us (34%)
  Pallas kernels  30.8 us (15%)
  waiting for transfers between devices  25.2 us (13%)
    pallas_call x9, Pallas kernels, call(): pl.pallas_call(body, out_shape=tuple(shapes), in_specs=[SPECS[at] for at...  30.8 us
    ppermute x3, starting transfers between devices, shards(): blocks.append(lax.ppermute(mine, 'zh', turn))  25.5 us
    all_to_all x1, blocking collectives, shards(): own1 = lax.all_to_all(rest, PLANE, 0, 0, tiled=True)  24.9 us
    all_to_all x1, blocking collectives, shards(): every = lax.all_to_all(fore, MEMBER, 0, 0, tiled=True)  21 us
    ppermute x1, waiting for transfers between devices, shards(): last = lax.ppermute(lower, GRID, down)  16.3 us
    all_to_all x1, blocking collectives, shards(): own0 = lax.all_to_all(plane, PLANE, 0, 0, tiled=True)  16 us
    all_to_all x1, blocking collectives, shards(): plane = lax.all_to_all(wg, PLANE, 0, 0, tiled=True)  12.3 us
    ppermute x1, starting transfers between devices, shards(): before = lax.ppermute(inputs[PTS - HALO:], GRID, up)  11.4 us
  transfers between devices with their start and end apart: 10, of which 4 were waited for; matrix products, arithmetic and copies ran while one was open for 0% of the time, Pallas kernels for 7%

profile of v2, /device:TPU:30, one launch (start us, length us, event | category | flops | bytes accessed | tf_op | source)
XLA Modules:
  0.0 199.4 jit_solution(12992639534153214279)
XLA Ops:
  0.6 1.7 shard_map.121
  2.4 9.1 %collective-permute-start.5 = (bf16[136,128]{1,0:T(8,128)(2,1)S(1)}, bf16[136,128]{1,0:T(8,128)(2,1)S(1)}, u32[]{:S(2)}, u32[]{:S(2)}) collective-permute-start(bf16[136,128]{1,0:T(8,128)(2,1)S(1)} %get-tuple-element.30), channel_id=1, source_target_pairs={{48,0},{0,16},{16,32},{32,48},{49,1},{1,17},{17,33},{33,49},{50,2}... | collective-permute-start | bytes 104456 | tf_op jit(solution)/shard_map/ppermute | solution.py:395
  11.5 10.9 %collective-permute-start.4 = (bf16[136,128]{1,0:T(8,128)(2,1)S(1)}, bf16[136,128]{1,0:T(8,128)(2,1)S(1)}, u32[]{:S(2)}, u32[]{:S(2)}) collective-permute-start(bf16[136,128]{1,0:T(8,128)(2,1)S(1)} %get-tuple-element.30), channel_id=1, source_target_pairs={{32,0},{48,16},{0,32},{16,48},{33,1},{49,17},{1,33},{17,49},{34,2}... | collective-permute-start | bytes 104456 | tf_op jit(solution)/shard_map/ppermute | solution.py:395
  22.4 5.5 %collective-permute-start.3 = (bf16[136,128]{1,0:T(8,128)(2,1)S(1)}, bf16[136,128]{1,0:T(8,128)(2,1)S(1)}, u32[]{:S(2)}, u32[]{:S(2)}) collective-permute-start(bf16[136,128]{1,0:T(8,128)(2,1)S(1)} %get-tuple-element.30), channel_id=1, source_target_pairs={{16,0},{32,16},{48,32},{0,48},{17,1},{33,17},{49,33},{1,49},{18,2}... | collective-permute-start | bytes 104456 | tf_op jit(solution)/shard_map/ppermute | solution.py:395
  27.9 5.1 %collective-permute-done.3.refs_0_ = bf16[136,128]{1,0:T(8,128)(2,1)S(1)} collective-permute-done((bf16[136,128]{1,0:T(8,128)(2,1)S(1)}, bf16[136,128]{1,0:T(8,128)(2,1)S(1)}, u32[]{:S(2)}, u32[]{:S(2)}) %collective-permute-start.3) | collective-permute-done | bytes 34848 | tf_op jit(solution)/shard_map/ppermute | solution.py:395
  34.7 24.9 %all_to_all.25.own1 = bf16[16,3,136,128]{3,2,1,0:T(8,128)(2,1)S(1)} all-to-all(bf16[16,3,136,128]{3,2,1,0:T(8,128)(2,1)} %shard_map.122), channel_id=1, replica_groups=mesh['zl'=4,'core'=2,'zh'=4,'y'=4,'x'=4] {'y','x'}, dimensions={0} | all-to-all | bytes 3342336 | tf_op jit(solution)/shard_map/all_to_all | solution.py:417
  59.6 1.9 collective-permute-start.6
  61.6 16.0 %all_to_all.26.own0 = bf16[16,136,128]{2,1,0:T(8,128)(2,1)S(1)} all-to-all(bf16[16,136,128]{2,1,0:T(8,128)(2,1)S(1)} %copy-done.1), channel_id=1, replica_groups=mesh['zl'=4,'core'=2,'zh'=4,'y'=4,'x'=4] {'y','x'}, dimensions={0} | all-to-all | bytes 1114112 | tf_op jit(solution)/shard_map/all_to_all | solution.py:391
  77.5 1.9 collective-permute-start.2
  79.5 2.5 %collective-permute-start.1 = (bf16[32,1024]{1,0:T(8,128)(2,1)S(1)}, bf16[32,1024]{1,0:T(8,128)(2,1)S(1)}, u32[]{:S(2)}, u32[]{:S(2)}) collective-permute-start(bf16[32,1024]{1,0:T(8,128)(2,1)S(1)} %get-tuple-element.50), channel_id=1, source_target_pairs={{1,0},{2,1},{3,2},{4,3},{5,4},{6,5},{7,6},{8,7},{9,8},{10,9},{11,1... | collective-permute-start | bytes 196616 | tf_op jit(solution)/shard_map/ppermute | solution.py:397
  82.0 11.4 %collective-permute-start = (bf16[32,1024]{1,0:T(8,128)(2,1)S(1)}, bf16[32,1024]{1,0:T(8,128)(2,1)S(1)}, u32[]{:S(2)}, u32[]{:S(2)}) collective-permute-start(bf16[32,1024]{1,0:T(8,128)(2,1)S(1)} %get-tuple-element.51), channel_id=1, source_target_pairs={{0,1},{1,2},{2,3},{3,4},{4,5},{5,6},{6,7},{7,8},{8,9},{9,10},{10,1... | collective-permute-start | bytes 196616 | tf_op jit(solution)/shard_map/ppermute | solution.py:396
  94.2 3.5 %collective-permute-done.1.after = bf16[32,1024]{1,0:T(8,128)(2,1)S(1)} collective-permute-done((bf16[32,1024]{1,0:T(8,128)(2,1)S(1)}, bf16[32,1024]{1,0:T(8,128)(2,1)S(1)}, u32[]{:S(2)}, u32[]{:S(2)}) %collective-permute-start.1) | collective-permute-done | bytes 65568 | tf_op jit(solution)/shard_map/ppermute | solution.py:397
  97.7 2.1 %shard_map.120 = (bf16[192,1024]{1,0:T(8,128)(2,1)}, f32[128,192]{1,0:T(8,128)}) custom-call(bf16[32,1024]{1,0:T(8,128)(2,1)S(1)} %collective-permute-done.before, bf16[128,1024]{1,0:T(8,128)(2,1)} %bitcast.9, bf16[32,1024]{1,0:T(8,128)(2,1)S(1)} %collective-permute-done.1.after, f32[1,1024]{1,0:T(1,128)} %bitcast.13, s32[128,8]{1,0:T(8,128)} %broadcast_subtract_fusion.rel), custom_call_target="tpu_custom_call" | custom-call | flops 4000000 | bytes 1000000 | tf_op jit(solution)/shard_map/pallas_call | solution.py:64
  99.8 9.4 %shard_map.123 = (bf16[64,16,1536]{2,1,0:T(8,128)(2,1)}, bf16[64,8,1024]{2,1,0:T(8,128)(2,1)}, bf16[64,2,8,128]{3,2,1,0:T(8,128)(2,1)}, bf16[128,512]{1,0:T(8,12...) custom-call(bf16[192,1024]{1,0:T(8,128)(2,1)} %get-tuple-element.27., ...), custom_call_target="tpu_custom_call" | custom-call | flops 2000000000 | bytes 10000000 | tf_op jit(solution)/shard_map/pallas_call | solution.py:64
  109.2 21.0 %all_to_all.27.every = f32[8,128,128]{2,1,0:T(8,128)S(1)} all-to-all(f32[8,128,128]{2,1,0:T(8,128)S(1)} %get-tuple-element.31.fore), channel_id=1, replica_groups=mesh['zl'=4,'core'=2,'zh'=4,'y'=4,'x'=4] {'zl','core'}, dimensions={0} | all-to-all | bytes 1048576 | tf_op jit(solution)/shard_map/all_to_all | solution.py:450
  130.3 2.0 shard_map.124
  132.2 12.3 %all_to_all.28.plane = bf16[16,4,24,128]{3,2,1,0:T(8,128)(2,1)S(1)} all-to-all(bf16[16,4,24,128]{3,2,1,0:T(8,128)(2,1)} %get-tuple-element.46), channel_id=1, replica_groups=mesh['zl'=4,'core'=2,'zh'=4,'y'=4,'x'=4] {'y','x'}, dimensions={0} | all-to-all | bytes 786432 | tf_op jit(solution)/shard_map/all_to_all | solution.py:462
  145.2 11.2 %all-to-all-start.4 = ((bf16[32,24,128]{2,1,0:T(8,128)(2,1)}), bf16[32,24,128]{2,1,0:T(8,128)(2,1)S(1)}, u32[]{:S(2)}, u32[]{:S(2)}) async-start(bf16[32,24,128]{2,1,0:T(8,128)(2,1)} %bitcast.12), calls=%async_computation.4 | async-start | bytes 393216 | tf_op jit(solution)/shard_map/all_to_all | solution.py:489
  156.4 6.2 %shard_map.125 = (bf16[128,512]{1,0:T(8,128)(2,1)}, f32[128,1024]{1,0:T(8,128)}, bf16[32,1024]{1,0:T(8,128)(2,1)}, bf16[32,1024]{1,0:T(8,128)(2,1)}) custom-call(bf16[128,128]{1,0:T(8,128)(2,1)} %get-tuple-element.34.gf, bf16[64,2,8,128]{3,2,1,0:T(8,128)(2,1)} %get-tuple-element.35.whead_in.whead, bf16[64,8,1024]{2,1,0:T(8,128)(2,1)} %get-tuple-element.37.wout_in, ...), custom_call_target="tpu_custom_call" | custom-call | flops 1000000000 | bytes 4000000 | tf_op jit(solution)/shard_map/pallas_call | solution.py:64
  162.7 11.2 %collective-permute-start.7 = (bf16[32,1024]{1,0:T(8,128)(2,1)}, bf16[32,1024]{1,0:T(8,128)(2,1)S(1)}, u32[]{:S(2)}, u32[]{:S(2)}) collective-permute-start(bf16[32,1024]{1,0:T(8,128)(2,1)} %get-tuple-element.43), channel_id=1, source_target_pairs={{0,1},{1,2},{2,3},{3,4},{4,5},{5,6},{6,7},{7,8},{8,9},{9,10},{10,1... | collective-permute-start | bytes 196616 | tf_op jit(solution)/shard_map/ppermute | solution.py:480
  173.9 1.9 collective-permute-start.8
  176.1 16.3 %collective-permute-done.8.last = bf16[32,1024]{1,0:T(8,128)(2,1)S(1)} collective-permute-done((bf16[32,1024]{1,0:T(8,128)(2,1)}, bf16[32,1024]{1,0:T(8,128)(2,1)S(1)}, u32[]{:S(2)}, u32[]{:S(2)}) %collective-permute-start.8) | collective-permute-done | bytes 65568 | tf_op jit(solution)/shard_map/ppermute | solution.py:479
  192.4 5.2 %shard_map.126 = (f32[128,1024]{1,0:T(8,128)}, bf16[128,1024]{1,0:T(8,128)(2,1)}) custom-call(bf16[128,1024]{1,0:T(8,128)(2,1)} %bitcast.11, f32[1,1024]{1,0:T(1,128)} %bitcast.14, bf16[128,128]{1,0:T(8,128)(2,1)} %get-tuple-element.34.gf, bf16[64,2,8,128]{3,2,1,0:T(8,128)(2,1)} %get-tuple-element.35.whead_in.whead, ...), custom_call_target="tpu_custom_call" | custom-call | flops 1000000000 | bytes 4000000 | tf_op jit(solution)/shard_map/pallas_call | solution.py:64
  197.6 1.8 shard_map.128
  (18 shorter events, 3.4 us)
Async XLA Ops:
  2.4 25.5 %collective-permute-start.5 = (bf16[136,128]{1,0:T(8,128)(2,1)S(1)}, bf16[136,128]{1,0:T(8,128)(2,1)S(1)}, u32[]{:S(2)}, u32[]{:S(2)}) collective-permute-start(bf16[136,128]{1,0:T(8,128)(2,1)S(1)} %get-tuple-element.30), channel_id=1, source_target_pairs={{48,0},{0,16},{16,32},{32,48},{49,1},{1,17},{17,33},{33,49},{50,2}... | collective-permute-start | bytes 104456 | tf_op jit(solution)/shard_map/ppermute | solution.py:395
  11.5 16.4 %collective-permute-start.4 = (bf16[136,128]{1,0:T(8,128)(2,1)S(1)}, bf16[136,128]{1,0:T(8,128)(2,1)S(1)}, u32[]{:S(2)}, u32[]{:S(2)}) collective-permute-start(bf16[136,128]{1,0:T(8,128)(2,1)S(1)} %get-tuple-element.30), channel_id=1, source_target_pairs={{32,0},{48,16},{0,32},{16,48},{33,1},{49,17},{1,33},{17,49},{34,2}... | collective-permute-start | bytes 104456 | tf_op jit(solution)/shard_map/ppermute | solution.py:395
  22.4 10.6 %collective-permute-start.3 = (bf16[136,128]{1,0:T(8,128)(2,1)S(1)}, bf16[136,128]{1,0:T(8,128)(2,1)S(1)}, u32[]{:S(2)}, u32[]{:S(2)}) collective-permute-start(bf16[136,128]{1,0:T(8,128)(2,1)S(1)} %get-tuple-element.30), channel_id=1, source_target_pairs={{16,0},{32,16},{48,32},{0,48},{17,1},{33,17},{49,33},{1,49},{18,2}... | collective-permute-start | bytes 104456 | tf_op jit(solution)/shard_map/ppermute | solution.py:395
  34.7 26.9 %copy-start.1 = (bf16[16,136,128]{2,1,0:T(8,128)(2,1)S(1)}, bf16[16,136,128]{2,1,0:T(8,128)(2,1)}, u32[]{:S(2)}) copy-start(bf16[16,136,128]{2,1,0:T(8,128)(2,1)} %get-tuple-element.29) | copy-start | bytes 1671172
  34.7 44.8 %copy-start = (bf16[1,128,1024]{2,1,0:T(8,128)(2,1)S(1)}, bf16[1,128,1024]{2,1,0:T(8,128)(2,1)}, u32[]{:S(2)}) copy-start(bf16[1,128,1024]{2,1,0:T(8,128)(2,1)} %param.9) | copy-start | bytes 786436
  34.7 58.8 %copy-start.2 = (s32[128,8]{0,1:T(8,128)S(1)}, s32[128,8]{0,1:T(8,128)}, u32[]{:S(2)}) copy-start(s32[128,8]{0,1:T(8,128)} %param.16) | copy-start | bytes 12292
  59.6 40.2 %collective-permute-start.6 = (bf16[16,3,136,128]{3,2,1,0:T(8,128)(2,1)S(1)}, bf16[16,3,136,128]{3,2,1,0:T(8,128)(2,1)}, u32[]{:S(2)}, u32[]{:S(2)}) collective-permute-start(bf16[16,3,136,128]{3,2,1,0:T(8,128)(2,1)S(1)} %all_to_all.25.own1), channel_id=1, source_target_pairs={{0,64},{64,0},{1,65},{65,1},{2,66},{66,2},{3,67},{67,3},{4,68},{68... | collective-permute-start | bytes 5013512 | tf_op jit(solution)/shard_map/ppermute | solution.py:419
  77.5 22.2 %collective-permute-start.2 = (bf16[16,136,128]{2,1,0:T(8,128)(2,1)S(1)}, bf16[16,136,128]{2,1,0:T(8,128)(2,1)S(1)}, u32[]{:S(2)}, u32[]{:S(2)}) collective-permute-start(bf16[16,136,128]{2,1,0:T(8,128)(2,1)S(1)} %all_to_all.26.own0), channel_id=1, source_target_pairs={{0,64},{64,0},{1,65},{65,1},{2,66},{66,2},{3,67},{67,3},{4,68},{68... | collective-permute-start | bytes 1671176 | tf_op jit(solution)/shard_map/ppermute | solution.py:418
  79.5 18.2 %collective-permute-start.1 = (bf16[32,1024]{1,0:T(8,128)(2,1)S(1)}, bf16[32,1024]{1,0:T(8,128)(2,1)S(1)}, u32[]{:S(2)}, u32[]{:S(2)}) collective-permute-start(bf16[32,1024]{1,0:T(8,128)(2,1)S(1)} %get-tuple-element.50), channel_id=1, source_target_pairs={{1,0},{2,1},{3,2},{4,3},{5,4},{6,5},{7,6},{8,7},{9,8},{10,9},{11,1... | collective-permute-start | bytes 196616 | tf_op jit(solution)/shard_map/ppermute | solution.py:397
  82.0 15.7 %collective-permute-start = (bf16[32,1024]{1,0:T(8,128)(2,1)S(1)}, bf16[32,1024]{1,0:T(8,128)(2,1)S(1)}, u32[]{:S(2)}, u32[]{:S(2)}) collective-permute-start(bf16[32,1024]{1,0:T(8,128)(2,1)S(1)} %get-tuple-element.51), channel_id=1, source_target_pairs={{0,1},{1,2},{2,3},{3,4},{4,5},{5,6},{6,7},{7,8},{8,9},{9,10},{10,1... | collective-permute-start | bytes 196616 | tf_op jit(solution)/shard_map/ppermute | solution.py:396
  145.2 52.4 %all-to-all-start.4 = ((bf16[32,24,128]{2,1,0:T(8,128)(2,1)}), bf16[32,24,128]{2,1,0:T(8,128)(2,1)S(1)}, u32[]{:S(2)}, u32[]{:S(2)}) async-start(bf16[32,24,128]{2,1,0:T(8,128)(2,1)} %bitcast.12), calls=%async_computation.4 | async-start | bytes 393216 | tf_op jit(solution)/shard_map/all_to_all | solution.py:489
  162.7 13.4 %collective-permute-start.7 = (bf16[32,1024]{1,0:T(8,128)(2,1)}, bf16[32,1024]{1,0:T(8,128)(2,1)S(1)}, u32[]{:S(2)}, u32[]{:S(2)}) collective-permute-start(bf16[32,1024]{1,0:T(8,128)(2,1)} %get-tuple-element.43), channel_id=1, source_target_pairs={{0,1},{1,2},{2,3},{3,4},{4,5},{5,6},{6,7},{7,8},{8,9},{9,10},{10,1... | collective-permute-start | bytes 196616 | tf_op jit(solution)/shard_map/ppermute | solution.py:480
  173.9 18.5 %collective-permute-start.8 = (bf16[32,1024]{1,0:T(8,128)(2,1)}, bf16[32,1024]{1,0:T(8,128)(2,1)S(1)}, u32[]{:S(2)}, u32[]{:S(2)}) collective-permute-start(bf16[32,1024]{1,0:T(8,128)(2,1)} %get-tuple-element.44), channel_id=1, source_target_pairs={{1,0},{2,1},{3,2},{4,3},{5,4},{6,5},{7,6},{8,7},{9,8},{10,9},{11,1... | collective-permute-start | bytes 196616 | tf_op jit(solution)/shard_map/ppermute | solution.py:479

commit v3 on v2

--- a/solution.py
+++ b/solution.py
@@ -26,7 +26,6 @@
 MEMBER = ("zl", "core")
 GRID = ("zh", "y", "x")
 PLANE = ("y", "x")
-COLUMN = ("zl", "core", "zh")
 
 BF = jnp.bfloat16
 F32 = jnp.float32
@@ -109,7 +108,7 @@
         copy.wait()
 
 
-def pack_body(query, key, value, out, head, mine, plane, sems):
+def pack_body(query, key, value, out, head, column, mine, sems):
     rs, ro = query.shape[0], out.shape[0]
 
     def put(row, tile):
@@ -129,27 +128,15 @@
                 put(6 * rs + t * ro, out[:, lane : lane + LANE])
             put(6 * rs + 4 * ro, head[c * rs // 2 : (c + 1) * rs // 2, :])
 
-    send_out([(mine, plane.at[i]) for i in range(plane.shape[0])], sems)
-
-
-def rest_body(*refs):
-    *blocks, rest, sems = refs
-    send_out(
-        [
-            (block, rest.at[i, k])
-            for k, block in enumerate(blocks)
-            for i in range(rest.shape[0])
-        ],
-        sems,
-    )
+    send_out([(mine, column.at[i]) for i in range(column.shape[0])], sems)
 
 
 def forward_body(
-    zh_n, rs, ro, normed, states, count, own0, other0, own1, other1,
-    wqkv_out, wout_out, whead_out, q_out, kv_out, probs_out, mixed, out, fore,
+    zh_n, rs, ro, normed, states, count, own, other,
+    wqkv_out, wout_out, whead_out, q_out, kv_out, probs_out, mixed, out, fore, alone,
     wqkv, wout, whead, q, kv, probs, sq, so, sh, sems,
 ):
-    core, zh = lax.axis_index("core"), lax.axis_index("zh")
+    core = lax.axis_index("core")
 
     def leaving(i):
         src, dst = (
@@ -166,48 +153,51 @@
     qrows = 6 * rs
     orows = 4 * ro
 
-    def pieces(first, rest, c):
-        for k in range(zh_n):
-            at = pl.ds(lax.rem(zh + k, zh_n) * pn, pn)
-
-            def rows(start, size):
-                if k == 0:
-                    return first.at[:, pl.ds(start, size), :]
-                return rest.at[:, k - 1, pl.ds(start, size), :]
-
+    def inner(buf, c):
+        for zh in range(zh_n):
             for t in range(6):
                 yield (
-                    rows(t * rs, rs),
-                    wqkv.at[at, :, pl.ds((6 * c + t) * LANE, LANE)],
-                    sq.at[c, k, t],
+                    buf.at[:, zh, pl.ds(t * rs, rs), :],
+                    wqkv.at[pl.ds(zh * pn, pn), :, pl.ds((6 * c + t) * LANE, LANE)],
+                    sq.at[c, zh, t],
                 )
+
+    def outer(buf, c):
+        for zh in range(zh_n):
+            at = pl.ds(zh * pn, pn)
             for t in range(4):
                 yield (
-                    rows(qrows + t * ro, ro),
+                    buf.at[:, zh, pl.ds(qrows + t * ro, ro), :],
                     wout.at[at, :, pl.ds((4 * c + t) * LANE, LANE)],
-                    so.at[c, k, t],
+                    so.at[c, zh, t],
                 )
-            yield rows(qrows + orows, rs // 2), whead.at[at, c], sh.at[c, k]
-
-    def begin(a, b):
-        for c, pair in enumerate((a, b)):
-            for src, dst, sem in pieces(*pair, c):
-                pltpu.make_async_copy(src, dst, sem).start()
+            yield (
+                buf.at[:, zh, pl.ds(qrows + orows, rs // 2), :],
+                whead.at[at, c],
+                sh.at[c, zh],
+            )
+
+    def begin(*halves_of):
+        for part in (inner, outer):
+            for c in range(2):
+                for src, dst, sem in part(halves_of[c], c):
+                    pltpu.make_async_copy(src, dst, sem).start()
+
+    def end(part):
+        for c in range(2):
+            for src, dst, sem in part(own, c):
+                pltpu.make_async_copy(src, dst, sem).wait()
 
     @pl.when(core == 0)
     def _():
-        begin((own0, own1), (other0, other1))
+        begin(own, other)
 
     @pl.when(core != 0)
     def _():
-        begin((other0, other1), (own0, own1))
-
-    for c in range(2):
-        for src, dst, sem in pieces(own0, own1, c):
-            pltpu.make_async_copy(src, dst, sem).wait()
-
-    for i in range(3):
-        leaving(i).start()
+        begin(other, own)
+
+    end(inner)
+    leaving(0).start()
     rows = normed[...]
     weights = wqkv[...].reshape(D, 3 * HD)
     q[...] = nn(rows[HALO : HALO + PTS], weights[:, :HD]).astype(BF)
@@ -232,13 +222,17 @@
             got.append(nn(weight, v2))
         mixed[:, at] = jnp.where(halves((PTS, LANE), 0), got[0], got[1]).astype(BF)
     leaving(5).start()
+    end(outer)
+    for i in range(1, 3):
+        leaving(i).start()
     flat_out = wout[...].astype(F32).reshape(HD, D).astype(BF)
     flat_head = whead[...].astype(F32).reshape(D, NVAR).astype(BF)
     layer = (states[...].astype(F32) + nn(mixed[...], flat_out)).astype(BF)
     out[...] = layer
     mine = nn(layer, flat_head)
+    alone[...] = mine
     for i in range(fore.shape[0]):
-        fore[i] = mine
+        fore[i] = mine.astype(BF)
     for i in range(6):
         leaving(i).wait()
 
@@ -247,11 +241,12 @@
     return z * lax.rsqrt(z * z + smooth * smooth)
 
 
-def score_body(members, zh_n, every, fore, observed, mixed, out, gf, wg):
-    mine = fore[0]
+def score_body(members, zh_n, every, alone, observed, mixed, out, gf, wg):
+    mine = alone[...]
+    sent = mine.astype(BF).astype(F32)
     total = jnp.zeros_like(mine)
     for m in range(members):
-        total = total + slope(mine - every[m])
+        total = total + slope(sent - every[m].astype(F32))
     grad = (slope(mine - observed[...]) - total * (1.0 / (members - 1))).astype(BF)
     gf[...] = grad
     pn = wg.shape[0]
@@ -342,11 +337,19 @@
     grad[...] = (nt(gf[...], flat_head) + back).astype(BF)
 
 
-def spread_body(plane, spread):
-    total = plane[0].astype(F32)
-    for i in range(1, plane.shape[0]):
-        total = total + plane[i].astype(F32)
-    total = total.astype(BF)
+def added(parts):
+    total = parts[0].astype(F32)
+    for i in range(1, parts.shape[0]):
+        total = total + parts[i].astype(F32)
+    return total
+
+
+def sum_body(parts, total):
+    total[...] = added(parts).astype(BF)
+
+
+def spread_body(parts, spread):
+    total = added(parts).astype(BF)
     for i in range(spread.shape[0]):
         spread[i] = total
 
@@ -354,10 +357,7 @@
 def weights_body(scaling, parts, whead, mixing, head):
     flat_head = whead[...].astype(F32).reshape(D, NVAR).astype(BF)
     rb = head.shape[0]
-    total = jnp.zeros(parts.shape[1:], F32)
-    for i in range(parts.shape[0]):
-        total = total + parts[i].astype(F32)
-    total = total * scaling
+    total = added(parts) * scaling
     head[...] = total[:rb]
     factor = total[rb:]
     high = factor.astype(BF)
@@ -379,20 +379,16 @@
     up = [(i, i + 1) for i in range(devices - 1)]
     down = [(j, i) for i, j in up]
 
-    mine, plane = call(
+    column, _ = call(
         pack_body,
-        [((packed, LANE), BF), ((pn, packed, LANE), BF)],
+        [((zh_n, packed, LANE), BF), ((packed, LANE), BF)],
         (query, key, value, out_w, head_w),
-        "AAAAA>VH",
-        scratch=(pltpu.SemaphoreType.DMA((pn,)),),
+        "AAAAA>HV",
+        scratch=(pltpu.SemaphoreType.DMA((zh_n,)),),
         cost=(1e6, 1e6),
         limit=4,
     )
-    own0 = lax.all_to_all(plane, PLANE, 0, 0, tiled=True)
-    blocks = []
-    for k in range(1, zh_n):
-        turn = [((i + k) % zh_n, i) for i in range(zh_n)]
-        blocks.append(lax.ppermute(mine, "zh", turn))
+    column = lax.all_to_all(column, "zh", 0, 0, tiled=True)
     before = lax.ppermute(inputs[PTS - HALO :], GRID, up)
     after = lax.ppermute(inputs[:HALO], GRID, down)
     rel = neighbours - (lax.axis_index(GRID) * PTS - HALO)
@@ -405,19 +401,10 @@
         cost=(4e6, 1e6),
         limit=8,
     )
-    (rest,) = call(
-        rest_body,
-        [((pn, zh_n - 1, packed, LANE), BF)],
-        blocks,
-        "V" * (zh_n - 1) + ">H",
-        scratch=(pltpu.SemaphoreType.DMA((pn * (zh_n - 1),)),),
-        cost=(1e6, 2e6),
-        limit=4,
-    )
-    own1 = lax.all_to_all(rest, PLANE, 0, 0, tiled=True)
-    other0 = lax.ppermute(own0, "core", swap)
-    other1 = lax.ppermute(own1, "core", swap)
-    wqkv, wout, whead, q, kv, probs, mixed, out, fore = call(
+    spread = jnp.broadcast_to(column[None], (pn, *column.shape))
+    own = lax.all_to_all(spread, PLANE, 0, 0, tiled=True)
+    other = lax.ppermute(own, "core", swap)
+    wqkv, wout, whead, q, kv, probs, mixed, out, fore, alone = call(
         functools.partial(forward_body, zh_n, rs, ro),
         [
             ((devices, rs, 3 * HD), BF),
@@ -428,10 +415,11 @@
             ((HEADS, PTS, EXT), BF),
             ((PTS, HD), BF),
             ((PTS, D), BF),
-            ((members, PTS, NVAR), F32),
+            ((members, PTS, NVAR), BF),
+            ((PTS, NVAR), F32),
         ],
-        (normed, inputs, count, own0, other0, own1, other1),
-        "AAAVVVV>HHHHHHVVV",
+        (normed, inputs, count, own, other),
+        "AAAVV>HHHHHHVVVV",
         scratch=(
             pltpu.VMEM((devices, rs, 3 * HD), BF),
             pltpu.VMEM((devices, ro, D), BF),
@@ -454,8 +442,8 @@
             ((PTS, NVAR), BF),
             ((pn, zh_n, (D + HD) // devices, NVAR), BF),
         ],
-        (every, fore, observed, mixed, out),
-        "VVAVV>AA",
+        (every, alone, observed, mixed, out),
+        "VVVVV>AA",
         cost=(1e8, 2e6),
         limit=8,
     )
@@ -478,17 +466,24 @@
     )
     last = lax.ppermute(lower, GRID, down)
     first = lax.ppermute(upper, GRID, up)
-    (spread,) = call(
-        spread_body,
-        [((members, *wg.shape[1:]), BF)],
+    (partial,) = call(
+        sum_body,
+        [(wg.shape[1:], BF)],
         (plane,),
         "V>A",
         cost=(1e6, 1e6),
         limit=4,
     )
-    parts = lax.all_to_all(
-        spread.reshape(members * zh_n, *wg.shape[2:]), COLUMN, 0, 0, tiled=True
-    )
+    column = lax.all_to_all(partial, "zh", 0, 0, tiled=True)
+    (spread,) = call(
+        spread_body,
+        [((members, *wg.shape[2:]), BF)],
+        (column,),
+        "V>A",
+        cost=(1e6, 1e6),
+        limit=4,
+    )
+    parts = lax.all_to_all(spread, MEMBER, 0, 0, tiled=True)
     total, grad_input = call(
         final_body,
         [((PTS, D), F32), ((PTS, D), BF)],

time: 200 us -> 188 us (0.940)
  starting transfers between devices: 67.6 us -> 27.2 us
  blocking collectives: 74.2 us -> 112 us
  waiting for transfers between devices: 25.2 us -> 17.3 us
  Pallas kernels: 30.8 us -> 28.2 us
    all_to_all x2 -> x3, blocking collectives: 40.9 us -> 84.1 us  [the longest x1 30.7 us: shards(): own = lax.all_to_all(spread, PLANE, 0, 0, tiled=True)]
    ppermute x5 -> x1, starting transfers between devices: 29.3 us -> 1.91 us  [shards(): other = lax.ppermute(own, 'core', swap)]
    all_to_all x1, starting transfers between devices: 11.2 us -> 3.34 us  [shards(): parts = lax.all_to_all(spread, MEMBER, 0, 0, tiled=True)]
    all_to_all x1, blocking collectives: 21 us -> 15.8 us  [shards(): every = lax.all_to_all(fore, MEMBER, 0, 0, tiled=True)]
    ppermute x5 -> x1, waiting for transfers between devices: 5.16 us -> 0.01 us  [shards(): other = lax.ppermute(own, 'core', swap)]
    ppermute x1, starting transfers between devices: 11.2 us -> 6.08 us  [shards(): first = lax.ppermute(upper, GRID, up)]
    ppermute x1, waiting for transfers between devices: 3.45 us -> 0.01 us  [shards(): after = lax.ppermute(inputs[:HALO], GRID, down)]
    pallas_call x9, Pallas kernels: 30.8 us -> 28.2 us  [call(): pl.pallas_call(body, out_shape=tuple(shapes), in_specs=[SPECS[at] for at...]
  transfers between devices with their start and end apart: 10 -> 6, of which waited for: 4 -> 3; matrix products, arithmetic and copies ran while one was open for 0% -> 0% of each run, Pallas kernels for 7% -> 7%
where the time goes in v3:
time: 188 us; the launch traced here: 187 us
  blocking collectives  112 us (60%)
  Pallas kernels  28.2 us (15%)
  starting transfers between devices  27.2 us (14%)
  waiting for transfers between devices  17.3 us (9%)
    all_to_all x1, blocking collectives, shards(): own = lax.all_to_all(spread, PLANE, 0, 0, tiled=True)  30.7 us
    all_to_all x1, blocking collectives, shards(): column = lax.all_to_all(column, 'zh', 0, 0, tiled=True)  30.1 us
    pallas_call x9, Pallas kernels, call(): pl.pallas_call(body, out_shape=tuple(shapes), in_specs=[SPECS[at] for at...  28.2 us
    all_to_all x1, blocking collectives, shards(): column = lax.all_to_all(partial, 'zh', 0, 0, tiled=True)  23.3 us
    ppermute x1, waiting for transfers between devices, shards(): last = lax.ppermute(lower, GRID, down)  15.9 us
    all_to_all x1, blocking collectives, shards(): every = lax.all_to_all(fore, MEMBER, 0, 0, tiled=True)  15.8 us
    all_to_all x1, blocking collectives, shards(): plane = lax.all_to_all(wg, PLANE, 0, 0, tiled=True)  12.3 us
    ppermute x1, starting transfers between devices, shards(): before = lax.ppermute(inputs[PTS - HALO:], GRID, up)  11.2 us
  transfers between devices with their start and end apart: 6, of which 3 were waited for; matrix products, arithmetic and copies ran while one was open for 0% of the time, Pallas kernels for 7%

profile of v3, /device:TPU:30, one launch (start us, length us, event | category | flops | bytes accessed | tf_op | source)
XLA Modules:
  0.0 186.8 jit_solution(2295923898774426357)
XLA Ops:
  0.6 2.1 %shard_map.121 = (bf16[4,136,128]{2,1,0:T(8,128)(2,1)}, bf16[136,128]{1,0:T(8,128)(2,1)}) custom-call(bf16[16,512]{1,0:T(8,128)(2,1)} %query.1, bf16[16,512]{1,0:T(8,128)(2,1)} %key.1, bf16[16,512]{1,0:T(8,128)(2,1)} %value.1, bf16[8,1024]{1,0:T(8,128)(2,1)} %out.1, bf16[16,128]{1,0:T(8,128)(2,1)} %head.1), custom_call_target="tpu_custom_call" | custom-call | flops 1000000 | bytes 1000000 | tf_op jit(solution)/shard_map/pallas_call | solution.py:63
  2.7 30.1 %all_to_all.30 = bf16[4,136,128]{2,1,0:T(8,128)(2,1)S(1)} all-to-all(bf16[4,136,128]{2,1,0:T(8,128)(2,1)} %get-tuple-element.29), channel_id=1, replica_groups=mesh['zl'=4,'core'=2,'zh'=4,'y'=4,'x'=4] {'zh'}, dimensions={0} | all-to-all | bytes 278528 | tf_op jit(solution)/shard_map/all_to_all | solution.py:391
  32.8 0.3 broadcast_in_dim.12
  33.1 30.7 %all_to_all.31.own = bf16[16,4,136,128]{3,2,1,0:T(8,128)(2,1)S(1)} all-to-all(bf16[16,4,136,128]{3,2,1,0:T(8,128)(2,1)S(1)} %broadcast_in_dim.12), channel_id=1, replica_groups=mesh['zl'=4,'core'=2,'zh'=4,'y'=4,'x'=4] {'y','x'}, dimensions={0} | all-to-all | bytes 4456448 | tf_op jit(solution)/shard_map/all_to_all | solution.py:405
  63.8 1.9 %collective-permute-start.2 = (bf16[16,4,136,128]{3,2,1,0:T(8,128)(2,1)S(1)}, bf16[16,4,136,128]{3,2,1,0:T(8,128)(2,1)}, u32[]{:S(2)}, u32[]{:S(2)}) collective-permute-start(bf16[16,4,136,128]{3,2,1,0:T(8,128)(2,1)S(1)} %all_to_all.31.own), channel_id=1, source_target_pairs={{0,64},{64,0},{1,65},{65,1},{2,66},{66,2},{3,67},{67,3},{4,68},{68... | collective-permute-start | bytes 6684680 | tf_op jit(solution)/shard_map/ppermute | solution.py:406
  65.7 2.8 %collective-permute-start.1 = (bf16[32,1024]{1,0:T(8,128)(2,1)S(1)}, bf16[32,1024]{1,0:T(8,128)(2,1)S(1)}, u32[]{:S(2)}, u32[]{:S(2)}) collective-permute-start(bf16[32,1024]{1,0:T(8,128)(2,1)S(1)} %get-tuple-element.50), channel_id=1, source_target_pairs={{1,0},{2,1},{3,2},{4,3},{5,4},{6,5},{7,6},{8,7},{9,8},{10,9},{11,1... | collective-permute-start | bytes 196616 | tf_op jit(solution)/shard_map/ppermute | solution.py:393
  68.5 11.2 %collective-permute-start = (bf16[32,1024]{1,0:T(8,128)(2,1)S(1)}, bf16[32,1024]{1,0:T(8,128)(2,1)S(1)}, u32[]{:S(2)}, u32[]{:S(2)}) collective-permute-start(bf16[32,1024]{1,0:T(8,128)(2,1)S(1)} %get-tuple-element.51), channel_id=1, source_target_pairs={{0,1},{1,2},{2,3},{3,4},{4,5},{5,6},{6,7},{7,8},{8,9},{9,10},{10,1... | collective-permute-start | bytes 196616 | tf_op jit(solution)/shard_map/ppermute | solution.py:392
  79.9 0.6 broadcast_subtract_fusion.rel
  80.5 1.1 collective-permute-done.before
  81.6 2.1 %shard_map.120 = (bf16[192,1024]{1,0:T(8,128)(2,1)}, f32[128,192]{1,0:T(8,128)}) custom-call(bf16[32,1024]{1,0:T(8,128)(2,1)S(1)} %collective-permute-done.before, bf16[128,1024]{1,0:T(8,128)(2,1)} %bitcast.8, bf16[32,1024]{1,0:T(8,128)(2,1)S(1)} %collective-permute-done.1.after, f32[1,1024]{1,0:T(1,128)} %bitcast.11, s32[128,8]{1,0:T(8,128)} %broadcast_subtract_fusion.rel), custom_call_target="tpu_custom_call" | custom-call | flops 4000000 | bytes 1000000 | tf_op jit(solution)/shard_map/pallas_call | solution.py:63
  83.7 8.4 %shard_map.122 = (bf16[64,16,1536]{2,1,0:T(8,128)(2,1)}, bf16[64,8,1024]{2,1,0:T(8,128)(2,1)}, bf16[64,2,8,128]{3,2,1,0:T(8,128)(2,1)}, bf16[128,512]{1,0:T(8,12...) custom-call(bf16[192,1024]{1,0:T(8,128)(2,1)} %get-tuple-element.27., ...), custom_call_target="tpu_custom_call" | custom-call | flops 2000000000 | bytes 10000000 | tf_op jit(solution)/shard_map/pallas_call | solution.py:63
  92.1 15.8 %all_to_all.32.every = bf16[8,128,128]{2,1,0:T(8,128)(2,1)S(1)} all-to-all(bf16[8,128,128]{2,1,0:T(8,128)(2,1)S(1)} %get-tuple-element.30), channel_id=1, replica_groups=mesh['zl'=4,'core'=2,'zh'=4,'y'=4,'x'=4] {'zl','core'}, dimensions={0} | all-to-all | bytes 524288 | tf_op jit(solution)/shard_map/all_to_all | solution.py:438
  107.9 1.2 shard_map.123
  109.1 12.3 %all_to_all.33.parts = bf16[16,4,24,128]{3,2,1,0:T(8,128)(2,1)S(1)} all-to-all(bf16[16,4,24,128]{3,2,1,0:T(8,128)(2,1)} %get-tuple-element.46), channel_id=1, replica_groups=mesh['zl'=4,'core'=2,'zh'=4,'y'=4,'x'=4] {'y','x'}, dimensions={0} | all-to-all | bytes 786432 | tf_op jit(solution)/shard_map/all_to_all | solution.py:450
  121.3 0.7 shard_map.126
  122.0 23.3 %all_to_all.34.parts = bf16[4,24,128]{2,1,0:T(8,128)(2,1)S(1)} all-to-all(bf16[4,24,128]{2,1,0:T(8,128)(2,1)} %shard_map.126), channel_id=1, replica_groups=mesh['zl'=4,'core'=2,'zh'=4,'y'=4,'x'=4] {'zh'}, dimensions={0} | all-to-all | bytes 49152 | tf_op jit(solution)/shard_map/all_to_all | solution.py:477
  145.4 0.6 shard_map.127
  146.0 3.3 %all-to-all-start.5 = ((bf16[8,24,128]{2,1,0:T(8,128)(2,1)}), bf16[8,24,128]{2,1,0:T(8,128)(2,1)S(1)}, u32[]{:S(2)}, u32[]{:S(2)}) async-start(bf16[8,24,128]{2,1,0:T(8,128)(2,1)} %shard_map.127), calls=%async_computation.5 | async-start | bytes 98304 | tf_op jit(solution)/shard_map/all_to_all | solution.py:486
  149.3 6.2 %shard_map.124 = (bf16[128,512]{1,0:T(8,128)(2,1)}, f32[128,1024]{1,0:T(8,128)}, bf16[32,1024]{1,0:T(8,128)(2,1)}, bf16[32,1024]{1,0:T(8,128)(2,1)}) custom-call(bf16[128,128]{1,0:T(8,128)(2,1)} %get-tuple-element.34.gf, bf16[64,2,8,128]{3,2,1,0:T(8,128)(2,1)} %get-tuple-element.35.whead_in.whead, bf16[64,8,1024]{2,1,0:T(8,128)(2,1)} %get-tuple-element.37.wout_in, ...), custom_call_target="tpu_custom_call" | custom-call | flops 1000000000 | bytes 4000000 | tf_op jit(solution)/shard_map/pallas_call | solution.py:63
  155.5 6.1 %collective-permute-start.3 = (bf16[32,1024]{1,0:T(8,128)(2,1)}, bf16[32,1024]{1,0:T(8,128)(2,1)S(1)}, u32[]{:S(2)}, u32[]{:S(2)}) collective-permute-start(bf16[32,1024]{1,0:T(8,128)(2,1)} %get-tuple-element.43), channel_id=1, source_target_pairs={{0,1},{1,2},{2,3},{3,4},{4,5},{5,6},{6,7},{7,8},{8,9},{9,10},{10,1... | collective-permute-start | bytes 196616 | tf_op jit(solution)/shard_map/ppermute | solution.py:468
  161.6 1.9 %collective-permute-start.4 = (bf16[32,1024]{1,0:T(8,128)(2,1)}, bf16[32,1024]{1,0:T(8,128)(2,1)S(1)}, u32[]{:S(2)}, u32[]{:S(2)}) collective-permute-start(bf16[32,1024]{1,0:T(8,128)(2,1)} %get-tuple-element.44), channel_id=1, source_target_pairs={{1,0},{2,1},{3,2},{4,3},{5,4},{6,5},{7,6},{8,7},{9,8},{10,9},{11,1... | collective-permute-start | bytes 196616 | tf_op jit(solution)/shard_map/ppermute | solution.py:467
  163.8 15.9 %collective-permute-done.4.last = bf16[32,1024]{1,0:T(8,128)(2,1)S(1)} collective-permute-done((bf16[32,1024]{1,0:T(8,128)(2,1)}, bf16[32,1024]{1,0:T(8,128)(2,1)S(1)}, u32[]{:S(2)}, u32[]{:S(2)}) %collective-permute-start.4) | collective-permute-done | bytes 65568 | tf_op jit(solution)/shard_map/ppermute | solution.py:467
  179.8 5.2 %shard_map.125 = (f32[128,1024]{1,0:T(8,128)}, bf16[128,1024]{1,0:T(8,128)(2,1)}) custom-call(bf16[128,1024]{1,0:T(8,128)(2,1)} %bitcast.10, f32[1,1024]{1,0:T(1,128)} %bitcast.12, bf16[128,128]{1,0:T(8,128)(2,1)} %get-tuple-element.34.gf, bf16[64,2,8,128]{3,2,1,0:T(8,128)(2,1)} %get-tuple-element.35.whead_in.whead, ...), custom_call_target="tpu_custom_call" | custom-call | flops 1000000000 | bytes 4000000 | tf_op jit(solution)/shard_map/pallas_call | solution.py:63
  185.0 1.8 shard_map.128
  (12 shorter events, 0.4 us)
Async XLA Ops:
  33.1 32.6 %copy-start.1 = (bf16[1,128,1024]{2,1,0:T(8,128)(2,1)S(1)}, bf16[1,128,1024]{2,1,0:T(8,128)(2,1)}, u32[]{:S(2)}) copy-start(bf16[1,128,1024]{2,1,0:T(8,128)(2,1)} %param.9) | copy-start | bytes 786436
  33.1 46.6 %copy-start.2 = (s32[128,8]{0,1:T(8,128)S(1)}, s32[128,8]{0,1:T(8,128)}, u32[]{:S(2)}) copy-start(s32[128,8]{0,1:T(8,128)} %param.16) | copy-start | bytes 12292
  63.8 19.9 %collective-permute-start.2 = (bf16[16,4,136,128]{3,2,1,0:T(8,128)(2,1)S(1)}, bf16[16,4,136,128]{3,2,1,0:T(8,128)(2,1)}, u32[]{:S(2)}, u32[]{:S(2)}) collective-permute-start(bf16[16,4,136,128]{3,2,1,0:T(8,128)(2,1)S(1)} %all_to_all.31.own), channel_id=1, source_target_pairs={{0,64},{64,0},{1,65},{65,1},{2,66},{66,2},{3,67},{67,3},{4,68},{68... | collective-permute-start | bytes 6684680 | tf_op jit(solution)/shard_map/ppermute | solution.py:406
  65.7 14.8 %collective-permute-start.1 = (bf16[32,1024]{1,0:T(8,128)(2,1)S(1)}, bf16[32,1024]{1,0:T(8,128)(2,1)S(1)}, u32[]{:S(2)}, u32[]{:S(2)}) collective-permute-start(bf16[32,1024]{1,0:T(8,128)(2,1)S(1)} %get-tuple-element.50), channel_id=1, source_target_pairs={{1,0},{2,1},{3,2},{4,3},{5,4},{6,5},{7,6},{8,7},{9,8},{10,9},{11,1... | collective-permute-start | bytes 196616 | tf_op jit(solution)/shard_map/ppermute | solution.py:393
  68.5 13.1 %collective-permute-start = (bf16[32,1024]{1,0:T(8,128)(2,1)S(1)}, bf16[32,1024]{1,0:T(8,128)(2,1)S(1)}, u32[]{:S(2)}, u32[]{:S(2)}) collective-permute-start(bf16[32,1024]{1,0:T(8,128)(2,1)S(1)} %get-tuple-element.51), channel_id=1, source_target_pairs={{0,1},{1,2},{2,3},{3,4},{4,5},{5,6},{6,7},{7,8},{8,9},{9,10},{10,1... | collective-permute-start | bytes 196616 | tf_op jit(solution)/shard_map/ppermute | solution.py:392
  83.7 24.2 %copy-start = (f32[128,128]{1,0:T(8,128)S(1)}, f32[128,128]{1,0:T(8,128)}, u32[]{:S(2)}) copy-start(f32[128,128]{1,0:T(8,128)} %observed.1) | copy-start | bytes 196612
  146.0 39.0 %all-to-all-start.5 = ((bf16[8,24,128]{2,1,0:T(8,128)(2,1)}), bf16[8,24,128]{2,1,0:T(8,128)(2,1)S(1)}, u32[]{:S(2)}, u32[]{:S(2)}) async-start(bf16[8,24,128]{2,1,0:T(8,128)(2,1)} %shard_map.127), calls=%async_computation.5 | async-start | bytes 98304 | tf_op jit(solution)/shard_map/all_to_all | solution.py:486
  155.5 8.3 %collective-permute-start.3 = (bf16[32,1024]{1,0:T(8,128)(2,1)}, bf16[32,1024]{1,0:T(8,128)(2,1)S(1)}, u32[]{:S(2)}, u32[]{:S(2)}) collective-permute-start(bf16[32,1024]{1,0:T(8,128)(2,1)} %get-tuple-element.43), channel_id=1, source_target_pairs={{0,1},{1,2},{2,3},{3,4},{4,5},{5,6},{6,7},{7,8},{8,9},{9,10},{10,1... | collective-permute-start | bytes 196616 | tf_op jit(solution)/shard_map/ppermute | solution.py:468
  161.6 18.1 %collective-permute-start.4 = (bf16[32,1024]{1,0:T(8,128)(2,1)}, bf16[32,1024]{1,0:T(8,128)(2,1)S(1)}, u32[]{:S(2)}, u32[]{:S(2)}) collective-permute-start(bf16[32,1024]{1,0:T(8,128)(2,1)} %get-tuple-element.44), channel_id=1, source_target_pairs={{1,0},{2,1},{3,2},{4,3},{5,4},{6,5},{7,6},{8,7},{9,8},{10,9},{11,1... | collective-permute-start | bytes 196616 | tf_op jit(solution)/shard_map/ppermute | solution.py:467

commit v4 on v3

--- a/solution.py
+++ b/solution.py
@@ -80,15 +80,20 @@
     return center * inverse, inverse
 
 
-def prepare_body(before, own, after, scale, rel, normed, count):
-    for part, at in ((before, 0), (own, HALO), (after, HALO + PTS)):
-        centred, _ = normalised(part[...])
-        normed[at : at + part.shape[0], :] = (centred * scale[...]).astype(BF)
+def taps_body(own, scale, rel, normed, count):
+    centred, _ = normalised(own[...])
+    normed[...] = (centred * scale[...]).astype(BF)
     place = lax.broadcasted_iota(jnp.int32, (PTS, EXT), 1)
     total = jnp.zeros((PTS, EXT), F32)
     for k in range(KNB):
         total = total + (place == rel[:, k : k + 1]).astype(F32)
     count[...] = total
+
+
+def prepare_body(before, after, scale, first, last):
+    for part, normed in ((before, first), (after, last)):
+        centred, _ = normalised(part[...])
+        normed[...] = (centred * scale[...]).astype(BF)
 
 
 def halves(tile_shape, head):
@@ -132,61 +137,41 @@
 
 
 def forward_body(
-    zh_n, rs, ro, normed, states, count, own, other,
+    zh_n, rs, ro, ahead, normed, behind, states, count, own, other,
     wqkv_out, wout_out, whead_out, q_out, kv_out, probs_out, mixed, out, fore, alone,
-    wqkv, wout, whead, q, kv, probs, sq, so, sh, sems,
+    qkv, probs, added_out, sq, so, sh, sems,
 ):
     core = lax.axis_index("core")
-
-    def leaving(i):
-        src, dst = (
-            (wqkv, wqkv_out),
-            (wout, wout_out),
-            (whead, whead_out),
-            (q, q_out),
-            (kv, kv_out),
-            (probs, probs_out),
-        )[i]
-        return pltpu.make_async_copy(src, dst, sems.at[i])
-
-    pn = wqkv.shape[0] // zh_n
+    pn = own.shape[0]
     qrows = 6 * rs
     orows = 4 * ro
-
-    def inner(buf, c):
+    hr = rs // 2
+
+    def pieces(buf, c):
         for zh in range(zh_n):
+            at = pl.ds(zh * pn, pn)
             for t in range(6):
                 yield (
                     buf.at[:, zh, pl.ds(t * rs, rs), :],
-                    wqkv.at[pl.ds(zh * pn, pn), :, pl.ds((6 * c + t) * LANE, LANE)],
+                    wqkv_out.at[at, :, pl.ds((6 * c + t) * LANE, LANE)],
                     sq.at[c, zh, t],
                 )
-
-    def outer(buf, c):
-        for zh in range(zh_n):
-            at = pl.ds(zh * pn, pn)
             for t in range(4):
                 yield (
                     buf.at[:, zh, pl.ds(qrows + t * ro, ro), :],
-                    wout.at[at, :, pl.ds((4 * c + t) * LANE, LANE)],
+                    wout_out.at[at, :, pl.ds((4 * c + t) * LANE, LANE)],
                     so.at[c, zh, t],
                 )
             yield (
-                buf.at[:, zh, pl.ds(qrows + orows, rs // 2), :],
-                whead.at[at, c],
+                buf.at[:, zh, pl.ds(qrows + orows, hr), :],
+                whead_out.at[at, c],
                 sh.at[c, zh],
             )
 
     def begin(*halves_of):
-        for part in (inner, outer):
-            for c in range(2):
-                for src, dst, sem in part(halves_of[c], c):
-                    pltpu.make_async_copy(src, dst, sem).start()
-
-    def end(part):
         for c in range(2):
-            for src, dst, sem in part(own, c):
-                pltpu.make_async_copy(src, dst, sem).wait()
+            for src, dst, sem in pieces(halves_of[c], c):
+                pltpu.make_async_copy(src, dst, sem).start()
 
     @pl.when(core == 0)
     def _():
@@ -196,19 +181,37 @@
     def _():
         begin(other, own)
 
-    end(inner)
-    leaving(0).start()
-    rows = normed[...]
-    weights = wqkv[...].reshape(D, 3 * HD)
-    q[...] = nn(rows[HALO : HALO + PTS], weights[:, :HD]).astype(BF)
-    kv[...] = nn(rows, weights[:, HD:]).astype(BF)
-    for i in range(3, 5):
-        leaving(i).start()
+    rows = jnp.concatenate([ahead[...], normed[...], behind[...]], axis=0)
+    width = 6 * LANE
+    for buf, side in ((own, core), (other, 1 - core)):
+        total = jnp.zeros((EXT, width), F32)
+        for zh in range(zh_n):
+            tiles = [
+                buf[:, zh, t * rs : (t + 1) * rs, :].reshape(pn * rs, LANE)
+                for t in range(6)
+            ]
+            depth = pn * rs
+            total = total + nn(
+                rows[:, zh * depth : (zh + 1) * depth], jnp.concatenate(tiles, axis=1)
+            )
+        qkv[:, pl.ds(pl.multiple_of(side * width, width), width)] = total.astype(BF)
+    leaving = fetched(
+        (
+            (qkv.at[HALO : HALO + PTS, 0:HD], q_out),
+            (qkv.at[:, HD : 3 * HD], kv_out),
+            (probs, probs_out),
+        ),
+        sems,
+    )
+    leaving[0].start()
+    leaving[1].start()
     times = count[...]
     here = times > 0
     for pair in range(HEADS // 2):
         at = pl.ds(pair * LANE, LANE)
-        q2, k2, v2 = q[:, at], kv[:, at], kv[:, pl.ds(HD + pair * LANE, LANE)]
+        q2 = qkv[HALO : HALO + PTS, pair * LANE : (pair + 1) * LANE]
+        k2 = qkv[:, HD + pair * LANE : HD + (pair + 1) * LANE]
+        v2 = qkv[:, 2 * HD + pair * LANE : 2 * HD + (pair + 1) * LANE]
         got = []
         for side in range(2):
             chosen = jnp.where(halves((PTS, LANE), side), q2, jnp.zeros_like(q2))
@@ -221,27 +224,56 @@
             probs[2 * pair + side] = weight
             got.append(nn(weight, v2))
         mixed[:, at] = jnp.where(halves((PTS, LANE), 0), got[0], got[1]).astype(BF)
-    leaving(5).start()
-    end(outer)
-    for i in range(1, 3):
-        leaving(i).start()
-    flat_out = wout[...].astype(F32).reshape(HD, D).astype(BF)
-    flat_head = whead[...].astype(F32).reshape(D, NVAR).astype(BF)
-    layer = (states[...].astype(F32) + nn(mixed[...], flat_out)).astype(BF)
+    leaving[2].start()
+    width = 4 * LANE
+    attended = mixed[...]
+    for buf, side in ((own, core), (other, 1 - core)):
+        total = jnp.zeros((PTS, width), F32)
+        depth = pn * ro
+        for zh in range(zh_n):
+            tiles = [
+                buf[:, zh, qrows + t * ro : qrows + (t + 1) * ro, :]
+                .astype(F32)
+                .reshape(depth, LANE)
+                .astype(BF)
+                for t in range(4)
+            ]
+            total = total + nn(
+                attended[:, zh * depth : (zh + 1) * depth],
+                jnp.concatenate(tiles, axis=1),
+            )
+        added_out[:, pl.ds(pl.multiple_of(side * width, width), width)] = total
+    layer = (states[...].astype(F32) + added_out[...]).astype(BF)
     out[...] = layer
+    blocks = [
+        [
+            buf[:, zh, qrows + orows : qrows + orows + hr, :].astype(F32)
+            for buf in (own, other)
+        ]
+        for zh in range(zh_n)
+    ]
+    mine_first = jnp.full((1, 1, 1), core, jnp.int32) == 0
+    ordered = [
+        jnp.stack([jnp.where(mine_first, a, b), jnp.where(mine_first, b, a)], axis=1)
+        for a, b in blocks
+    ]
+    flat_head = jnp.concatenate(ordered, axis=0).reshape(D, NVAR).astype(BF)
     mine = nn(layer, flat_head)
     alone[...] = mine
     for i in range(fore.shape[0]):
         fore[i] = mine.astype(BF)
-    for i in range(6):
-        leaving(i).wait()
+    for c in range(2):
+        for src, dst, sem in pieces(own, c):
+            pltpu.make_async_copy(src, dst, sem).wait()
+    for copy in leaving:
+        copy.wait()
 
 
 def slope(z):
     return z * lax.rsqrt(z * z + smooth * smooth)
 
 
-def score_body(members, zh_n, every, alone, observed, mixed, out, gf, wg):
+def score_body(members, zh_n, every, alone, observed, mixed, out, gf, held, wg):
     mine = alone[...]
     sent = mine.astype(BF).astype(F32)
     total = jnp.zeros_like(mine)
@@ -249,6 +281,7 @@
         total = total + slope(sent - every[m].astype(F32))
     grad = (slope(mine - observed[...]) - total * (1.0 / (members - 1))).astype(BF)
     gf[...] = grad
+    held[...] = grad
     pn = wg.shape[0]
     heads = tn(out[...], grad)
     factor = tn(mixed[...], grad)
@@ -311,21 +344,13 @@
             upper[:, where_at] = total[HALO + PTS :].astype(BF)
 
 
-def final_body(
-    states, scale, gf, whead_in, wqkv_in, gq, mid, first, last, total, grad,
-    whead, wqkv, sems,
-):
-    copies = fetched(((wqkv_in, wqkv), (whead_in, whead)), sems)
-    for copy in copies:
-        copy.start()
+def final_body(states, scale, gf, whead, wqkv, gq, mid, first, last, total, grad):
     centred, inverse = normalised(states[...])
-    copies[1].wait()
     flat_head = whead[...].astype(F32).reshape(D, NVAR).astype(BF)
     total[...] = mid[...]
     total[:HALO, :] += first[...].astype(F32)
     total[PTS - HALO :, :] += last[...].astype(F32)
     kvs = total[...].astype(BF)
-    copies[0].wait()
     weights = wqkv[...].reshape(D, 3 * HD)
     gn = nt(gq[...], weights[:, :HD]) + nt(kvs, weights[:, HD:])
     g = gn * scale[...]
@@ -394,10 +419,18 @@
     rel = neighbours - (lax.axis_index(GRID) * PTS - HALO)
     scale = norm_scale.reshape(1, D)
     normed, count = call(
+        taps_body,
+        [((PTS, D), BF), ((PTS, EXT), F32)],
+        (inputs, scale, rel),
+        "AAA>AA",
+        cost=(4e6, 1e6),
+        limit=8,
+    )
+    ahead, behind = call(
         prepare_body,
-        [((EXT, D), BF), ((PTS, EXT), F32)],
-        (before, inputs, after, scale, rel),
-        "VAVAA>AA",
+        [((HALO, D), BF), ((HALO, D), BF)],
+        (before, after, scale),
+        "VVA>VV",
         cost=(4e6, 1e6),
         limit=8,
     )
@@ -418,32 +451,30 @@
             ((members, PTS, NVAR), BF),
             ((PTS, NVAR), F32),
         ],
-        (normed, inputs, count, own, other),
-        "AAAVV>HHHHHHVVVV",
+        (ahead, normed, behind, inputs, count, own, other),
+        "VAVAAVV>HHHHHHVVVV",
         scratch=(
-            pltpu.VMEM((devices, rs, 3 * HD), BF),
-            pltpu.VMEM((devices, ro, D), BF),
-            pltpu.VMEM((devices, 2, rs // 2, NVAR), BF),
-            pltpu.VMEM((PTS, HD), BF),
-            pltpu.VMEM((EXT, D), BF),
+            pltpu.VMEM((EXT, 3 * HD), BF),
             pltpu.VMEM((HEADS, PTS, EXT), BF),
+            pltpu.VMEM((PTS, D), F32),
             pltpu.SemaphoreType.DMA((2, zh_n, 6)),
             pltpu.SemaphoreType.DMA((2, zh_n, 4)),
             pltpu.SemaphoreType.DMA((2, zh_n)),
-            pltpu.SemaphoreType.DMA((6,)),
+            pltpu.SemaphoreType.DMA((3,)),
         ),
         cost=(2e9, 1e7),
         limit=24,
     )
     every = lax.all_to_all(fore, MEMBER, 0, 0, tiled=True)
-    gf, wg = call(
+    gf, held, wg = call(
         functools.partial(score_body, members, zh_n),
         [
+            ((PTS, NVAR), BF),
             ((PTS, NVAR), BF),
             ((pn, zh_n, (D + HD) // devices, NVAR), BF),
         ],
         (every, alone, observed, mixed, out),
-        "VVVVV>AA",
+        "VVVVV>VAA",
         cost=(1e8, 2e6),
         limit=8,
     )
@@ -452,7 +483,7 @@
         backward_body,
         [((PTS, HD), BF), ((PTS, D), F32), ((HALO, D), BF), ((HALO, D), BF)],
         (gf, whead, wout, q, kv, probs),
-        "AHHHHH>AAAA",
+        "VHHHHH>AAAA",
         scratch=(
             pltpu.VMEM(whead.shape, BF),
             pltpu.VMEM(wout.shape, BF),
@@ -487,13 +518,8 @@
     total, grad_input = call(
         final_body,
         [((PTS, D), F32), ((PTS, D), BF)],
-        (inputs, scale, gf, whead, wqkv, gq, mid, first, last),
-        "AAAHHAAVV>AA",
-        scratch=(
-            pltpu.VMEM(whead.shape, BF),
-            pltpu.VMEM(wqkv.shape, BF),
-            pltpu.SemaphoreType.DMA((2,)),
-        ),
+        (inputs, scale, held, whead, wqkv, gq, mid, first, last),
+        "AAAAVAAVV>AA",
         cost=(1e9, 4e6),
         limit=16,
     )

time: 188 us -> 184 us (0.979)
  Pallas kernels: 28.2 us -> 25.9 us
    pallas_call x9 -> x10, Pallas kernels: 28.2 us -> 25.9 us  [call(): pl.pallas_call(body, out_shape=tuple(shapes), in_specs=[SPECS[at] for at...]
  transfers between devices with their start and end apart: 6 -> 6, of which waited for: 3 -> 2; matrix products, arithmetic and copies ran while one was open for 0% -> 0% of each run, Pallas kernels for 7% -> 6%
where the time goes in v4:
time: 184 us; the launch traced here: 183 us
  blocking collectives  111 us (60%)
  starting transfers between devices  27.2 us (15%)
  Pallas kernels  25.9 us (14%)
  waiting for transfers between devices  16.2 us (9%)
    all_to_all x1, blocking collectives, shards(): own = lax.all_to_all(spread, PLANE, 0, 0, tiled=True)  30.7 us
    all_to_all x1, blocking collectives, shards(): column = lax.all_to_all(column, 'zh', 0, 0, tiled=True)  30.1 us
    pallas_call x10, Pallas kernels, call(): pl.pallas_call(body, out_shape=tuple(shapes), in_specs=[SPECS[at] for at...  25.9 us
    all_to_all x1, blocking collectives, shards(): column = lax.all_to_all(partial, 'zh', 0, 0, tiled=True)  23.5 us
    ppermute x1, waiting for transfers between devices, shards(): last = lax.ppermute(lower, GRID, down)  15.9 us
    all_to_all x1, blocking collectives, shards(): every = lax.all_to_all(fore, MEMBER, 0, 0, tiled=True)  15 us
    all_to_all x1, blocking collectives, shards(): plane = lax.all_to_all(wg, PLANE, 0, 0, tiled=True)  12.3 us
    ppermute x1, starting transfers between devices, shards(): before = lax.ppermute(inputs[PTS - HALO:], GRID, up)  11.2 us
  transfers between devices with their start and end apart: 6, of which 2 were waited for; matrix products, arithmetic and copies ran while one was open for 0% of the time, Pallas kernels for 6%

profile of v4, /device:TPU:30, one launch (start us, length us, event | category | flops | bytes accessed | tf_op | source)
XLA Modules:
  0.0 182.7 jit_solution(7040111443921651761)
XLA Ops:
  0.6 2.1 %shard_map.122 = (bf16[4,136,128]{2,1,0:T(8,128)(2,1)}, bf16[136,128]{1,0:T(8,128)(2,1)}) custom-call(bf16[16,512]{1,0:T(8,128)(2,1)} %query.1, bf16[16,512]{1,0:T(8,128)(2,1)} %key.1, bf16[16,512]{1,0:T(8,128)(2,1)} %value.1, bf16[8,1024]{1,0:T(8,128)(2,1)} %out.1, bf16[16,128]{1,0:T(8,128)(2,1)} %head.1), custom_call_target="tpu_custom_call" | custom-call | flops 1000000 | bytes 1000000 | tf_op jit(solution)/shard_map/pallas_call | solution.py:63
  2.7 30.1 %all_to_all.30 = bf16[4,136,128]{2,1,0:T(8,128)(2,1)S(1)} all-to-all(bf16[4,136,128]{2,1,0:T(8,128)(2,1)} %get-tuple-element.34), channel_id=1, replica_groups=mesh['zl'=4,'core'=2,'zh'=4,'y'=4,'x'=4] {'zh'}, dimensions={0} | all-to-all | bytes 278528 | tf_op jit(solution)/shard_map/all_to_all | solution.py:416
  32.8 0.3 broadcast_in_dim.12
  33.1 30.7 %all_to_all.31.own = bf16[16,4,136,128]{3,2,1,0:T(8,128)(2,1)S(1)} all-to-all(bf16[16,4,136,128]{3,2,1,0:T(8,128)(2,1)S(1)} %broadcast_in_dim.12), channel_id=1, replica_groups=mesh['zl'=4,'core'=2,'zh'=4,'y'=4,'x'=4] {'y','x'}, dimensions={0} | all-to-all | bytes 4456448 | tf_op jit(solution)/shard_map/all_to_all | solution.py:438
  63.8 1.9 %collective-permute-start.2 = (bf16[16,4,136,128]{3,2,1,0:T(8,128)(2,1)S(1)}, bf16[16,4,136,128]{3,2,1,0:T(8,128)(2,1)}, u32[]{:S(2)}, u32[]{:S(2)}) collective-permute-start(bf16[16,4,136,128]{3,2,1,0:T(8,128)(2,1)S(1)} %all_to_all.31.own), channel_id=1, source_target_pairs={{0,64},{64,0},{1,65},{65,1},{2,66},{66,2},{3,67},{67,3},{4,68},{68... | collective-permute-start | bytes 6684680 | tf_op jit(solution)/shard_map/ppermute | solution.py:439
  65.8 2.8 %collective-permute-start.1 = (bf16[32,1024]{1,0:T(8,128)(2,1)S(1)}, bf16[32,1024]{1,0:T(8,128)(2,1)S(1)}, u32[]{:S(2)}, u32[]{:S(2)}) collective-permute-start(bf16[32,1024]{1,0:T(8,128)(2,1)S(1)} %get-tuple-element.56), channel_id=1, source_target_pairs={{1,0},{2,1},{3,2},{4,3},{5,4},{6,5},{7,6},{8,7},{9,8},{10,9},{11,1... | collective-permute-start | bytes 196616 | tf_op jit(solution)/shard_map/ppermute | solution.py:418
  68.5 11.2 %collective-permute-start = (bf16[32,1024]{1,0:T(8,128)(2,1)S(1)}, bf16[32,1024]{1,0:T(8,128)(2,1)S(1)}, u32[]{:S(2)}, u32[]{:S(2)}) collective-permute-start(bf16[32,1024]{1,0:T(8,128)(2,1)S(1)} %get-tuple-element.57), channel_id=1, source_target_pairs={{0,1},{1,2},{2,3},{3,4},{4,5},{5,6},{6,7},{7,8},{8,9},{9,10},{10,1... | collective-permute-start | bytes 196616 | tf_op jit(solution)/shard_map/ppermute | solution.py:417
  79.9 0.6 broadcast_subtract_fusion.rel
  80.5 2.0 %shard_map.121 = (bf16[128,1024]{1,0:T(8,128)(2,1)}, f32[128,192]{1,0:T(8,128)}) custom-call(bf16[128,1024]{1,0:T(8,128)(2,1)} %bitcast.8, f32[1,1024]{1,0:T(1,128)} %bitcast.11, s32[128,8]{1,0:T(8,128)} %broadcast_subtract_fusion.rel), custom_call_target="tpu_custom_call" | custom-call | flops 4000000 | bytes 1000000 | tf_op jit(solution)/shard_map/pallas_call | solution.py:63
  82.5 0.9 shard_map.120
  83.4 7.9 %shard_map.123 = (bf16[64,16,1536]{2,1,0:T(8,128)(2,1)}, bf16[64,8,1024]{2,1,0:T(8,128)(2,1)}, bf16[64,2,8,128]{3,2,1,0:T(8,128)(2,1)}, bf16[128,512]{1,0:T(8,12...) custom-call(bf16[32,1024]{1,0:T(8,128)(2,1)S(1)} %get-tuple-element., ...), custom_call_target="tpu_custom_call" | custom-call | flops 2000000000 | bytes 10000000 | tf_op jit(solution)/shard_map/pallas_call | solution.py:63
  91.3 15.0 %all_to_all.32.every = bf16[8,128,128]{2,1,0:T(8,128)(2,1)S(1)} all-to-all(bf16[8,128,128]{2,1,0:T(8,128)(2,1)S(1)} %get-tuple-element.35), channel_id=1, replica_groups=mesh['zl'=4,'core'=2,'zh'=4,'y'=4,'x'=4] {'zl','core'}, dimensions={0} | all-to-all | bytes 524288 | tf_op jit(solution)/shard_map/all_to_all | solution.py:468
  106.3 1.2 shard_map.124
  107.4 12.3 %all_to_all.33.parts = bf16[16,4,24,128]{3,2,1,0:T(8,128)(2,1)S(1)} all-to-all(bf16[16,4,24,128]{3,2,1,0:T(8,128)(2,1)} %get-tuple-element.52), channel_id=1, replica_groups=mesh['zl'=4,'core'=2,'zh'=4,'y'=4,'x'=4] {'y','x'}, dimensions={0} | all-to-all | bytes 786432 | tf_op jit(solution)/shard_map/all_to_all | solution.py:481
  119.7 0.7 shard_map.127
  120.4 23.5 %all_to_all.34.parts = bf16[4,24,128]{2,1,0:T(8,128)(2,1)S(1)} all-to-all(bf16[4,24,128]{2,1,0:T(8,128)(2,1)} %shard_map.127), channel_id=1, replica_groups=mesh['zl'=4,'core'=2,'zh'=4,'y'=4,'x'=4] {'zh'}, dimensions={0} | all-to-all | bytes 49152 | tf_op jit(solution)/shard_map/all_to_all | solution.py:508
  143.8 0.6 shard_map.128
  144.5 3.3 %all-to-all-start.5 = ((bf16[8,24,128]{2,1,0:T(8,128)(2,1)}), bf16[8,24,128]{2,1,0:T(8,128)(2,1)S(1)}, u32[]{:S(2)}, u32[]{:S(2)}) async-start(bf16[8,24,128]{2,1,0:T(8,128)(2,1)} %shard_map.128), calls=%async_computation.5 | async-start | bytes 98304 | tf_op jit(solution)/shard_map/all_to_all | solution.py:517
  147.8 5.4 %shard_map.125 = (bf16[128,512]{1,0:T(8,128)(2,1)}, f32[128,1024]{1,0:T(8,128)}, bf16[32,1024]{1,0:T(8,128)(2,1)}, bf16[32,1024]{1,0:T(8,128)(2,1)}) custom-call(bf16[128,128]{1,0:T(8,128)(2,1)S(1)} %get-tuple-element.42.gf, bf16[64,2,8,128]{3,2,1,0:T(8,128)(2,1)} %get-tuple-element.40.whead_in.whead, bf16[64,8,1024]{2,1,0:T(8,128)(2,1)} %get-tuple-element.43.wout_in, ...), custom_call_target="tpu_custom_call" | custom-call | flops 1000000000 | bytes 4000000 | tf_op jit(solution)/shard_map/pallas_call | solution.py:63
  153.3 6.1 %collective-permute-start.3 = (bf16[32,1024]{1,0:T(8,128)(2,1)}, bf16[32,1024]{1,0:T(8,128)(2,1)S(1)}, u32[]{:S(2)}, u32[]{:S(2)}) collective-permute-start(bf16[32,1024]{1,0:T(8,128)(2,1)} %get-tuple-element.49), channel_id=1, source_target_pairs={{0,1},{1,2},{2,3},{3,4},{4,5},{5,6},{6,7},{7,8},{8,9},{9,10},{10,1... | collective-permute-start | bytes 196616 | tf_op jit(solution)/shard_map/ppermute | solution.py:499
  159.4 1.9 %collective-permute-start.4 = (bf16[32,1024]{1,0:T(8,128)(2,1)}, bf16[32,1024]{1,0:T(8,128)(2,1)S(1)}, u32[]{:S(2)}, u32[]{:S(2)}) collective-permute-start(bf16[32,1024]{1,0:T(8,128)(2,1)} %get-tuple-element.50), channel_id=1, source_target_pairs={{1,0},{2,1},{3,2},{4,3},{5,4},{6,5},{7,6},{8,7},{9,8},{10,9},{11,1... | collective-permute-start | bytes 196616 | tf_op jit(solution)/shard_map/ppermute | solution.py:498
  161.6 15.9 %collective-permute-done.4.last = bf16[32,1024]{1,0:T(8,128)(2,1)S(1)} collective-permute-done((bf16[32,1024]{1,0:T(8,128)(2,1)}, bf16[32,1024]{1,0:T(8,128)(2,1)S(1)}, u32[]{:S(2)}, u32[]{:S(2)}) %collective-permute-start.4) | collective-permute-done | bytes 65568 | tf_op jit(solution)/shard_map/ppermute | solution.py:498
  177.5 3.3 %shard_map.126 = (f32[128,1024]{1,0:T(8,128)}, bf16[128,1024]{1,0:T(8,128)(2,1)}) custom-call(bf16[128,1024]{1,0:T(8,128)(2,1)} %bitcast.10, f32[1,1024]{1,0:T(1,128)} %bitcast.13, bf16[128,128]{1,0:T(8,128)(2,1)} %get-tuple-element.39.gf, bf16[64,2,8,128]{3,2,1,0:T(8,128)(2,1)} %get-tuple-element.40.whead_in.whead, bf16[64,16,1536]{2,1,0:T(8,128)(2,1)S(1)} %copy-done, ...), custom_call_target="tpu_custom_call" | custom-call | flops 1000000000 | bytes 4000000 | tf_op jit(solution)/shard_map/pallas_call | solution.py:63
  180.9 1.8 shard_map.129
  (15 shorter events, 0.4 us)
Async XLA Ops:
  33.1 32.6 %copy-start.2 = (bf16[1,128,1024]{2,1,0:T(8,128)(2,1)S(1)}, bf16[1,128,1024]{2,1,0:T(8,128)(2,1)}, u32[]{:S(2)}) copy-start(bf16[1,128,1024]{2,1,0:T(8,128)(2,1)} %param.9) | copy-start | bytes 786436
  33.1 46.6 %copy-start.3 = (s32[128,8]{0,1:T(8,128)S(1)}, s32[128,8]{0,1:T(8,128)}, u32[]{:S(2)}) copy-start(s32[128,8]{0,1:T(8,128)} %param.16) | copy-start | bytes 12292
  63.8 19.6 %collective-permute-start.2 = (bf16[16,4,136,128]{3,2,1,0:T(8,128)(2,1)S(1)}, bf16[16,4,136,128]{3,2,1,0:T(8,128)(2,1)}, u32[]{:S(2)}, u32[]{:S(2)}) collective-permute-start(bf16[16,4,136,128]{3,2,1,0:T(8,128)(2,1)S(1)} %all_to_all.31.own), channel_id=1, source_target_pairs={{0,64},{64,0},{1,65},{65,1},{2,66},{66,2},{3,67},{67,3},{4,68},{68... | collective-permute-start | bytes 6684680 | tf_op jit(solution)/shard_map/ppermute | solution.py:439
  65.8 16.7 %collective-permute-start.1 = (bf16[32,1024]{1,0:T(8,128)(2,1)S(1)}, bf16[32,1024]{1,0:T(8,128)(2,1)S(1)}, u32[]{:S(2)}, u32[]{:S(2)}) collective-permute-start(bf16[32,1024]{1,0:T(8,128)(2,1)S(1)} %get-tuple-element.56), channel_id=1, source_target_pairs={{1,0},{2,1},{3,2},{4,3},{5,4},{6,5},{7,6},{8,7},{9,8},{10,9},{11,1... | collective-permute-start | bytes 196616 | tf_op jit(solution)/shard_map/ppermute | solution.py:418
  68.5 13.9 %collective-permute-start = (bf16[32,1024]{1,0:T(8,128)(2,1)S(1)}, bf16[32,1024]{1,0:T(8,128)(2,1)S(1)}, u32[]{:S(2)}, u32[]{:S(2)}) collective-permute-start(bf16[32,1024]{1,0:T(8,128)(2,1)S(1)} %get-tuple-element.57), channel_id=1, source_target_pairs={{0,1},{1,2},{2,3},{3,4},{4,5},{5,6},{6,7},{7,8},{8,9},{9,10},{10,1... | collective-permute-start | bytes 196616 | tf_op jit(solution)/shard_map/ppermute | solution.py:417
  83.4 22.9 %copy-start.1 = (f32[128,128]{1,0:T(8,128)S(1)}, f32[128,128]{1,0:T(8,128)}, u32[]{:S(2)}) copy-start(f32[128,128]{1,0:T(8,128)} %observed.1) | copy-start | bytes 196612
  119.7 57.8 %copy-start = (bf16[64,16,1536]{2,1,0:T(8,128)(2,1)S(1)}, bf16[64,16,1536]{2,1,0:T(8,128)(2,1)}, u32[]{:S(2)}) copy-start(bf16[64,16,1536]{2,1,0:T(8,128)(2,1)} %get-tuple-element.41.wqkv) | copy-start | bytes 9437188
  144.5 36.4 %all-to-all-start.5 = ((bf16[8,24,128]{2,1,0:T(8,128)(2,1)}), bf16[8,24,128]{2,1,0:T(8,128)(2,1)S(1)}, u32[]{:S(2)}, u32[]{:S(2)}) async-start(bf16[8,24,128]{2,1,0:T(8,128)(2,1)} %shard_map.128), calls=%async_computation.5 | async-start | bytes 98304 | tf_op jit(solution)/shard_map/all_to_all | solution.py:517
  153.3 8.3 %collective-permute-start.3 = (bf16[32,1024]{1,0:T(8,128)(2,1)}, bf16[32,1024]{1,0:T(8,128)(2,1)S(1)}, u32[]{:S(2)}, u32[]{:S(2)}) collective-permute-start(bf16[32,1024]{1,0:T(8,128)(2,1)} %get-tuple-element.49), channel_id=1, source_target_pairs={{0,1},{1,2},{2,3},{3,4},{4,5},{5,6},{6,7},{7,8},{8,9},{9,10},{10,1... | collective-permute-start | bytes 196616 | tf_op jit(solution)/shard_map/ppermute | solution.py:499
  159.4 18.1 %collective-permute-start.4 = (bf16[32,1024]{1,0:T(8,128)(2,1)}, bf16[32,1024]{1,0:T(8,128)(2,1)S(1)}, u32[]{:S(2)}, u32[]{:S(2)}) collective-permute-start(bf16[32,1024]{1,0:T(8,128)(2,1)} %get-tuple-element.50), channel_id=1, source_target_pairs={{1,0},{2,1},{3,2},{4,3},{5,4},{6,5},{7,6},{8,7},{9,8},{10,9},{11,1... | collective-permute-start | bytes 196616 | tf_op jit(solution)/shard_map/ppermute | solution.py:498

commit v5 on v4

--- a/solution.py
+++ b/solution.py
@@ -136,65 +136,59 @@
     send_out([(mine, column.at[i]) for i in range(column.shape[0])], sems)
 
 
+def places(side, ny, nx):
+    return [
+        jnp.where(side == 0, y * nx + x, x * ny + y)
+        for y in range(ny)
+        for x in range(nx)
+    ]
+
+
+def tile_at(buf, order, zh, start, size):
+    return jnp.concatenate([buf[i, zh, start : start + size, :] for i in order], axis=0)
+
+
+def narrow_tile(buf, order, zh, start, size):
+    parts = [buf[i, zh, start : start + size, :].astype(F32) for i in order]
+    return jnp.concatenate(parts, axis=0).astype(BF)
+
+
+def lanes(side, width):
+    return pl.ds(pl.multiple_of(side * width, width), width)
+
+
 def forward_body(
-    zh_n, rs, ro, ahead, normed, behind, states, count, own, other,
-    wqkv_out, wout_out, whead_out, q_out, kv_out, probs_out, mixed, out, fore, alone,
-    qkv, probs, added_out, sq, so, sh, sems,
+    ny, nx, rs, ro, ahead, normed, behind, states, count, own, other,
+    own_out, other_out, q_out, kv_out, probs_out, whead, mixed, out, fore, alone,
+    qkv, probs, added_out, sems,
 ):
     core = lax.axis_index("core")
-    pn = own.shape[0]
+    pn, zh_n = own.shape[:2]
     qrows = 6 * rs
     orows = 4 * ro
     hr = rs // 2
-
-    def pieces(buf, c):
-        for zh in range(zh_n):
-            at = pl.ds(zh * pn, pn)
-            for t in range(6):
-                yield (
-                    buf.at[:, zh, pl.ds(t * rs, rs), :],
-                    wqkv_out.at[at, :, pl.ds((6 * c + t) * LANE, LANE)],
-                    sq.at[c, zh, t],
-                )
-            for t in range(4):
-                yield (
-                    buf.at[:, zh, pl.ds(qrows + t * ro, ro), :],
-                    wout_out.at[at, :, pl.ds((4 * c + t) * LANE, LANE)],
-                    so.at[c, zh, t],
-                )
-            yield (
-                buf.at[:, zh, pl.ds(qrows + orows, hr), :],
-                whead_out.at[at, c],
-                sh.at[c, zh],
-            )
-
-    def begin(*halves_of):
-        for c in range(2):
-            for src, dst, sem in pieces(halves_of[c], c):
-                pltpu.make_async_copy(src, dst, sem).start()
-
-    @pl.when(core == 0)
-    def _():
-        begin(own, other)
-
-    @pl.when(core != 0)
-    def _():
-        begin(other, own)
+    raw = [
+        pltpu.make_async_copy(own, own_out, sems.at[3]),
+        pltpu.make_async_copy(other, other_out, sems.at[4]),
+    ]
+    for copy in raw:
+        copy.start()
+    sides = [
+        (own, core, places(core, ny, nx)),
+        (other, 1 - core, places(1 - core, ny, nx)),
+    ]
 
     rows = jnp.concatenate([ahead[...], normed[...], behind[...]], axis=0)
     width = 6 * LANE
-    for buf, side in ((own, core), (other, 1 - core)):
+    for buf, side, order in sides:
         total = jnp.zeros((EXT, width), F32)
         for zh in range(zh_n):
-            tiles = [
-                buf[:, zh, t * rs : (t + 1) * rs, :].reshape(pn * rs, LANE)
-                for t in range(6)
-            ]
+            tiles = [tile_at(buf, order, zh, t * rs, rs) for t in range(6)]
             depth = pn * rs
             total = total + nn(
                 rows[:, zh * depth : (zh + 1) * depth], jnp.concatenate(tiles, axis=1)
             )
-        qkv[:, pl.ds(pl.multiple_of(side * width, width), width)] = total.astype(BF)
+        qkv[:, lanes(side, width)] = total.astype(BF)
     leaving = fetched(
         (
             (qkv.at[HALO : HALO + PTS, 0:HD], q_out),
@@ -227,45 +221,33 @@
     leaving[2].start()
     width = 4 * LANE
     attended = mixed[...]
-    for buf, side in ((own, core), (other, 1 - core)):
+    for buf, side, order in sides:
         total = jnp.zeros((PTS, width), F32)
         depth = pn * ro
         for zh in range(zh_n):
-            tiles = [
-                buf[:, zh, qrows + t * ro : qrows + (t + 1) * ro, :]
-                .astype(F32)
-                .reshape(depth, LANE)
-                .astype(BF)
-                for t in range(4)
-            ]
+            tiles = [narrow_tile(buf, order, zh, qrows + t * ro, ro) for t in range(4)]
             total = total + nn(
                 attended[:, zh * depth : (zh + 1) * depth],
                 jnp.concatenate(tiles, axis=1),
             )
-        added_out[:, pl.ds(pl.multiple_of(side * width, width), width)] = total
+        added_out[:, lanes(side, width)] = total
     layer = (states[...].astype(F32) + added_out[...]).astype(BF)
     out[...] = layer
-    blocks = [
-        [
-            buf[:, zh, qrows + orows : qrows + orows + hr, :].astype(F32)
-            for buf in (own, other)
-        ]
-        for zh in range(zh_n)
-    ]
-    mine_first = jnp.full((1, 1, 1), core, jnp.int32) == 0
-    ordered = [
-        jnp.stack([jnp.where(mine_first, a, b), jnp.where(mine_first, b, a)], axis=1)
-        for a, b in blocks
-    ]
-    flat_head = jnp.concatenate(ordered, axis=0).reshape(D, NVAR).astype(BF)
+    at_head = qrows + orows
+    first_is_own = jnp.full((hr, NVAR), core, jnp.int32) == 0
+    pieces = []
+    for zh in range(zh_n):
+        for i, j in zip(sides[0][2], sides[1][2]):
+            a = own[i, zh, at_head : at_head + hr, :].astype(F32)
+            b = other[j, zh, at_head : at_head + hr, :].astype(F32)
+            pieces += [jnp.where(first_is_own, a, b), jnp.where(first_is_own, b, a)]
+    flat_head = jnp.concatenate(pieces, axis=0).astype(BF)
+    whead[...] = flat_head
     mine = nn(layer, flat_head)
     alone[...] = mine
     for i in range(fore.shape[0]):
         fore[i] = mine.astype(BF)
-    for c in range(2):
-        for src, dst, sem in pieces(own, c):
-            pltpu.make_async_copy(src, dst, sem).wait()
-    for copy in leaving:
+    for copy in raw + leaving:
         copy.wait()
 
 
@@ -273,7 +255,7 @@
     return z * lax.rsqrt(z * z + smooth * smooth)
 
 
-def score_body(members, zh_n, every, alone, observed, mixed, out, gf, held, wg):
+def score_body(members, zh_n, every, alone, observed, mixed, out, gf, wg):
     mine = alone[...]
     sent = mine.astype(BF).astype(F32)
     total = jnp.zeros_like(mine)
@@ -281,7 +263,6 @@
         total = total + slope(sent - every[m].astype(F32))
     grad = (slope(mine - observed[...]) - total * (1.0 / (members - 1))).astype(BF)
     gf[...] = grad
-    held[...] = grad
     pn = wg.shape[0]
     heads = tn(out[...], grad)
     factor = tn(mixed[...], grad)
@@ -296,13 +277,19 @@
 
 
 def backward_body(
-    gf, whead_in, wout_in, q_in, kv_in, probs_in, gq, mid, lower, upper,
-    whead, wout, q, kv, probs, sems,
+    ny, nx, at_out, ro, gf_in, whead_in, own_in, other_in, q_in, kv_in, probs_in,
+    gq, mid, lower, upper,
+    gf, whead, own, other, q, kv, probs, go, sems,
 ):
+    zh_n = own.shape[1]
+    core = lax.axis_index("core")
+    size = own.shape[2]
     copies = fetched(
         (
+            (gf_in, gf),
             (whead_in, whead),
-            (wout_in, wout),
+            (own_in.at[:, :, pl.ds(at_out, size), :], own),
+            (other_in.at[:, :, pl.ds(at_out, size), :], other),
             (kv_in, kv),
             (probs_in, probs),
             (q_in, q),
@@ -312,12 +299,19 @@
     for copy in copies:
         copy.start()
     copies[0].wait()
-    flat_head = whead[...].astype(F32).reshape(D, NVAR).astype(BF)
-    go = nt(gf[...], flat_head).astype(BF)
     copies[1].wait()
-    flat_out = wout[...].astype(F32).reshape(HD, D).astype(BF)
-    gm = nt(go, flat_out).astype(BF)
-    for copy in copies[2:]:
+    go[...] = nt(gf[...], whead[...]).astype(BF)
+    copies[2].wait()
+    copies[3].wait()
+    columns = [0.0] * zh_n
+    for buf, side in ((own, core), (other, 1 - core)):
+        order = places(side, ny, nx)
+        given = go[:, lanes(side, 4 * LANE)]
+        for zh in range(zh_n):
+            tiles = [narrow_tile(buf, order, zh, t * ro, ro) for t in range(4)]
+            columns[zh] = columns[zh] + nt(given, jnp.concatenate(tiles, axis=1))
+    gm = jnp.concatenate(columns, axis=1).astype(BF)
+    for copy in copies[4:]:
         copy.wait()
     for pair in range(HEADS // 2):
         at = pl.ds(pair * LANE, LANE)
@@ -344,22 +338,39 @@
             upper[:, where_at] = total[HALO + PTS :].astype(BF)
 
 
-def final_body(states, scale, gf, whead, wqkv, gq, mid, first, last, total, grad):
+def final_body(
+    ny, nx, rs, states, scale, gf, whead, own, other_in, gq, mid, first, last,
+    total, grad, given, other, sems,
+):
+    (arriving,) = fetched(
+        ((other_in.at[:, :, pl.ds(0, other.shape[2]), :], other),), sems
+    )
+    arriving.start()
+    zh_n = own.shape[1]
+    core = lax.axis_index("core")
     centred, inverse = normalised(states[...])
-    flat_head = whead[...].astype(F32).reshape(D, NVAR).astype(BF)
     total[...] = mid[...]
     total[:HALO, :] += first[...].astype(F32)
     total[PTS - HALO :, :] += last[...].astype(F32)
-    kvs = total[...].astype(BF)
-    weights = wqkv[...].reshape(D, 3 * HD)
-    gn = nt(gq[...], weights[:, :HD]) + nt(kvs, weights[:, HD:])
+    given[:, :HD] = gq[...]
+    given[:, HD:] = total[...].astype(BF)
+    columns = [0.0] * zh_n
+    for buf, side in ((own, core), (other, 1 - core)):
+        if buf is other:
+            arriving.wait()
+        order = places(side, ny, nx)
+        part = given[:, lanes(side, 6 * LANE)]
+        for zh in range(zh_n):
+            tiles = [tile_at(buf, order, zh, t * rs, rs) for t in range(6)]
+            columns[zh] = columns[zh] + nt(part, jnp.concatenate(tiles, axis=1))
+    gn = jnp.concatenate(columns, axis=1)
     g = gn * scale[...]
     back = inverse * (
         g
         - jnp.mean(g, axis=-1, keepdims=True)
         - centred * jnp.mean(g * centred, axis=-1, keepdims=True)
     )
-    grad[...] = (nt(gf[...], flat_head) + back).astype(BF)
+    grad[...] = (nt(gf[...], whead[...]) + back).astype(BF)
 
 
 def added(parts):
@@ -380,7 +391,7 @@
 
 
 def weights_body(scaling, parts, whead, mixing, head):
-    flat_head = whead[...].astype(F32).reshape(D, NVAR).astype(BF)
+    flat_head = whead[...]
     rb = head.shape[0]
     total = added(parts) * scaling
     head[...] = total[:rb]
@@ -434,63 +445,78 @@
         cost=(4e6, 1e6),
         limit=8,
     )
-    spread = jnp.broadcast_to(column[None], (pn, *column.shape))
-    own = lax.all_to_all(spread, PLANE, 0, 0, tiled=True)
+    ny, nx = lax.axis_size("y"), lax.axis_size("x")
+    along_x = [[y * nx + x for x in range(nx)] for y in range(ny)]
+    along_y = [[y * nx + x for y in range(ny)] for x in range(nx)]
+
+    def widened(block, first, second):
+        groups = first + [[pn + i for i in group] for group in second]
+        n = len(first[0])
+        return lax.all_to_all(
+            jnp.broadcast_to(block[None], (n, *block.shape)),
+            ("core", "y", "x"),
+            0,
+            0,
+            axis_index_groups=groups,
+            tiled=True,
+        )
+
+    line = widened(column, along_x, along_y)
+    own = widened(line, along_y, along_x).reshape(pn, *column.shape)
     other = lax.ppermute(own, "core", swap)
-    wqkv, wout, whead, q, kv, probs, mixed, out, fore, alone = call(
-        functools.partial(forward_body, zh_n, rs, ro),
+    own_hbm, other_hbm, q, kv, probs, whead, mixed, out, fore, alone = call(
+        functools.partial(forward_body, ny, nx, rs, ro),
         [
-            ((devices, rs, 3 * HD), BF),
-            ((devices, ro, D), BF),
-            ((devices, 2, rs // 2, NVAR), BF),
+            (own.shape, BF),
+            (own.shape, BF),
             ((PTS, HD), BF),
             ((EXT, D), BF),
             ((HEADS, PTS, EXT), BF),
+            ((D, NVAR), BF),
             ((PTS, HD), BF),
             ((PTS, D), BF),
             ((members, PTS, NVAR), BF),
             ((PTS, NVAR), F32),
         ],
         (ahead, normed, behind, inputs, count, own, other),
-        "VAVAAVV>HHHHHHVVVV",
+        "VAVAAVV>HHHHHAVVVV",
         scratch=(
             pltpu.VMEM((EXT, 3 * HD), BF),
             pltpu.VMEM((HEADS, PTS, EXT), BF),
             pltpu.VMEM((PTS, D), F32),
-            pltpu.SemaphoreType.DMA((2, zh_n, 6)),
-            pltpu.SemaphoreType.DMA((2, zh_n, 4)),
-            pltpu.SemaphoreType.DMA((2, zh_n)),
-            pltpu.SemaphoreType.DMA((3,)),
+            pltpu.SemaphoreType.DMA((5,)),
         ),
         cost=(2e9, 1e7),
         limit=24,
     )
     every = lax.all_to_all(fore, MEMBER, 0, 0, tiled=True)
-    gf, held, wg = call(
+    gf, wg = call(
         functools.partial(score_body, members, zh_n),
         [
-            ((PTS, NVAR), BF),
             ((PTS, NVAR), BF),
             ((pn, zh_n, (D + HD) // devices, NVAR), BF),
         ],
         (every, alone, observed, mixed, out),
-        "VVVVV>VAA",
+        "VVVVV>AA",
         cost=(1e8, 2e6),
         limit=8,
     )
     plane = lax.all_to_all(wg, PLANE, 0, 0, tiled=True)
     gq, mid, lower, upper = call(
-        backward_body,
+        functools.partial(backward_body, ny, nx, 6 * rs, ro),
         [((PTS, HD), BF), ((PTS, D), F32), ((HALO, D), BF), ((HALO, D), BF)],
-        (gf, whead, wout, q, kv, probs),
-        "VHHHHH>AAAA",
+        (gf, whead, own_hbm, other_hbm, q, kv, probs),
+        "HHHHHHH>AAAA",
         scratch=(
+            pltpu.VMEM(gf.shape, BF),
             pltpu.VMEM(whead.shape, BF),
-            pltpu.VMEM(wout.shape, BF),
+            pltpu.VMEM((pn, zh_n, 4 * ro, LANE), BF),
+            pltpu.VMEM((pn, zh_n, 4 * ro, LANE), BF),
             pltpu.VMEM(q.shape, BF),
             pltpu.VMEM(kv.shape, BF),
             pltpu.VMEM(probs.shape, BF),
-            pltpu.SemaphoreType.DMA((5,)),
+            pltpu.VMEM((PTS, D), BF),
+            pltpu.SemaphoreType.DMA((7,)),
         ),
         cost=(1e9, 4e6),
         limit=16,
@@ -516,10 +542,15 @@
     )
     parts = lax.all_to_all(spread, MEMBER, 0, 0, tiled=True)
     total, grad_input = call(
-        final_body,
+        functools.partial(final_body, ny, nx, rs),
         [((PTS, D), F32), ((PTS, D), BF)],
-        (inputs, scale, held, whead, wqkv, gq, mid, first, last),
-        "AAAAVAAVV>AA",
+        (inputs, scale, gf, whead, own_hbm, other_hbm, gq, mid, first, last),
+        "AAAAVHAAVV>AA",
+        scratch=(
+            pltpu.VMEM((PTS, 3 * HD), BF),
+            pltpu.VMEM((pn, zh_n, 6 * rs, LANE), BF),
+            pltpu.SemaphoreType.DMA((1,)),
+        ),
         cost=(1e9, 4e6),
         limit=16,
     )

time: 184 us -> 186 us (1.011)
  Pallas kernels: 25.9 us -> 28.5 us
  waiting for transfers between devices: 16.2 us -> 18.8 us
  blocking collectives: 111 us -> 109 us
    pallas_call x10, Pallas kernels: 25.9 us -> 28.5 us  [call(): pl.pallas_call(body, out_shape=tuple(shapes), in_specs=[SPECS[at] for at...]
    ppermute x1, waiting for transfers between devices: 0.01 us -> 2.01 us  [shards(): after = lax.ppermute(inputs[:HALO], GRID, down)]
    all_to_all x1 -> x2, blocking collectives: 30.7 us -> 30.5 us  [widened(): lax.all_to_all(jnp.broadcast_to(block[None], (n, *block.shape)), ('core',...]
  transfers between devices with their start and end apart: 6 -> 6, of which waited for: 2 -> 3; matrix products, arithmetic and copies ran while one was open for 0% -> 0% of each run, Pallas kernels for 6% -> 7%
where the time goes in v5:
time: 186 us; the launch traced here: 185 us
  blocking collectives  109 us (59%)
  Pallas kernels  28.5 us (15%)
  starting transfers between devices  27.2 us (15%)
  waiting for transfers between devices  18.8 us (10%)
    all_to_all x2, blocking collectives, widened(): lax.all_to_all(jnp.broadcast_to(block[None], (n, *block.shape)), ('core',...  30.5 us
    all_to_all x1, blocking collectives, shards(): column = lax.all_to_all(column, 'zh', 0, 0, tiled=True)  30.1 us
    pallas_call x10, Pallas kernels, call(): pl.pallas_call(body, out_shape=tuple(shapes), in_specs=[SPECS[at] for at...  28.5 us
    all_to_all x1, blocking collectives, shards(): column = lax.all_to_all(partial, 'zh', 0, 0, tiled=True)  22.1 us
    ppermute x1, waiting for transfers between devices, shards(): last = lax.ppermute(lower, GRID, down)  16.5 us
    all_to_all x1, blocking collectives, shards(): every = lax.all_to_all(fore, MEMBER, 0, 0, tiled=True)  13.9 us
    all_to_all x1, blocking collectives, shards(): plane = lax.all_to_all(wg, PLANE, 0, 0, tiled=True)  12.3 us
    ppermute x1, starting transfers between devices, shards(): before = lax.ppermute(inputs[PTS - HALO:], GRID, up)  11.6 us
  transfers between devices with their start and end apart: 6, of which 3 were waited for; matrix products, arithmetic and copies ran while one was open for 0% of the time, Pallas kernels for 7%

profile of v5, /device:TPU:30, one launch (start us, length us, event | category | flops | bytes accessed | tf_op | source)
XLA Modules:
  0.0 185.4 jit_solution(9787652209463373622)
XLA Ops:
  0.6 2.1 %shard_map.122 = (bf16[4,136,128]{2,1,0:T(8,128)(2,1)}, bf16[136,128]{1,0:T(8,128)(2,1)}) custom-call(bf16[16,512]{1,0:T(8,128)(2,1)} %query.1, bf16[16,512]{1,0:T(8,128)(2,1)} %key.1, bf16[16,512]{1,0:T(8,128)(2,1)} %value.1, bf16[8,1024]{1,0:T(8,128)(2,1)} %out.1, bf16[16,128]{1,0:T(8,128)(2,1)} %head.1), custom_call_target="tpu_custom_call" | custom-call | flops 1000000 | bytes 1000000 | tf_op jit(solution)/shard_map/pallas_call | solution.py:63
  2.7 30.1 %all_to_all.35 = bf16[4,136,128]{2,1,0:T(8,128)(2,1)S(1)} all-to-all(bf16[4,136,128]{2,1,0:T(8,128)(2,1)} %get-tuple-element.33), channel_id=1, replica_groups=mesh['zl'=4,'core'=2,'zh'=4,'y'=4,'x'=4] {'zh'}, dimensions={0} | all-to-all | bytes 278528 | tf_op jit(solution)/shard_map/all_to_all | solution.py:427
  32.9 10.8 %all_to_all.36 = bf16[4,4,136,128]{3,2,1,0:T(8,128)(2,1)S(1)} all-to-all(bf16[4,4,136,128]{3,2,1,0:T(8,128)(2,1)S(1)} %broadcast_in_dim.8), channel_id=1, replica_groups={{0,1,2,3},{4,5,6,7},{8,9,10,11},{12,13,14,15},{64,68,72,76},{65,69,73,7..., dimensions={0} | all-to-all | bytes 1114112 | tf_op jit(solution)/shard_map/all_to_all | solution.py:455
  44.0 19.8 %all_to_all.37 = bf16[4,4,4,136,128]{4,3,2,1,0:T(8,128)(2,1)S(1)} all-to-all(bf16[4,4,4,136,128]{4,3,2,1,0:T(8,128)(2,1)S(1)} %broadcast_in_dim.9), channel_id=1, replica_groups={{0,4,8,12},{1,5,9,13},{2,6,10,14},{3,7,11,15},{64,65,66,67},{68,69,70,7..., dimensions={0} | all-to-all | bytes 4456448 | tf_op jit(solution)/shard_map/all_to_all | solution.py:455
  63.8 1.9 %collective-permute-start.2 = (bf16[16,4,136,128]{3,2,1,0:T(8,128)(2,1)S(1)}, bf16[16,4,136,128]{3,2,1,0:T(8,128)(2,1)}, u32[]{:S(2)}, u32[]{:S(2)}) collective-permute-start(bf16[16,4,136,128]{3,2,1,0:T(8,128)(2,1)S(1)} %bitcast.9), channel_id=1, source_target_pairs={{0,64},{64,0},{1,65},{65,1},{2,66},{66,2},{3,67},{67,3},{4,68},{68... | collective-permute-start | bytes 6684680 | tf_op jit(solution)/shard_map/ppermute | solution.py:466
  65.7 2.4 %collective-permute-start.1 = (bf16[32,1024]{1,0:T(8,128)(2,1)S(1)}, bf16[32,1024]{1,0:T(8,128)(2,1)S(1)}, u32[]{:S(2)}, u32[]{:S(2)}) collective-permute-start(bf16[32,1024]{1,0:T(8,128)(2,1)S(1)} %get-tuple-element.54), channel_id=1, source_target_pairs={{1,0},{2,1},{3,2},{4,3},{5,4},{6,5},{7,6},{8,7},{9,8},{10,9},{11,1... | collective-permute-start | bytes 196616 | tf_op jit(solution)/shard_map/ppermute | solution.py:429
  68.1 11.6 %collective-permute-start = (bf16[32,1024]{1,0:T(8,128)(2,1)S(1)}, bf16[32,1024]{1,0:T(8,128)(2,1)S(1)}, u32[]{:S(2)}, u32[]{:S(2)}) collective-permute-start(bf16[32,1024]{1,0:T(8,128)(2,1)S(1)} %get-tuple-element.55), channel_id=1, source_target_pairs={{0,1},{1,2},{2,3},{3,4},{4,5},{5,6},{6,7},{7,8},{8,9},{9,10},{10,1... | collective-permute-start | bytes 196616 | tf_op jit(solution)/shard_map/ppermute | solution.py:428
  79.8 0.6 broadcast_subtract_fusion.rel
  80.4 2.0 %shard_map.121 = (bf16[128,1024]{1,0:T(8,128)(2,1)}, f32[128,192]{1,0:T(8,128)}) custom-call(bf16[128,1024]{1,0:T(8,128)(2,1)} %bitcast.11, f32[1,1024]{1,0:T(1,128)} %bitcast.14, s32[128,8]{1,0:T(8,128)} %broadcast_subtract_fusion.rel), custom_call_target="tpu_custom_call" | custom-call | flops 4000000 | bytes 1000000 | tf_op jit(solution)/shard_map/pallas_call | solution.py:63
  82.4 2.0 %collective-permute-done.1.after = bf16[32,1024]{1,0:T(8,128)(2,1)S(1)} collective-permute-done((bf16[32,1024]{1,0:T(8,128)(2,1)S(1)}, bf16[32,1024]{1,0:T(8,128)(2,1)S(1)}, u32[]{:S(2)}, u32[]{:S(2)}) %collective-permute-start.1) | collective-permute-done | bytes 65568 | tf_op jit(solution)/shard_map/ppermute | solution.py:429
  84.4 0.9 shard_map.120
  85.4 8.9 %shard_map.123 = (bf16[16,4,136,128]{3,2,1,0:T(8,128)(2,1)}, bf16[16,4,136,128]{3,2,1,0:T(8,128)(2,1)}, bf16[128,512]{1,0:T(8,128)(2,1)}, bf16[192,1024]{1,0:T(8...) custom-call(bf16[32,1024]{1,0:T(8,128)(2,1)S(1)} %get-tuple-element., ...), custom_call_target="tpu_custom_call" | custom-call | flops 2000000000 | bytes 10000000 | tf_op jit(solution)/shard_map/pallas_call | solution.py:63
  94.2 13.9 %all_to_all.38.every = bf16[8,128,128]{2,1,0:T(8,128)(2,1)S(1)} all-to-all(bf16[8,128,128]{2,1,0:T(8,128)(2,1)S(1)} %get-tuple-element.34), channel_id=1, replica_groups=mesh['zl'=4,'core'=2,'zh'=4,'y'=4,'x'=4] {'zl','core'}, dimensions={0} | all-to-all | bytes 524288 | tf_op jit(solution)/shard_map/all_to_all | solution.py:492
  108.2 1.2 shard_map.124
  109.3 12.3 %all_to_all.39.parts = bf16[16,4,24,128]{3,2,1,0:T(8,128)(2,1)S(1)} all-to-all(bf16[16,4,24,128]{3,2,1,0:T(8,128)(2,1)} %get-tuple-element.50), channel_id=1, replica_groups=mesh['zl'=4,'core'=2,'zh'=4,'y'=4,'x'=4] {'y','x'}, dimensions={0} | all-to-all | bytes 786432 | tf_op jit(solution)/shard_map/all_to_all | solution.py:504
  121.6 0.7 shard_map.127
  122.3 22.1 %all_to_all.40.parts = bf16[4,24,128]{2,1,0:T(8,128)(2,1)S(1)} all-to-all(bf16[4,24,128]{2,1,0:T(8,128)(2,1)} %shard_map.127), channel_id=1, replica_groups=mesh['zl'=4,'core'=2,'zh'=4,'y'=4,'x'=4] {'zh'}, dimensions={0} | all-to-all | bytes 49152 | tf_op jit(solution)/shard_map/all_to_all | solution.py:534
  145.0 3.3 %all-to-all-start.6 = ((bf16[8,24,128]{2,1,0:T(8,128)(2,1)}), bf16[8,24,128]{2,1,0:T(8,128)(2,1)S(1)}, u32[]{:S(2)}, u32[]{:S(2)}) async-start(bf16[8,24,128]{2,1,0:T(8,128)(2,1)} %shard_map.128), calls=%async_computation.6 | async-start | bytes 98304 | tf_op jit(solution)/shard_map/all_to_all | solution.py:543
  148.3 5.6 %shard_map.125 = (bf16[128,512]{1,0:T(8,128)(2,1)}, f32[128,1024]{1,0:T(8,128)}, bf16[32,1024]{1,0:T(8,128)(2,1)}, bf16[32,1024]{1,0:T(8,128)(2,1)}) custom-call(bf16[128,128]{1,0:T(8,128)(2,1)} %get-tuple-element.38.gf_in.gf, bf16[1024,128]{1,0:T(8,128)(2,1)} %get-tuple-element.39.whead_in.whead, bf16[16,4,136,128]{3,2,1,0:T(8,128)(2,1)} %get-tuple-element.40.own_in.own, ...), custom_call_target="tpu_custom_call" | custom-call | flops 1000000000 | bytes 4000000 | tf_op jit(solution)/shard_map/pallas_call | solution.py:63
  153.9 6.1 %collective-permute-start.3 = (bf16[32,1024]{1,0:T(8,128)(2,1)}, bf16[32,1024]{1,0:T(8,128)(2,1)S(1)}, u32[]{:S(2)}, u32[]{:S(2)}) collective-permute-start(bf16[32,1024]{1,0:T(8,128)(2,1)} %get-tuple-element.47), channel_id=1, source_target_pairs={{0,1},{1,2},{2,3},{3,4},{4,5},{5,6},{6,7},{7,8},{8,9},{9,10},{10,1... | collective-permute-start | bytes 196616 | tf_op jit(solution)/shard_map/ppermute | solution.py:525
  160.0 1.9 %collective-permute-start.4 = (bf16[32,1024]{1,0:T(8,128)(2,1)}, bf16[32,1024]{1,0:T(8,128)(2,1)S(1)}, u32[]{:S(2)}, u32[]{:S(2)}) collective-permute-start(bf16[32,1024]{1,0:T(8,128)(2,1)} %get-tuple-element.48), channel_id=1, source_target_pairs={{1,0},{2,1},{3,2},{4,3},{5,4},{6,5},{7,6},{8,7},{9,8},{10,9},{11,1... | collective-permute-start | bytes 196616 | tf_op jit(solution)/shard_map/ppermute | solution.py:524
  162.2 16.5 %collective-permute-done.4.last = bf16[32,1024]{1,0:T(8,128)(2,1)S(1)} collective-permute-done((bf16[32,1024]{1,0:T(8,128)(2,1)}, bf16[32,1024]{1,0:T(8,128)(2,1)S(1)}, u32[]{:S(2)}, u32[]{:S(2)}) %collective-permute-start.4) | collective-permute-done | bytes 65568 | tf_op jit(solution)/shard_map/ppermute | solution.py:524
  178.7 4.9 %shard_map.126 = (f32[128,1024]{1,0:T(8,128)}, bf16[128,1024]{1,0:T(8,128)(2,1)}) custom-call(bf16[128,1024]{1,0:T(8,128)(2,1)} %bitcast.13, f32[1,1024]{1,0:T(1,128)} %bitcast.16, bf16[128,128]{1,0:T(8,128)(2,1)} %get-tuple-element.38.gf_in.gf, bf16[1024,128]{1,0:T(8,128)(2,1)} %get-tuple-element.39.whead_in.whead, bf16[16,4,136,128]{3,2,1,0:T(8,128)(2,1)S(1)} %copy-done, ...), custom_call_target="tpu_custom_call" | custom-call | flops 1000000000 | bytes 4000000 | tf_op jit(solution)/shard_map/pallas_call | solution.py:63
  183.6 1.8 shard_map.129
  (17 shorter events, 1.4 us)
Async XLA Ops:
  44.0 21.7 %copy-start.2 = (bf16[1,128,1024]{2,1,0:T(8,128)(2,1)S(1)}, bf16[1,128,1024]{2,1,0:T(8,128)(2,1)}, u32[]{:S(2)}) copy-start(bf16[1,128,1024]{2,1,0:T(8,128)(2,1)} %param.9) | copy-start | bytes 786436
  44.0 35.7 %copy-start.3 = (s32[128,8]{0,1:T(8,128)S(1)}, s32[128,8]{0,1:T(8,128)}, u32[]{:S(2)}) copy-start(s32[128,8]{0,1:T(8,128)} %param.16) | copy-start | bytes 12292
  63.8 21.6 %collective-permute-start.2 = (bf16[16,4,136,128]{3,2,1,0:T(8,128)(2,1)S(1)}, bf16[16,4,136,128]{3,2,1,0:T(8,128)(2,1)}, u32[]{:S(2)}, u32[]{:S(2)}) collective-permute-start(bf16[16,4,136,128]{3,2,1,0:T(8,128)(2,1)S(1)} %bitcast.9), channel_id=1, source_target_pairs={{0,64},{64,0},{1,65},{65,1},{2,66},{66,2},{3,67},{67,3},{4,68},{68... | collective-permute-start | bytes 6684680 | tf_op jit(solution)/shard_map/ppermute | solution.py:466
  65.7 18.7 %collective-permute-start.1 = (bf16[32,1024]{1,0:T(8,128)(2,1)S(1)}, bf16[32,1024]{1,0:T(8,128)(2,1)S(1)}, u32[]{:S(2)}, u32[]{:S(2)}) collective-permute-start(bf16[32,1024]{1,0:T(8,128)(2,1)S(1)} %get-tuple-element.54), channel_id=1, source_target_pairs={{1,0},{2,1},{3,2},{4,3},{5,4},{6,5},{7,6},{8,7},{9,8},{10,9},{11,1... | collective-permute-start | bytes 196616 | tf_op jit(solution)/shard_map/ppermute | solution.py:429
  68.1 16.3 %collective-permute-start = (bf16[32,1024]{1,0:T(8,128)(2,1)S(1)}, bf16[32,1024]{1,0:T(8,128)(2,1)S(1)}, u32[]{:S(2)}, u32[]{:S(2)}) collective-permute-start(bf16[32,1024]{1,0:T(8,128)(2,1)S(1)} %get-tuple-element.55), channel_id=1, source_target_pairs={{0,1},{1,2},{2,3},{3,4},{4,5},{5,6},{6,7},{7,8},{8,9},{9,10},{10,1... | collective-permute-start | bytes 196616 | tf_op jit(solution)/shard_map/ppermute | solution.py:428
  85.3 22.8 %copy-start.1 = (f32[128,128]{1,0:T(8,128)S(1)}, f32[128,128]{1,0:T(8,128)}, u32[]{:S(2)}) copy-start(f32[128,128]{1,0:T(8,128)} %observed.1) | copy-start | bytes 196612
  145.0 38.6 %all-to-all-start.6 = ((bf16[8,24,128]{2,1,0:T(8,128)(2,1)}), bf16[8,24,128]{2,1,0:T(8,128)(2,1)S(1)}, u32[]{:S(2)}, u32[]{:S(2)}) async-start(bf16[8,24,128]{2,1,0:T(8,128)(2,1)} %shard_map.128), calls=%async_computation.6 | async-start | bytes 98304 | tf_op jit(solution)/shard_map/all_to_all | solution.py:543
  148.3 30.4 %copy-start = (bf16[16,4,136,128]{3,2,1,0:T(8,128)(2,1)S(1)}, bf16[16,4,136,128]{3,2,1,0:T(8,128)(2,1)}, u32[]{:S(2)}) copy-start(bf16[16,4,136,128]{3,2,1,0:T(8,128)(2,1)} %get-tuple-element.40.own_in.own) | copy-start | bytes 6684676
  153.9 8.3 %collective-permute-start.3 = (bf16[32,1024]{1,0:T(8,128)(2,1)}, bf16[32,1024]{1,0:T(8,128)(2,1)S(1)}, u32[]{:S(2)}, u32[]{:S(2)}) collective-permute-start(bf16[32,1024]{1,0:T(8,128)(2,1)} %get-tuple-element.47), channel_id=1, source_target_pairs={{0,1},{1,2},{2,3},{3,4},{4,5},{5,6},{6,7},{7,8},{8,9},{9,10},{10,1... | collective-permute-start | bytes 196616 | tf_op jit(solution)/shard_map/ppermute | solution.py:525
  160.0 18.7 %collective-permute-start.4 = (bf16[32,1024]{1,0:T(8,128)(2,1)}, bf16[32,1024]{1,0:T(8,128)(2,1)S(1)}, u32[]{:S(2)}, u32[]{:S(2)}) collective-permute-start(bf16[32,1024]{1,0:T(8,128)(2,1)} %get-tuple-element.48), channel_id=1, source_target_pairs={{1,0},{2,1},{3,2},{4,3},{5,4},{6,5},{7,6},{8,7},{9,8},{10,9},{11,1... | collective-permute-start | bytes 196616 | tf_op jit(solution)/shard_map/ppermute | solution.py:524

commit v6 on v5

--- a/solution.py
+++ b/solution.py
@@ -90,12 +90,6 @@
     count[...] = total
 
 
-def prepare_body(before, after, scale, first, last):
-    for part, normed in ((before, first), (after, last)):
-        centred, _ = normalised(part[...])
-        normed[...] = (centred * scale[...]).astype(BF)
-
-
 def halves(tile_shape, head):
     lane = lax.broadcasted_iota(jnp.int32, tile_shape, 1)
     return (lane < HDIM) if head == 0 else (lane >= HDIM)
@@ -105,20 +99,13 @@
     return [pltpu.make_async_copy(s, d, sems.at[i]) for i, (s, d) in enumerate(pairs)]
 
 
-def send_out(pairs, sems):
-    copies = fetched(pairs, sems)
-    for copy in copies:
-        copy.start()
-    for copy in copies:
-        copy.wait()
-
-
-def pack_body(query, key, value, out, head, column, mine, sems):
+def pack_body(query, key, value, out, head, column):
     rs, ro = query.shape[0], out.shape[0]
 
     def put(row, tile):
         size = tile.shape[0]
-        mine[row : row + size, :] = tile
+        for i in range(column.shape[0]):
+            column[i, row : row + size, :] = tile
 
     for c in range(2):
 
@@ -133,15 +120,16 @@
                 put(6 * rs + t * ro, out[:, lane : lane + LANE])
             put(6 * rs + 4 * ro, head[c * rs // 2 : (c + 1) * rs // 2, :])
 
-    send_out([(mine, column.at[i]) for i in range(column.shape[0])], sems)
-
 
 def places(side, ny, nx):
     return [
-        jnp.where(side == 0, y * nx + x, x * ny + y)
-        for y in range(ny)
-        for x in range(nx)
+        y * nx + x if side == 0 else x * ny + y for y in range(ny) for x in range(nx)
     ]
+
+
+def on_each_core(body):
+    for c in range(2):
+        pl.when(lax.axis_index("core") == c)(functools.partial(body, c))
 
 
 def tile_at(buf, order, zh, start, size):
@@ -153,42 +141,52 @@
     return jnp.concatenate(parts, axis=0).astype(BF)
 
 
-def lanes(side, width):
-    return pl.ds(pl.multiple_of(side * width, width), width)
+def projected(rows, buf, order, rs):
+    total = 0.0
+    depth = buf.shape[0] * rs
+    for zh in range(buf.shape[1]):
+        tiles = [tile_at(buf, order, zh, t * rs, rs) for t in range(6)]
+        total = total + nn(
+            rows[:, zh * depth : (zh + 1) * depth], jnp.concatenate(tiles, axis=1)
+        )
+    return total.astype(BF)
+
+
+def early_body(
+    ny, nx, rs, before, after, scale, normed, own, ahead, behind, part
+):
+    for block, to in ((before, ahead), (after, behind)):
+        centred, _ = normalised(block[...])
+        to[...] = (centred * scale[...]).astype(BF)
+    rows = jnp.concatenate([ahead[...], normed[...], behind[...]], axis=0)
+
+    def project(c):
+        part[...] = projected(rows, own, places(c, ny, nx), rs)
+
+    on_each_core(project)
 
 
 def forward_body(
-    ny, nx, rs, ro, ahead, normed, behind, states, count, own, other,
-    own_out, other_out, q_out, kv_out, probs_out, whead, mixed, out, fore, alone,
+    ny, nx, rs, ro, ahead, normed, behind, part, states, count, own, other,
+    raw, q_out, kv_out, probs_out, whead, mixed, out, fore, alone,
     qkv, probs, added_out, sems,
 ):
-    core = lax.axis_index("core")
     pn, zh_n = own.shape[:2]
     qrows = 6 * rs
     orows = 4 * ro
     hr = rs // 2
-    raw = [
-        pltpu.make_async_copy(own, own_out, sems.at[3]),
-        pltpu.make_async_copy(other, other_out, sems.at[4]),
-    ]
-    for copy in raw:
+    raws = fetched(((own, raw.at[0]), (other, raw.at[1])), sems.at[pl.ds(3, 2)])
+    for copy in raws:
         copy.start()
-    sides = [
-        (own, core, places(core, ny, nx)),
-        (other, 1 - core, places(1 - core, ny, nx)),
-    ]
-
     rows = jnp.concatenate([ahead[...], normed[...], behind[...]], axis=0)
     width = 6 * LANE
-    for buf, side, order in sides:
-        total = jnp.zeros((EXT, width), F32)
-        for zh in range(zh_n):
-            tiles = [tile_at(buf, order, zh, t * rs, rs) for t in range(6)]
-            depth = pn * rs
-            total = total + nn(
-                rows[:, zh * depth : (zh + 1) * depth], jnp.concatenate(tiles, axis=1)
-            )
-        qkv[:, lanes(side, width)] = total.astype(BF)
+
+    def project(c):
+        there = projected(rows, other, places(1 - c, ny, nx), rs)
+        qkv[:, c * width : (c + 1) * width] = part[...]
+        qkv[:, (1 - c) * width : (2 - c) * width] = there
+
+    on_each_core(project)
     leaving = fetched(
         (
             (qkv.at[HALO : HALO + PTS, 0:HD], q_out),
@@ -219,35 +217,42 @@
             got.append(nn(weight, v2))
         mixed[:, at] = jnp.where(halves((PTS, LANE), 0), got[0], got[1]).astype(BF)
     leaving[2].start()
-    width = 4 * LANE
     attended = mixed[...]
-    for buf, side, order in sides:
-        total = jnp.zeros((PTS, width), F32)
+    at_head = qrows + orows
+
+    def finish(c):
+        wide = 4 * LANE
         depth = pn * ro
+        orders = [places(0, ny, nx), places(1, ny, nx)]
+        bufs = (own, other) if c == 0 else (other, own)
+        for side in range(2):
+            total = 0.0
+            for zh in range(zh_n):
+                tiles = [
+                    narrow_tile(bufs[side], orders[side], zh, qrows + t * ro, ro)
+                    for t in range(4)
+                ]
+                total = total + nn(
+                    attended[:, zh * depth : (zh + 1) * depth],
+                    jnp.concatenate(tiles, axis=1),
+                )
+            added_out[:, side * wide : (side + 1) * wide] = total
+        pieces = []
         for zh in range(zh_n):
-            tiles = [narrow_tile(buf, order, zh, qrows + t * ro, ro) for t in range(4)]
-            total = total + nn(
-                attended[:, zh * depth : (zh + 1) * depth],
-                jnp.concatenate(tiles, axis=1),
-            )
-        added_out[:, lanes(side, width)] = total
+            for ij in zip(*orders):
+                for side in range(2):
+                    block = bufs[side][ij[side], zh, at_head : at_head + hr, :]
+                    pieces.append(block.astype(F32))
+        whead[...] = jnp.concatenate(pieces, axis=0).astype(BF)
+
+    on_each_core(finish)
     layer = (states[...].astype(F32) + added_out[...]).astype(BF)
     out[...] = layer
-    at_head = qrows + orows
-    first_is_own = jnp.full((hr, NVAR), core, jnp.int32) == 0
-    pieces = []
-    for zh in range(zh_n):
-        for i, j in zip(sides[0][2], sides[1][2]):
-            a = own[i, zh, at_head : at_head + hr, :].astype(F32)
-            b = other[j, zh, at_head : at_head + hr, :].astype(F32)
-            pieces += [jnp.where(first_is_own, a, b), jnp.where(first_is_own, b, a)]
-    flat_head = jnp.concatenate(pieces, axis=0).astype(BF)
-    whead[...] = flat_head
-    mine = nn(layer, flat_head)
+    mine = nn(layer, whead[...])
     alone[...] = mine
     for i in range(fore.shape[0]):
         fore[i] = mine.astype(BF)
-    for copy in raw + leaving:
+    for copy in raws + leaving:
         copy.wait()
 
 
@@ -277,19 +282,17 @@
 
 
 def backward_body(
-    ny, nx, at_out, ro, gf_in, whead_in, own_in, other_in, q_in, kv_in, probs_in,
+    ny, nx, at_out, ro, gf_in, whead_in, raw_in, q_in, kv_in, probs_in,
     gq, mid, lower, upper,
-    gf, whead, own, other, q, kv, probs, go, sems,
+    gf, whead, raw, q, kv, probs, gm_held, sems,
 ):
-    zh_n = own.shape[1]
-    core = lax.axis_index("core")
-    size = own.shape[2]
+    zh_n = raw.shape[2]
+    size = raw.shape[3]
     copies = fetched(
         (
             (gf_in, gf),
             (whead_in, whead),
-            (own_in.at[:, :, pl.ds(at_out, size), :], own),
-            (other_in.at[:, :, pl.ds(at_out, size), :], other),
+            (raw_in.at[:, :, :, pl.ds(at_out, size), :], raw),
             (kv_in, kv),
             (probs_in, probs),
             (q_in, q),
@@ -300,18 +303,25 @@
         copy.start()
     copies[0].wait()
     copies[1].wait()
-    go[...] = nt(gf[...], whead[...]).astype(BF)
+    go = nt(gf[...], whead[...]).astype(BF)
     copies[2].wait()
-    copies[3].wait()
-    columns = [0.0] * zh_n
-    for buf, side in ((own, core), (other, 1 - core)):
-        order = places(side, ny, nx)
-        given = go[:, lanes(side, 4 * LANE)]
-        for zh in range(zh_n):
-            tiles = [narrow_tile(buf, order, zh, t * ro, ro) for t in range(4)]
-            columns[zh] = columns[zh] + nt(given, jnp.concatenate(tiles, axis=1))
-    gm = jnp.concatenate(columns, axis=1).astype(BF)
-    for copy in copies[4:]:
+
+    def widen(c):
+        columns = [0.0] * zh_n
+        for side in range(2):
+            order = places(side, ny, nx)
+            given = go[:, side * 4 * LANE : (side + 1) * 4 * LANE]
+            for zh in range(zh_n):
+                tiles = [
+                    narrow_tile(raw.at[side ^ c], order, zh, t * ro, ro)
+                    for t in range(4)
+                ]
+                columns[zh] = columns[zh] + nt(given, jnp.concatenate(tiles, axis=1))
+        gm_held[...] = jnp.concatenate(columns, axis=1).astype(BF)
+
+    on_each_core(widen)
+    gm = gm_held[...]
+    for copy in copies[3:]:
         copy.wait()
     for pair in range(HEADS // 2):
         at = pl.ds(pair * LANE, LANE)
@@ -339,31 +349,42 @@
 
 
 def final_body(
-    ny, nx, rs, states, scale, gf, whead, own, other_in, gq, mid, first, last,
-    total, grad, given, other, sems,
+    ny, nx, rs, states, scale, gf, whead, raw_in, gq, mid, first, last,
+    total, grad, given, held, raw, sems,
 ):
-    (arriving,) = fetched(
-        ((other_in.at[:, :, pl.ds(0, other.shape[2]), :], other),), sems
-    )
-    arriving.start()
-    zh_n = own.shape[1]
-    core = lax.axis_index("core")
+    zh_n = raw.shape[2]
+    copies = fetched(
+        [
+            (raw_in.at[:, :, zh, pl.ds(0, raw.shape[3]), :], raw.at[:, :, zh])
+            for zh in range(zh_n)
+        ],
+        sems,
+    )
+    for copy in copies:
+        copy.start()
     centred, inverse = normalised(states[...])
     total[...] = mid[...]
     total[:HALO, :] += first[...].astype(F32)
     total[PTS - HALO :, :] += last[...].astype(F32)
     given[:, :HD] = gq[...]
     given[:, HD:] = total[...].astype(BF)
-    columns = [0.0] * zh_n
-    for buf, side in ((own, core), (other, 1 - core)):
-        if buf is other:
-            arriving.wait()
-        order = places(side, ny, nx)
-        part = given[:, lanes(side, 6 * LANE)]
+
+    def widen(c):
+        depth = raw.shape[1] * rs
         for zh in range(zh_n):
-            tiles = [tile_at(buf, order, zh, t * rs, rs) for t in range(6)]
-            columns[zh] = columns[zh] + nt(part, jnp.concatenate(tiles, axis=1))
-    gn = jnp.concatenate(columns, axis=1)
+            copies[zh].wait()
+            column = 0.0
+            for side in range(2):
+                order = places(side, ny, nx)
+                part = given[:, side * 6 * LANE : (side + 1) * 6 * LANE]
+                tiles = [
+                    tile_at(raw.at[side ^ c], order, zh, t * rs, rs) for t in range(6)
+                ]
+                column = column + nt(part, jnp.concatenate(tiles, axis=1))
+            held[:, zh * depth : (zh + 1) * depth] = column
+
+    on_each_core(widen)
+    gn = held[...]
     g = gn * scale[...]
     back = inverse * (
         g
@@ -415,12 +436,11 @@
     up = [(i, i + 1) for i in range(devices - 1)]
     down = [(j, i) for i, j in up]
 
-    column, _ = call(
+    (column,) = call(
         pack_body,
-        [((zh_n, packed, LANE), BF), ((packed, LANE), BF)],
+        [((zh_n, packed, LANE), BF)],
         (query, key, value, out_w, head_w),
-        "AAAAA>HV",
-        scratch=(pltpu.SemaphoreType.DMA((zh_n,)),),
+        "AAAAA>V",
         cost=(1e6, 1e6),
         limit=4,
     )
@@ -437,14 +457,6 @@
         cost=(4e6, 1e6),
         limit=8,
     )
-    ahead, behind = call(
-        prepare_body,
-        [((HALO, D), BF), ((HALO, D), BF)],
-        (before, after, scale),
-        "VVA>VV",
-        cost=(4e6, 1e6),
-        limit=8,
-    )
     ny, nx = lax.axis_size("y"), lax.axis_size("x")
     along_x = [[y * nx + x for x in range(nx)] for y in range(ny)]
     along_y = [[y * nx + x for y in range(ny)] for x in range(nx)]
@@ -464,11 +476,18 @@
     line = widened(column, along_x, along_y)
     own = widened(line, along_y, along_x).reshape(pn, *column.shape)
     other = lax.ppermute(own, "core", swap)
-    own_hbm, other_hbm, q, kv, probs, whead, mixed, out, fore, alone = call(
+    ahead, behind, part = call(
+        functools.partial(early_body, ny, nx, rs),
+        [((HALO, D), BF), ((HALO, D), BF), ((EXT, 6 * LANE), BF)],
+        (before, after, scale, normed, own),
+        "VVAAV>VVV",
+        cost=(3e8, 4e6),
+        limit=8,
+    )
+    raw, q, kv, probs, whead, mixed, out, fore, alone = call(
         functools.partial(forward_body, ny, nx, rs, ro),
         [
-            (own.shape, BF),
-            (own.shape, BF),
+            ((2, *own.shape), BF),
             ((PTS, HD), BF),
             ((EXT, D), BF),
             ((HEADS, PTS, EXT), BF),
@@ -478,8 +497,8 @@
             ((members, PTS, NVAR), BF),
             ((PTS, NVAR), F32),
         ],
-        (ahead, normed, behind, inputs, count, own, other),
-        "VAVAAVV>HHHHHAVVVV",
+        (ahead, normed, behind, part, inputs, count, own, other),
+        "VAVVAAVV>HHHHAVVVV",
         scratch=(
             pltpu.VMEM((EXT, 3 * HD), BF),
             pltpu.VMEM((HEADS, PTS, EXT), BF),
@@ -505,18 +524,17 @@
     gq, mid, lower, upper = call(
         functools.partial(backward_body, ny, nx, 6 * rs, ro),
         [((PTS, HD), BF), ((PTS, D), F32), ((HALO, D), BF), ((HALO, D), BF)],
-        (gf, whead, own_hbm, other_hbm, q, kv, probs),
-        "HHHHHHH>AAAA",
+        (gf, whead, raw, q, kv, probs),
+        "HHHHHH>AAAA",
         scratch=(
             pltpu.VMEM(gf.shape, BF),
             pltpu.VMEM(whead.shape, BF),
-            pltpu.VMEM((pn, zh_n, 4 * ro, LANE), BF),
-            pltpu.VMEM((pn, zh_n, 4 * ro, LANE), BF),
+            pltpu.VMEM((2, pn, zh_n, 4 * ro, LANE), BF),
             pltpu.VMEM(q.shape, BF),
             pltpu.VMEM(kv.shape, BF),
             pltpu.VMEM(probs.shape, BF),
-            pltpu.VMEM((PTS, D), BF),
-            pltpu.SemaphoreType.DMA((7,)),
+            pltpu.VMEM((PTS, HD), BF),
+            pltpu.SemaphoreType.DMA((6,)),
         ),
         cost=(1e9, 4e6),
         limit=16,
@@ -544,12 +562,13 @@
     total, grad_input = call(
         functools.partial(final_body, ny, nx, rs),
         [((PTS, D), F32), ((PTS, D), BF)],
-        (inputs, scale, gf, whead, own_hbm, other_hbm, gq, mid, first, last),
-        "AAAAVHAAVV>AA",
+        (inputs, scale, gf, whead, raw, gq, mid, first, last),
+        "AAAAHAAVV>AA",
         scratch=(
             pltpu.VMEM((PTS, 3 * HD), BF),
-            pltpu.VMEM((pn, zh_n, 6 * rs, LANE), BF),
-            pltpu.SemaphoreType.DMA((1,)),
+            pltpu.VMEM((PTS, D), F32),
+            pltpu.VMEM((2, pn, zh_n, 6 * rs, LANE), BF),
+            pltpu.SemaphoreType.DMA((zh_n,)),
         ),
         cost=(1e9, 4e6),
         limit=16,

time: 186 us -> 183 us (0.984)
  Pallas kernels: 28.5 us -> 26.3 us
    pallas_call x10, Pallas kernels: 28.5 us -> 26.3 us  [call(): pl.pallas_call(body, out_shape=tuple(shapes), in_specs=[SPECS[at] for at...]
  transfers between devices with their start and end apart: 6 -> 6, of which waited for: 3 -> 3; matrix products, arithmetic and copies ran while one was open for 0% -> 0% of each run, Pallas kernels for 7% -> 8%
where the time goes in v6:
time: 183 us; the launch traced here: 182 us
  blocking collectives  109 us (60%)
  starting transfers between devices  27.2 us (15%)
  Pallas kernels  26.3 us (14%)
  waiting for transfers between devices  18.2 us (10%)
    all_to_all x2, blocking collectives, widened(): lax.all_to_all(jnp.broadcast_to(block[None], (n, *block.shape)), ('core',...  30.5 us
    all_to_all x1, blocking collectives, shards(): column = lax.all_to_all(column, 'zh', 0, 0, tiled=True)  29.9 us
    pallas_call x10, Pallas kernels, call(): pl.pallas_call(body, out_shape=tuple(shapes), in_specs=[SPECS[at] for at...  26.3 us
    all_to_all x1, blocking collectives, shards(): column = lax.all_to_all(partial, 'zh', 0, 0, tiled=True)  22.1 us
    ppermute x1, waiting for transfers between devices, shards(): last = lax.ppermute(lower, GRID, down)  15.9 us
    all_to_all x1, blocking collectives, shards(): every = lax.all_to_all(fore, MEMBER, 0, 0, tiled=True)  13.9 us
    all_to_all x1, blocking collectives, shards(): plane = lax.all_to_all(wg, PLANE, 0, 0, tiled=True)  12.3 us
    ppermute x1, starting transfers between devices, shards(): before = lax.ppermute(inputs[PTS - HALO:], GRID, up)  11.6 us
  transfers between devices with their start and end apart: 6, of which 3 were waited for; matrix products, arithmetic and copies ran while one was open for 0% of the time, Pallas kernels for 8%

profile of v6, /device:TPU:30, one launch (start us, length us, event | category | flops | bytes accessed | tf_op | source)
XLA Modules:
  0.0 182.4 jit_solution(12994286273957926872)
XLA Ops:
  0.6 0.8 shard_map.121
  1.4 29.9 %all_to_all.35 = bf16[4,136,128]{2,1,0:T(8,128)(2,1)S(1)} all-to-all(bf16[4,136,128]{2,1,0:T(8,128)(2,1)S(1)} %shard_map.121), channel_id=1, replica_groups=mesh['zl'=4,'core'=2,'zh'=4,'y'=4,'x'=4] {'zh'}, dimensions={0} | all-to-all | bytes 278528 | tf_op jit(solution)/shard_map/all_to_all | solution.py:447
  31.4 10.8 %all_to_all.36 = bf16[4,4,136,128]{3,2,1,0:T(8,128)(2,1)S(1)} all-to-all(bf16[4,4,136,128]{3,2,1,0:T(8,128)(2,1)S(1)} %broadcast_in_dim.8), channel_id=1, replica_groups={{0,1,2,3},{4,5,6,7},{8,9,10,11},{12,13,14,15},{64,68,72,76},{65,69,73,7..., dimensions={0} | all-to-all | bytes 1114112 | tf_op jit(solution)/shard_map/all_to_all | solution.py:467
  42.5 19.8 %all_to_all.37 = bf16[4,4,4,136,128]{4,3,2,1,0:T(8,128)(2,1)S(1)} all-to-all(bf16[4,4,4,136,128]{4,3,2,1,0:T(8,128)(2,1)S(1)} %broadcast_in_dim.9), channel_id=1, replica_groups={{0,4,8,12},{1,5,9,13},{2,6,10,14},{3,7,11,15},{64,65,66,67},{68,69,70,7..., dimensions={0} | all-to-all | bytes 4456448 | tf_op jit(solution)/shard_map/all_to_all | solution.py:467
  62.3 1.9 %collective-permute-start.2 = (bf16[16,4,136,128]{3,2,1,0:T(8,128)(2,1)S(1)}, bf16[16,4,136,128]{3,2,1,0:T(8,128)(2,1)}, u32[]{:S(2)}, u32[]{:S(2)}) collective-permute-start(bf16[16,4,136,128]{3,2,1,0:T(8,128)(2,1)S(1)} %bitcast.9), channel_id=1, source_target_pairs={{0,64},{64,0},{1,65},{65,1},{2,66},{66,2},{3,67},{67,3},{4,68},{68... | collective-permute-start | bytes 6684680 | tf_op jit(solution)/shard_map/ppermute | solution.py:478
  64.2 2.4 %collective-permute-start.1 = (bf16[32,1024]{1,0:T(8,128)(2,1)S(1)}, bf16[32,1024]{1,0:T(8,128)(2,1)S(1)}, u32[]{:S(2)}, u32[]{:S(2)}) collective-permute-start(bf16[32,1024]{1,0:T(8,128)(2,1)S(1)} %get-tuple-element.52), channel_id=1, source_target_pairs={{1,0},{2,1},{3,2},{4,3},{5,4},{6,5},{7,6},{8,7},{9,8},{10,9},{11,1... | collective-permute-start | bytes 196616 | tf_op jit(solution)/shard_map/ppermute | solution.py:449
  66.6 11.6 %collective-permute-start = (bf16[32,1024]{1,0:T(8,128)(2,1)S(1)}, bf16[32,1024]{1,0:T(8,128)(2,1)S(1)}, u32[]{:S(2)}, u32[]{:S(2)}) collective-permute-start(bf16[32,1024]{1,0:T(8,128)(2,1)S(1)} %get-tuple-element.53), channel_id=1, source_target_pairs={{0,1},{1,2},{2,3},{3,4},{4,5},{5,6},{6,7},{7,8},{8,9},{9,10},{10,1... | collective-permute-start | bytes 196616 | tf_op jit(solution)/shard_map/ppermute | solution.py:448
  78.3 0.6 broadcast_subtract_fusion.rel
  79.0 2.0 %shard_map.120 = (bf16[128,1024]{1,0:T(8,128)(2,1)}, f32[128,192]{1,0:T(8,128)}) custom-call(bf16[128,1024]{1,0:T(8,128)(2,1)} %bitcast.12, f32[1,1024]{1,0:T(1,128)} %bitcast.15, s32[128,8]{1,0:T(8,128)} %broadcast_subtract_fusion.rel), custom_call_target="tpu_custom_call" | custom-call | flops 4000000 | bytes 1000000 | tf_op jit(solution)/shard_map/pallas_call | solution.py:63
  80.9 2.0 %collective-permute-done.1.after = bf16[32,1024]{1,0:T(8,128)(2,1)S(1)} collective-permute-done((bf16[32,1024]{1,0:T(8,128)(2,1)S(1)}, bf16[32,1024]{1,0:T(8,128)(2,1)S(1)}, u32[]{:S(2)}, u32[]{:S(2)}) %collective-permute-start.1) | collective-permute-done | bytes 65568 | tf_op jit(solution)/shard_map/ppermute | solution.py:449
  82.9 1.7 shard_map.122
  84.7 6.5 %shard_map.123 = (bf16[2,16,4,136,128]{4,3,2,1,0:T(8,128)(2,1)}, bf16[128,512]{1,0:T(8,128)(2,1)}, bf16[192,1024]{1,0:T(8,128)(2,1)}, bf16[8,128,192]{2,1,0:T(8,...) custom-call(bf16[32,1024]{1,0:T(8,128)(2,1)S(1)} %get-tuple-element., ...), custom_call_target="tpu_custom_call" | custom-call | flops 2000000000 | bytes 10000000 | tf_op jit(solution)/shard_map/pallas_call | solution.py:63
  91.1 13.9 %all_to_all.38.every = bf16[8,128,128]{2,1,0:T(8,128)(2,1)S(1)} all-to-all(bf16[8,128,128]{2,1,0:T(8,128)(2,1)S(1)} %get-tuple-element.33), channel_id=1, replica_groups=mesh['zl'=4,'core'=2,'zh'=4,'y'=4,'x'=4] {'zl','core'}, dimensions={0} | all-to-all | bytes 524288 | tf_op jit(solution)/shard_map/all_to_all | solution.py:511
  105.0 1.1 shard_map.124
  106.2 12.3 %all_to_all.39.parts = bf16[16,4,24,128]{3,2,1,0:T(8,128)(2,1)S(1)} all-to-all(bf16[16,4,24,128]{3,2,1,0:T(8,128)(2,1)} %get-tuple-element.48), channel_id=1, replica_groups=mesh['zl'=4,'core'=2,'zh'=4,'y'=4,'x'=4] {'y','x'}, dimensions={0} | all-to-all | bytes 786432 | tf_op jit(solution)/shard_map/all_to_all | solution.py:523
  118.5 0.7 shard_map.127
  119.1 22.1 %all_to_all.40.parts = bf16[4,24,128]{2,1,0:T(8,128)(2,1)S(1)} all-to-all(bf16[4,24,128]{2,1,0:T(8,128)(2,1)} %shard_map.127), channel_id=1, replica_groups=mesh['zl'=4,'core'=2,'zh'=4,'y'=4,'x'=4] {'zh'}, dimensions={0} | all-to-all | bytes 49152 | tf_op jit(solution)/shard_map/all_to_all | solution.py:552
  141.8 3.3 %all-to-all-start.6 = ((bf16[8,24,128]{2,1,0:T(8,128)(2,1)}), bf16[8,24,128]{2,1,0:T(8,128)(2,1)S(1)}, u32[]{:S(2)}, u32[]{:S(2)}) async-start(bf16[8,24,128]{2,1,0:T(8,128)(2,1)} %shard_map.128), calls=%async_computation.6 | async-start | bytes 98304 | tf_op jit(solution)/shard_map/all_to_all | solution.py:561
  145.2 5.4 %shard_map.125 = (bf16[128,512]{1,0:T(8,128)(2,1)}, f32[128,1024]{1,0:T(8,128)}, bf16[32,1024]{1,0:T(8,128)(2,1)}, bf16[32,1024]{1,0:T(8,128)(2,1)}) custom-call(bf16[128,128]{1,0:T(8,128)(2,1)} %get-tuple-element.37.gf_in.gf, bf16[1024,128]{1,0:T(8,128)(2,1)} %get-tuple-element.38.whead_in.whead, bf16[2,16,4,136,128]{4,3,2,1,0:T(8,128)(2,1)} %get-tuple-element.39.raw_in, ...), custom_call_target="tpu_custom_call" | custom-call | flops 1000000000 | bytes 4000000 | tf_op jit(solution)/shard_map/pallas_call | solution.py:63
  150.6 6.1 %collective-permute-start.3 = (bf16[32,1024]{1,0:T(8,128)(2,1)}, bf16[32,1024]{1,0:T(8,128)(2,1)S(1)}, u32[]{:S(2)}, u32[]{:S(2)}) collective-permute-start(bf16[32,1024]{1,0:T(8,128)(2,1)} %get-tuple-element.45), channel_id=1, source_target_pairs={{0,1},{1,2},{2,3},{3,4},{4,5},{5,6},{6,7},{7,8},{8,9},{9,10},{10,1... | collective-permute-start | bytes 196616 | tf_op jit(solution)/shard_map/ppermute | solution.py:543
  156.7 1.9 %collective-permute-start.4 = (bf16[32,1024]{1,0:T(8,128)(2,1)}, bf16[32,1024]{1,0:T(8,128)(2,1)S(1)}, u32[]{:S(2)}, u32[]{:S(2)}) collective-permute-start(bf16[32,1024]{1,0:T(8,128)(2,1)} %get-tuple-element.46), channel_id=1, source_target_pairs={{1,0},{2,1},{3,2},{4,3},{5,4},{6,5},{7,6},{8,7},{9,8},{10,9},{11,1... | collective-permute-start | bytes 196616 | tf_op jit(solution)/shard_map/ppermute | solution.py:542
  158.9 15.9 %collective-permute-done.4.last = bf16[32,1024]{1,0:T(8,128)(2,1)S(1)} collective-permute-done((bf16[32,1024]{1,0:T(8,128)(2,1)}, bf16[32,1024]{1,0:T(8,128)(2,1)S(1)}, u32[]{:S(2)}, u32[]{:S(2)}) %collective-permute-start.4) | collective-permute-done | bytes 65568 | tf_op jit(solution)/shard_map/ppermute | solution.py:542
  174.8 5.7 %shard_map.126 = (f32[128,1024]{1,0:T(8,128)}, bf16[128,1024]{1,0:T(8,128)(2,1)}) custom-call(bf16[128,1024]{1,0:T(8,128)(2,1)} %bitcast.14, f32[1,1024]{1,0:T(1,128)} %bitcast.17, bf16[128,128]{1,0:T(8,128)(2,1)} %get-tuple-element.37.gf_in.gf, bf16[1024,128]{1,0:T(8,128)(2,1)} %get-tuple-element.38.whead_in.whead, ...), custom_call_target="tpu_custom_call" | custom-call | flops 1000000000 | bytes 4000000 | tf_op jit(solution)/shard_map/pallas_call | solution.py:63
  180.6 1.8 shard_map.129
  (15 shorter events, 1.4 us)
Async XLA Ops:
  42.5 21.7 %copy-start.1 = (bf16[1,128,1024]{2,1,0:T(8,128)(2,1)S(1)}, bf16[1,128,1024]{2,1,0:T(8,128)(2,1)}, u32[]{:S(2)}) copy-start(bf16[1,128,1024]{2,1,0:T(8,128)(2,1)} %param.9) | copy-start | bytes 786436
  42.5 35.7 %copy-start.2 = (s32[128,8]{0,1:T(8,128)S(1)}, s32[128,8]{0,1:T(8,128)}, u32[]{:S(2)}) copy-start(s32[128,8]{0,1:T(8,128)} %param.16) | copy-start | bytes 12292
  62.3 22.4 %collective-permute-start.2 = (bf16[16,4,136,128]{3,2,1,0:T(8,128)(2,1)S(1)}, bf16[16,4,136,128]{3,2,1,0:T(8,128)(2,1)}, u32[]{:S(2)}, u32[]{:S(2)}) collective-permute-start(bf16[16,4,136,128]{3,2,1,0:T(8,128)(2,1)S(1)} %bitcast.9), channel_id=1, source_target_pairs={{0,64},{64,0},{1,65},{65,1},{2,66},{66,2},{3,67},{67,3},{4,68},{68... | collective-permute-start | bytes 6684680 | tf_op jit(solution)/shard_map/ppermute | solution.py:478
  64.2 18.7 %collective-permute-start.1 = (bf16[32,1024]{1,0:T(8,128)(2,1)S(1)}, bf16[32,1024]{1,0:T(8,128)(2,1)S(1)}, u32[]{:S(2)}, u32[]{:S(2)}) collective-permute-start(bf16[32,1024]{1,0:T(8,128)(2,1)S(1)} %get-tuple-element.52), channel_id=1, source_target_pairs={{1,0},{2,1},{3,2},{4,3},{5,4},{6,5},{7,6},{8,7},{9,8},{10,9},{11,1... | collective-permute-start | bytes 196616 | tf_op jit(solution)/shard_map/ppermute | solution.py:449
  66.6 16.3 %collective-permute-start = (bf16[32,1024]{1,0:T(8,128)(2,1)S(1)}, bf16[32,1024]{1,0:T(8,128)(2,1)S(1)}, u32[]{:S(2)}, u32[]{:S(2)}) collective-permute-start(bf16[32,1024]{1,0:T(8,128)(2,1)S(1)} %get-tuple-element.53), channel_id=1, source_target_pairs={{0,1},{1,2},{2,3},{3,4},{4,5},{5,6},{6,7},{7,8},{8,9},{9,10},{10,1... | collective-permute-start | bytes 196616 | tf_op jit(solution)/shard_map/ppermute | solution.py:448
  84.6 20.4 %copy-start = (f32[128,128]{1,0:T(8,128)S(1)}, f32[128,128]{1,0:T(8,128)}, u32[]{:S(2)}) copy-start(f32[128,128]{1,0:T(8,128)} %observed.1) | copy-start | bytes 196612
  141.8 38.7 %all-to-all-start.6 = ((bf16[8,24,128]{2,1,0:T(8,128)(2,1)}), bf16[8,24,128]{2,1,0:T(8,128)(2,1)S(1)}, u32[]{:S(2)}, u32[]{:S(2)}) async-start(bf16[8,24,128]{2,1,0:T(8,128)(2,1)} %shard_map.128), calls=%async_computation.6 | async-start | bytes 98304 | tf_op jit(solution)/shard_map/all_to_all | solution.py:561
  150.6 8.3 %collective-permute-start.3 = (bf16[32,1024]{1,0:T(8,128)(2,1)}, bf16[32,1024]{1,0:T(8,128)(2,1)S(1)}, u32[]{:S(2)}, u32[]{:S(2)}) collective-permute-start(bf16[32,1024]{1,0:T(8,128)(2,1)} %get-tuple-element.45), channel_id=1, source_target_pairs={{0,1},{1,2},{2,3},{3,4},{4,5},{5,6},{6,7},{7,8},{8,9},{9,10},{10,1... | collective-permute-start | bytes 196616 | tf_op jit(solution)/shard_map/ppermute | solution.py:543
  156.7 18.1 %collective-permute-start.4 = (bf16[32,1024]{1,0:T(8,128)(2,1)}, bf16[32,1024]{1,0:T(8,128)(2,1)S(1)}, u32[]{:S(2)}, u32[]{:S(2)}) collective-permute-start(bf16[32,1024]{1,0:T(8,128)(2,1)} %get-tuple-element.46), channel_id=1, source_target_pairs={{1,0},{2,1},{3,2},{4,3},{5,4},{6,5},{7,6},{8,7},{9,8},{10,9},{11,1... | collective-permute-start | bytes 196616 | tf_op jit(solution)/shard_map/ppermute | solution.py:542

commit v7 on v6

--- a/solution.py
+++ b/solution.py
@@ -152,11 +152,17 @@
     return total.astype(BF)
 
 
+def is_even(shape):
+    return jnp.full(shape, lax.rem(lax.axis_index("x"), 2), jnp.int32) == 0
+
+
 def early_body(
-    ny, nx, rs, before, after, scale, normed, own, ahead, behind, part
+    ny, nx, rs, inside, across, scale, normed, own, ahead, behind, part
 ):
-    for block, to in ((before, ahead), (after, behind)):
-        centred, _ = normalised(block[...])
+    even = is_even((HALO, D))
+    a, b = inside[...].astype(F32), across[...].astype(F32)
+    for block, to in ((jnp.where(even, b, a), ahead), (jnp.where(even, a, b), behind)):
+        centred, _ = normalised(block)
         to[...] = (centred * scale[...]).astype(BF)
     rows = jnp.concatenate([ahead[...], normed[...], behind[...]], axis=0)
 
@@ -168,14 +174,21 @@
 
 def forward_body(
     ny, nx, rs, ro, ahead, normed, behind, part, states, count, own, other,
-    raw, q_out, kv_out, probs_out, whead, mixed, out, fore, alone,
+    raw_in, raw_out, q_out, kv_out, probs_out, whead, mixed, out, fore, alone,
     qkv, probs, added_out, sems,
 ):
     pn, zh_n = own.shape[:2]
     qrows = 6 * rs
     orows = 4 * ro
     hr = rs // 2
-    raws = fetched(((own, raw.at[0]), (other, raw.at[1])), sems.at[pl.ds(3, 2)])
+    raws = fetched(
+        [
+            (buf.at[:, :, pl.ds(start, to.shape[3]), :], to.at[i])
+            for i, buf in enumerate((own, other))
+            for start, to in ((qrows, raw_out), (0, raw_in))
+        ],
+        sems.at[pl.ds(3, 4)],
+    )
     for copy in raws:
         copy.start()
     rows = jnp.concatenate([ahead[...], normed[...], behind[...]], axis=0)
@@ -282,17 +295,16 @@
 
 
 def backward_body(
-    ny, nx, at_out, ro, gf_in, whead_in, raw_in, q_in, kv_in, probs_in,
-    gq, mid, lower, upper,
+    ny, nx, ro, gf_in, whead_in, raw_in, q_in, kv_in, probs_in,
+    gq, mid, inside, across,
     gf, whead, raw, q, kv, probs, gm_held, sems,
 ):
     zh_n = raw.shape[2]
-    size = raw.shape[3]
     copies = fetched(
         (
             (gf_in, gf),
             (whead_in, whead),
-            (raw_in.at[:, :, :, pl.ds(at_out, size), :], raw),
+            (raw_in, raw),
             (kv_in, kv),
             (probs_in, probs),
             (q_in, q),
@@ -341,38 +353,32 @@
             gvs.append(tn(held, g2))
         gq[:, at] = jnp.where(halves((PTS, LANE), 0), gqs[0], gqs[1]).astype(BF)
         pick = halves((EXT, LANE), 0)
+        even = is_even((HALO, LANE))
         for where_at, parts in ((at, gks), (vat, gvs)):
             total = jnp.where(pick, parts[0], parts[1])
-            lower[:, where_at] = total[:HALO].astype(BF)
+            lower, upper = total[:HALO], total[HALO + PTS :]
+            inside[:, where_at] = jnp.where(even, upper, lower).astype(BF)
+            across[:, where_at] = jnp.where(even, lower, upper).astype(BF)
             mid[:, where_at] = total[HALO : HALO + PTS]
-            upper[:, where_at] = total[HALO + PTS :].astype(BF)
 
 
 def final_body(
-    ny, nx, rs, states, scale, gf, whead, raw_in, gq, mid, first, last,
-    total, grad, given, held, raw, sems,
+    ny, nx, rs, states, scale, gf, whead, raw, gq, mid, inside, across,
+    total, grad, given, held,
 ):
     zh_n = raw.shape[2]
-    copies = fetched(
-        [
-            (raw_in.at[:, :, zh, pl.ds(0, raw.shape[3]), :], raw.at[:, :, zh])
-            for zh in range(zh_n)
-        ],
-        sems,
-    )
-    for copy in copies:
-        copy.start()
     centred, inverse = normalised(states[...])
     total[...] = mid[...]
-    total[:HALO, :] += first[...].astype(F32)
-    total[PTS - HALO :, :] += last[...].astype(F32)
+    even = is_even((HALO, D))
+    a, b = inside[...].astype(F32), across[...].astype(F32)
+    total[:HALO, :] += jnp.where(even, b, a)
+    total[PTS - HALO :, :] += jnp.where(even, a, b)
     given[:, :HD] = gq[...]
     given[:, HD:] = total[...].astype(BF)
 
     def widen(c):
         depth = raw.shape[1] * rs
         for zh in range(zh_n):
-            copies[zh].wait()
             column = 0.0
             for side in range(2):
                 order = places(side, ny, nx)
@@ -433,8 +439,8 @@
     rs, ro = query.shape[0], out_w.shape[0]
     packed = 6 * rs + 4 * ro + rs // 2
     swap = [(0, 1), (1, 0)]
-    up = [(i, i + 1) for i in range(devices - 1)]
-    down = [(j, i) for i, j in up]
+    inner = [(i, i ^ 1) for i in range(devices)]
+    outer = [(i, i + 1 if i % 2 else i - 1) for i in range(1, devices - 1)]
 
     (column,) = call(
         pack_body,
@@ -445,8 +451,13 @@
         limit=4,
     )
     column = lax.all_to_all(column, "zh", 0, 0, tiled=True)
-    before = lax.ppermute(inputs[PTS - HALO :], GRID, up)
-    after = lax.ppermute(inputs[:HALO], GRID, down)
+    even = lax.rem(lax.axis_index("x"), 2) == 0
+    inside = lax.ppermute(
+        jnp.where(even, inputs[PTS - HALO :], inputs[:HALO]), GRID, inner
+    )
+    across = lax.ppermute(
+        jnp.where(even, inputs[:HALO], inputs[PTS - HALO :]), GRID, outer
+    )
     rel = neighbours - (lax.axis_index(GRID) * PTS - HALO)
     scale = norm_scale.reshape(1, D)
     normed, count = call(
@@ -479,15 +490,16 @@
     ahead, behind, part = call(
         functools.partial(early_body, ny, nx, rs),
         [((HALO, D), BF), ((HALO, D), BF), ((EXT, 6 * LANE), BF)],
-        (before, after, scale, normed, own),
+        (inside, across, scale, normed, own),
         "VVAAV>VVV",
         cost=(3e8, 4e6),
         limit=8,
     )
-    raw, q, kv, probs, whead, mixed, out, fore, alone = call(
+    raw_in, raw_out, q, kv, probs, whead, mixed, out, fore, alone = call(
         functools.partial(forward_body, ny, nx, rs, ro),
         [
-            ((2, *own.shape), BF),
+            ((2, pn, zh_n, 6 * rs, LANE), BF),
+            ((2, pn, zh_n, 4 * ro, LANE), BF),
             ((PTS, HD), BF),
             ((EXT, D), BF),
             ((HEADS, PTS, EXT), BF),
@@ -498,12 +510,12 @@
             ((PTS, NVAR), F32),
         ],
         (ahead, normed, behind, part, inputs, count, own, other),
-        "VAVVAAVV>HHHHAVVVV",
+        "VAVVAAVV>HHHHHAVVVV",
         scratch=(
             pltpu.VMEM((EXT, 3 * HD), BF),
             pltpu.VMEM((HEADS, PTS, EXT), BF),
             pltpu.VMEM((PTS, D), F32),
-            pltpu.SemaphoreType.DMA((5,)),
+            pltpu.SemaphoreType.DMA((7,)),
         ),
         cost=(2e9, 1e7),
         limit=24,
@@ -521,10 +533,10 @@
         limit=8,
     )
     plane = lax.all_to_all(wg, PLANE, 0, 0, tiled=True)
-    gq, mid, lower, upper = call(
-        functools.partial(backward_body, ny, nx, 6 * rs, ro),
+    gq, mid, inside, across = call(
+        functools.partial(backward_body, ny, nx, ro),
         [((PTS, HD), BF), ((PTS, D), F32), ((HALO, D), BF), ((HALO, D), BF)],
-        (gf, whead, raw, q, kv, probs),
+        (gf, whead, raw_out, q, kv, probs),
         "HHHHHH>AAAA",
         scratch=(
             pltpu.VMEM(gf.shape, BF),
@@ -539,8 +551,8 @@
         cost=(1e9, 4e6),
         limit=16,
     )
-    last = lax.ppermute(lower, GRID, down)
-    first = lax.ppermute(upper, GRID, up)
+    inside = lax.ppermute(inside, GRID, inner)
+    across = lax.ppermute(across, GRID, outer)
     (partial,) = call(
         sum_body,
         [(wg.shape[1:], BF)],
@@ -562,13 +574,11 @@
     total, grad_input = call(
         functools.partial(final_body, ny, nx, rs),
         [((PTS, D), F32), ((PTS, D), BF)],
-        (inputs, scale, gf, whead, raw, gq, mid, first, last),
-        "AAAAHAAVV>AA",
+        (inputs, scale, gf, whead, raw_in, gq, mid, inside, across),
+        "AAAAVAAVV>AA",
         scratch=(
             pltpu.VMEM((PTS, 3 * HD), BF),
             pltpu.VMEM((PTS, D), F32),
-            pltpu.VMEM((2, pn, zh_n, 6 * rs, LANE), BF),
-            pltpu.SemaphoreType.DMA((zh_n,)),
         ),
         cost=(1e9, 4e6),
         limit=16,

time: 183 us -> 172 us (0.940)
  blocking collectives: 109 us -> 102 us
  starting transfers between devices: 27.2 us -> 23.4 us
  Pallas kernels: 26.3 us -> 24.4 us
    all_to_all x1, blocking collectives: 22.1 us -> 17.5 us  [shards(): column = lax.all_to_all(partial, 'zh', 0, 0, tiled=True)]
    ppermute x4, starting transfers between devices: 22 us -> 18.2 us  [the longest x1 7.71 us: shards(): lax.ppermute(jnp.where(even, inputs[:HALO], inputs[PTS - HALO:]), GRID, o...]
    pallas_call x10, Pallas kernels: 26.3 us -> 24.4 us  [call(): pl.pallas_call(body, out_shape=tuple(shapes), in_specs=[SPECS[at] for at...]
  transfers between devices with their start and end apart: 6 -> 6, of which waited for: 3 -> 2; matrix products, arithmetic and copies ran while one was open for 0% -> 0% of each run, Pallas kernels for 8% -> 7%
where the time goes in v7:
time: 172 us; the launch traced here: 171 us
  blocking collectives  102 us (59%)
  Pallas kernels  24.4 us (14%)
  starting transfers between devices  23.4 us (14%)
  waiting for transfers between devices  19.2 us (11%)
    all_to_all x2, blocking collectives, widened(): lax.all_to_all(jnp.broadcast_to(block[None], (n, *block.shape)), ('core',...  30.5 us
    all_to_all x1, blocking collectives, shards(): column = lax.all_to_all(column, 'zh', 0, 0, tiled=True)  29.9 us
    pallas_call x10, Pallas kernels, call(): pl.pallas_call(body, out_shape=tuple(shapes), in_specs=[SPECS[at] for at...  24.4 us
    all_to_all x1, blocking collectives, shards(): column = lax.all_to_all(partial, 'zh', 0, 0, tiled=True)  17.5 us
    ppermute x1, waiting for transfers between devices, shards(): across = lax.ppermute(across, GRID, outer)  12.8 us
    all_to_all x1, blocking collectives, shards(): plane = lax.all_to_all(wg, PLANE, 0, 0, tiled=True)  12.3 us
    all_to_all x1, blocking collectives, shards(): every = lax.all_to_all(fore, MEMBER, 0, 0, tiled=True)  12.1 us
    ppermute x1, starting transfers between devices, shards(): lax.ppermute(jnp.where(even, inputs[:HALO], inputs[PTS - HALO:]), GRID, o...  7.71 us
  transfers between devices with their start and end apart: 6, of which 2 were waited for; matrix products, arithmetic and copies ran while one was open for 0% of the time, Pallas kernels for 7%

profile of v7, /device:TPU:30, one launch (start us, length us, event | category | flops | bytes accessed | tf_op | source)
XLA Modules:
  0.0 171.3 jit_solution(10287313477914057542)
XLA Ops:
  0.6 0.8 shard_map.121
  1.4 29.9 %all_to_all.35 = bf16[4,136,128]{2,1,0:T(8,128)(2,1)S(1)} all-to-all(bf16[4,136,128]{2,1,0:T(8,128)(2,1)S(1)} %shard_map.121), channel_id=1, replica_groups=mesh['zl'=4,'core'=2,'zh'=4,'y'=4,'x'=4] {'zh'}, dimensions={0} | all-to-all | bytes 278528 | tf_op jit(solution)/shard_map/all_to_all | solution.py:453
  31.4 10.8 %all_to_all.36 = bf16[4,4,136,128]{3,2,1,0:T(8,128)(2,1)S(1)} all-to-all(bf16[4,4,136,128]{3,2,1,0:T(8,128)(2,1)S(1)} %broadcast_in_dim.8), channel_id=1, replica_groups={{0,1,2,3},{4,5,6,7},{8,9,10,11},{12,13,14,15},{64,68,72,76},{65,69,73,7..., dimensions={0} | all-to-all | bytes 1114112 | tf_op jit(solution)/shard_map/all_to_all | solution.py:478
  42.5 19.8 %all_to_all.37 = bf16[4,4,4,136,128]{4,3,2,1,0:T(8,128)(2,1)S(1)} all-to-all(bf16[4,4,4,136,128]{4,3,2,1,0:T(8,128)(2,1)S(1)} %broadcast_in_dim.9), channel_id=1, replica_groups={{0,4,8,12},{1,5,9,13},{2,6,10,14},{3,7,11,15},{64,65,66,67},{68,69,70,7..., dimensions={0} | all-to-all | bytes 4456448 | tf_op jit(solution)/shard_map/all_to_all | solution.py:478
  62.3 1.9 %collective-permute-start.2 = (bf16[16,4,136,128]{3,2,1,0:T(8,128)(2,1)S(1)}, bf16[16,4,136,128]{3,2,1,0:T(8,128)(2,1)}, u32[]{:S(2)}, u32[]{:S(2)}) collective-permute-start(bf16[16,4,136,128]{3,2,1,0:T(8,128)(2,1)S(1)} %bitcast.9), channel_id=1, source_target_pairs={{0,64},{64,0},{1,65},{65,1},{2,66},{66,2},{3,67},{67,3},{4,68},{68... | collective-permute-start | bytes 6684680 | tf_op jit(solution)/shard_map/ppermute | solution.py:489
  64.2 7.7 %collective-permute-start.1 = (bf16[32,1024]{1,0:T(8,128)(2,1)S(1)}, bf16[32,1024]{1,0:T(8,128)(2,1)S(1)}, u32[]{:S(2)}, u32[]{:S(2)}) collective-permute-start(bf16[32,1024]{1,0:T(8,128)(2,1)S(1)} %get-tuple-element.54), channel_id=1, source_target_pairs={{1,2},{2,1},{3,4},{4,3},{5,6},{6,5},{7,8},{8,7},{9,10},{10,9},{11,... | collective-permute-start | bytes 196616 | tf_op jit(solution)/shard_map/ppermute | solution.py:458
  71.9 1.9 %collective-permute-start = (bf16[32,1024]{1,0:T(8,128)(2,1)S(1)}, bf16[32,1024]{1,0:T(8,128)(2,1)S(1)}, u32[]{:S(2)}, u32[]{:S(2)}) collective-permute-start(bf16[32,1024]{1,0:T(8,128)(2,1)S(1)} %get-tuple-element.55), channel_id=1, source_target_pairs={{0,1},{1,0},{2,3},{3,2},{4,5},{5,4},{6,7},{7,6},{8,9},{9,8},{10,11... | collective-permute-start | bytes 196616 | tf_op jit(solution)/shard_map/ppermute | solution.py:455
  74.0 0.6 broadcast_subtract_fusion.rel
  74.6 2.0 %shard_map.120 = (bf16[128,1024]{1,0:T(8,128)(2,1)}, f32[128,192]{1,0:T(8,128)}) custom-call(bf16[128,1024]{1,0:T(8,128)(2,1)} %bitcast.12, f32[1,1024]{1,0:T(1,128)} %bitcast.15, s32[128,8]{1,0:T(8,128)} %broadcast_subtract_fusion.rel), custom_call_target="tpu_custom_call" | custom-call | flops 4000000 | bytes 1000000 | tf_op jit(solution)/shard_map/pallas_call | solution.py:63
  76.6 6.3 %collective-permute-done.1.across = bf16[32,1024]{1,0:T(8,128)(2,1)S(1)} collective-permute-done((bf16[32,1024]{1,0:T(8,128)(2,1)S(1)}, bf16[32,1024]{1,0:T(8,128)(2,1)S(1)}, u32[]{:S(2)}, u32[]{:S(2)}) %collective-permute-start.1) | collective-permute-done | bytes 65568 | tf_op jit(solution)/shard_map/ppermute | solution.py:458
  82.9 1.7 shard_map.122
  84.7 6.5 %shard_map.123 = (bf16[2,16,4,96,128]{4,3,2,1,0:T(8,128)(2,1)}, bf16[2,16,4,32,128]{4,3,2,1,0:T(8,128)(2,1)}, bf16[128,512]{1,0:T(8,128)(2,1)}, bf16[192,1024]{1...) custom-call(bf16[32,1024]{1,0:T(8,128)(2,1)S(1)} %get-tuple-element., ...), custom_call_target="tpu_custom_call" | custom-call | flops 2000000000 | bytes 10000000 | tf_op jit(solution)/shard_map/pallas_call | solution.py:63
  91.2 12.1 %all_to_all.38.every = bf16[8,128,128]{2,1,0:T(8,128)(2,1)S(1)} all-to-all(bf16[8,128,128]{2,1,0:T(8,128)(2,1)S(1)} %get-tuple-element.34), channel_id=1, replica_groups=mesh['zl'=4,'core'=2,'zh'=4,'y'=4,'x'=4] {'zl','core'}, dimensions={0} | all-to-all | bytes 524288 | tf_op jit(solution)/shard_map/all_to_all | solution.py:523
  103.3 1.2 shard_map.124
  104.5 12.3 %all_to_all.39.parts = bf16[16,4,24,128]{3,2,1,0:T(8,128)(2,1)S(1)} all-to-all(bf16[16,4,24,128]{3,2,1,0:T(8,128)(2,1)} %get-tuple-element.50), channel_id=1, replica_groups=mesh['zl'=4,'core'=2,'zh'=4,'y'=4,'x'=4] {'y','x'}, dimensions={0} | all-to-all | bytes 786432 | tf_op jit(solution)/shard_map/all_to_all | solution.py:535
  116.8 0.7 shard_map.127
  117.4 17.5 %all_to_all.40.parts = bf16[4,24,128]{2,1,0:T(8,128)(2,1)S(1)} all-to-all(bf16[4,24,128]{2,1,0:T(8,128)(2,1)} %shard_map.127), channel_id=1, replica_groups=mesh['zl'=4,'core'=2,'zh'=4,'y'=4,'x'=4] {'zh'}, dimensions={0} | all-to-all | bytes 49152 | tf_op jit(solution)/shard_map/all_to_all | solution.py:564
  135.5 3.3 %all-to-all-start.6 = ((bf16[8,24,128]{2,1,0:T(8,128)(2,1)}), bf16[8,24,128]{2,1,0:T(8,128)(2,1)S(1)}, u32[]{:S(2)}, u32[]{:S(2)}) async-start(bf16[8,24,128]{2,1,0:T(8,128)(2,1)} %shard_map.128), calls=%async_computation.6 | async-start | bytes 98304 | tf_op jit(solution)/shard_map/all_to_all | solution.py:573
  138.9 5.4 %shard_map.125 = (bf16[128,512]{1,0:T(8,128)(2,1)}, f32[128,1024]{1,0:T(8,128)}, bf16[32,1024]{1,0:T(8,128)(2,1)}, bf16[32,1024]{1,0:T(8,128)(2,1)}) custom-call(bf16[128,128]{1,0:T(8,128)(2,1)} %get-tuple-element.38.gf_in.gf, bf16[1024,128]{1,0:T(8,128)(2,1)} %get-tuple-element.39.whead_in.whead, bf16[2,16,4,32,128]{4,3,2,1,0:T(8,128)(2,1)} %get-tuple-element.41.raw_in, ...), custom_call_target="tpu_custom_call" | custom-call | flops 1000000000 | bytes 4000000 | tf_op jit(solution)/shard_map/pallas_call | solution.py:63
  144.3 2.7 %collective-permute-start.3 = (bf16[32,1024]{1,0:T(8,128)(2,1)}, bf16[32,1024]{1,0:T(8,128)(2,1)S(1)}, u32[]{:S(2)}, u32[]{:S(2)}) collective-permute-start(bf16[32,1024]{1,0:T(8,128)(2,1)} %get-tuple-element.47), channel_id=1, source_target_pairs={{0,1},{1,0},{2,3},{3,2},{4,5},{5,4},{6,7},{7,6},{8,9},{9,8},{10,11... | collective-permute-start | bytes 196616 | tf_op jit(solution)/shard_map/ppermute | solution.py:554
  147.0 5.9 %collective-permute-start.4 = (bf16[32,1024]{1,0:T(8,128)(2,1)}, bf16[32,1024]{1,0:T(8,128)(2,1)S(1)}, u32[]{:S(2)}, u32[]{:S(2)}) collective-permute-start(bf16[32,1024]{1,0:T(8,128)(2,1)} %get-tuple-element.48), channel_id=1, source_target_pairs={{1,2},{2,1},{3,4},{4,3},{5,6},{6,5},{7,8},{8,7},{9,10},{10,9},{11,... | collective-permute-start | bytes 196616 | tf_op jit(solution)/shard_map/ppermute | solution.py:555
  152.9 12.8 %collective-permute-done.4.across = bf16[32,1024]{1,0:T(8,128)(2,1)S(1)} collective-permute-done((bf16[32,1024]{1,0:T(8,128)(2,1)}, bf16[32,1024]{1,0:T(8,128)(2,1)S(1)}, u32[]{:S(2)}, u32[]{:S(2)}) %collective-permute-start.4) | collective-permute-done | bytes 65568 | tf_op jit(solution)/shard_map/ppermute | solution.py:555
  165.7 3.7 %shard_map.126 = (f32[128,1024]{1,0:T(8,128)}, bf16[128,1024]{1,0:T(8,128)(2,1)}) custom-call(bf16[128,1024]{1,0:T(8,128)(2,1)} %bitcast.14, f32[1,1024]{1,0:T(1,128)} %bitcast.17, bf16[128,128]{1,0:T(8,128)(2,1)} %get-tuple-element.38.gf_in.gf, bf16[1024,128]{1,0:T(8,128)(2,1)} %get-tuple-element.39.whead_in.whead, ...), custom_call_target="tpu_custom_call" | custom-call | flops 1000000000 | bytes 4000000 | tf_op jit(solution)/shard_map/pallas_call | solution.py:63
  169.5 1.8 %shard_map.129 = (f32[8,1024]{1,0:T(8,128)}, f32[16,128]{1,0:T(8,128)}) custom-call(bf16[8,24,128]{2,1,0:T(8,128)(2,1)S(1)} %all-to-all-done.6.parts, bf16[1024,128]{1,0:T(8,128)(2,1)} %get-tuple-element.39.whead_in.whead), custom_call_target="tpu_custom_call" | custom-call | flops 100000000 | bytes 1000000 | tf_op jit(solution)/shard_map/pallas_call | solution.py:63
  (17 shorter events, 1.1 us)
Async XLA Ops:
  42.5 21.7 %copy-start.2 = (bf16[1,128,1024]{2,1,0:T(8,128)(2,1)S(1)}, bf16[1,128,1024]{2,1,0:T(8,128)(2,1)}, u32[]{:S(2)}) copy-start(bf16[1,128,1024]{2,1,0:T(8,128)(2,1)} %param.9) | copy-start | bytes 786436
  42.5 31.4 %copy-start.3 = (s32[128,8]{0,1:T(8,128)S(1)}, s32[128,8]{0,1:T(8,128)}, u32[]{:S(2)}) copy-start(s32[128,8]{0,1:T(8,128)} %param.16) | copy-start | bytes 12292
  62.3 22.4 %collective-permute-start.2 = (bf16[16,4,136,128]{3,2,1,0:T(8,128)(2,1)S(1)}, bf16[16,4,136,128]{3,2,1,0:T(8,128)(2,1)}, u32[]{:S(2)}, u32[]{:S(2)}) collective-permute-start(bf16[16,4,136,128]{3,2,1,0:T(8,128)(2,1)S(1)} %bitcast.9), channel_id=1, source_target_pairs={{0,64},{64,0},{1,65},{65,1},{2,66},{66,2},{3,67},{67,3},{4,68},{68... | collective-permute-start | bytes 6684680 | tf_op jit(solution)/shard_map/ppermute | solution.py:489
  64.2 18.7 %collective-permute-start.1 = (bf16[32,1024]{1,0:T(8,128)(2,1)S(1)}, bf16[32,1024]{1,0:T(8,128)(2,1)S(1)}, u32[]{:S(2)}, u32[]{:S(2)}) collective-permute-start(bf16[32,1024]{1,0:T(8,128)(2,1)S(1)} %get-tuple-element.54), channel_id=1, source_target_pairs={{1,2},{2,1},{3,4},{4,3},{5,6},{6,5},{7,8},{8,7},{9,10},{10,9},{11,... | collective-permute-start | bytes 196616 | tf_op jit(solution)/shard_map/ppermute | solution.py:458
  71.9 11.0 %collective-permute-start = (bf16[32,1024]{1,0:T(8,128)(2,1)S(1)}, bf16[32,1024]{1,0:T(8,128)(2,1)S(1)}, u32[]{:S(2)}, u32[]{:S(2)}) collective-permute-start(bf16[32,1024]{1,0:T(8,128)(2,1)S(1)} %get-tuple-element.55), channel_id=1, source_target_pairs={{0,1},{1,0},{2,3},{3,2},{4,5},{5,4},{6,7},{7,6},{8,9},{9,8},{10,11... | collective-permute-start | bytes 196616 | tf_op jit(solution)/shard_map/ppermute | solution.py:455
  84.7 18.7 %copy-start.1 = (f32[128,128]{1,0:T(8,128)S(1)}, f32[128,128]{1,0:T(8,128)}, u32[]{:S(2)}) copy-start(f32[128,128]{1,0:T(8,128)} %observed.1) | copy-start | bytes 196612
  116.8 49.0 %copy-start = (bf16[2,16,4,96,128]{4,3,2,1,0:T(8,128)(2,1)S(1)}, bf16[2,16,4,96,128]{4,3,2,1,0:T(8,128)(2,1)}, u32[]{:S(2)}) copy-start(bf16[2,16,4,96,128]{4,3,2,1,0:T(8,128)(2,1)} %get-tuple-element.40.raw) | copy-start | bytes 9437188
  135.5 33.9 %all-to-all-start.6 = ((bf16[8,24,128]{2,1,0:T(8,128)(2,1)}), bf16[8,24,128]{2,1,0:T(8,128)(2,1)S(1)}, u32[]{:S(2)}, u32[]{:S(2)}) async-start(bf16[8,24,128]{2,1,0:T(8,128)(2,1)} %shard_map.128), calls=%async_computation.6 | async-start | bytes 98304 | tf_op jit(solution)/shard_map/all_to_all | solution.py:573
  144.3 8.6 %collective-permute-start.3 = (bf16[32,1024]{1,0:T(8,128)(2,1)}, bf16[32,1024]{1,0:T(8,128)(2,1)S(1)}, u32[]{:S(2)}, u32[]{:S(2)}) collective-permute-start(bf16[32,1024]{1,0:T(8,128)(2,1)} %get-tuple-element.47), channel_id=1, source_target_pairs={{0,1},{1,0},{2,3},{3,2},{4,5},{5,4},{6,7},{7,6},{8,9},{9,8},{10,11... | collective-permute-start | bytes 196616 | tf_op jit(solution)/shard_map/ppermute | solution.py:554
  147.0 18.7 %collective-permute-start.4 = (bf16[32,1024]{1,0:T(8,128)(2,1)}, bf16[32,1024]{1,0:T(8,128)(2,1)S(1)}, u32[]{:S(2)}, u32[]{:S(2)}) collective-permute-start(bf16[32,1024]{1,0:T(8,128)(2,1)} %get-tuple-element.48), channel_id=1, source_target_pairs={{1,2},{2,1},{3,4},{4,3},{5,6},{6,5},{7,8},{8,7},{9,10},{10,9},{11,... | collective-permute-start | bytes 196616 | tf_op jit(solution)/shard_map/ppermute | solution.py:555

commit v8 on v7

--- a/solution.py
+++ b/solution.py
@@ -26,6 +26,7 @@
 MEMBER = ("zl", "core")
 GRID = ("zh", "y", "x")
 PLANE = ("y", "x")
+COLUMN = ("zl", "core", "zh")
 
 BF = jnp.bfloat16
 F32 = jnp.float32
@@ -364,9 +365,10 @@
 
 def final_body(
     ny, nx, rs, states, scale, gf, whead, raw, gq, mid, inside, across,
-    total, grad, given, held,
+    total, grad, head_again, given, held,
 ):
     zh_n = raw.shape[2]
+    head_again[...] = whead[...]
     centred, inverse = normalised(states[...])
     total[...] = mid[...]
     even = is_even((HALO, D))
@@ -405,10 +407,6 @@
     for i in range(1, parts.shape[0]):
         total = total + parts[i].astype(F32)
     return total
-
-
-def sum_body(parts, total):
-    total[...] = added(parts).astype(BF)
 
 
 def spread_body(parts, spread):
@@ -553,29 +551,22 @@
     )
     inside = lax.ppermute(inside, GRID, inner)
     across = lax.ppermute(across, GRID, outer)
-    (partial,) = call(
-        sum_body,
-        [(wg.shape[1:], BF)],
+    (spread,) = call(
+        spread_body,
+        [((members, *wg.shape[1:]), BF)],
         (plane,),
         "V>A",
         cost=(1e6, 1e6),
         limit=4,
     )
-    column = lax.all_to_all(partial, "zh", 0, 0, tiled=True)
-    (spread,) = call(
-        spread_body,
-        [((members, *wg.shape[2:]), BF)],
-        (column,),
-        "V>A",
-        cost=(1e6, 1e6),
-        limit=4,
-    )
-    parts = lax.all_to_all(spread, MEMBER, 0, 0, tiled=True)
-    total, grad_input = call(
+    parts = lax.all_to_all(
+        spread.reshape(members * zh_n, *wg.shape[2:]), COLUMN, 0, 0, tiled=True
+    )
+    total, grad_input, head_again = call(
         functools.partial(final_body, ny, nx, rs),
-        [((PTS, D), F32), ((PTS, D), BF)],
+        [((PTS, D), F32), ((PTS, D), BF), ((D, NVAR), BF)],
         (inputs, scale, gf, whead, raw_in, gq, mid, inside, across),
-        "AAAAVAAVV>AA",
+        "AAAAVAAVV>AAV",
         scratch=(
             pltpu.VMEM((PTS, 3 * HD), BF),
             pltpu.VMEM((PTS, D), F32),
@@ -587,8 +578,8 @@
     mixing, head = call(
         functools.partial(weights_body, scaling),
         [((HD // devices, D), F32), ((D // devices, NVAR), F32)],
-        (parts, whead),
-        "VA>AA",
+        (parts, head_again),
+        "VV>AA",
         cost=(1e8, 1e6),
         limit=8,
     )

time: 172 us -> 157 us (0.913)
  the two profiles are of different devices: /device:TPU:30 before, /device:TPU:225 now
where the time goes in v8:
time: 157 us
  blocking collectives  81.1 us (52%)
  starting transfers between devices  32.8 us (21%)
  Pallas kernels  22.9 us (15%)
  waiting for transfers between devices  16.2 us (10%)
  local copies, waits for them, and re-layouts  2.13 us (1%)
    all_to_all x2, blocking collectives, widened(): lax.all_to_all(jnp.broadcast_to(block[None], (n, *block.shape)), ('core',...  31.3 us
    pallas_call x9, Pallas kernels, call(): pl.pallas_call(body, out_shape=tuple(shapes), in_specs=[SPECS[at] for at...  22.9 us
    all_to_all x1, blocking collectives, shards(): column = lax.all_to_all(column, 'zh', 0, 0, tiled=True)  20.1 us
    all_to_all x1, blocking collectives, shards(): every = lax.all_to_all(fore, MEMBER, 0, 0, tiled=True)  16.8 us
    ppermute x1, waiting for transfers between devices, shards(): across = lax.ppermute(across, GRID, outer)  15.1 us
    all_to_all x1, blocking collectives, shards(): plane = lax.all_to_all(wg, PLANE, 0, 0, tiled=True)  13 us
    all_to_all x1, starting transfers between devices, shards(): lax.all_to_all(spread.reshape(members * zh_n, *wg.shape[2:]), COLUMN, 0,...  11.7 us
    ppermute x1, starting transfers between devices, shards(): lax.ppermute(jnp.where(even, inputs[:HALO], inputs[PTS - HALO:]), GRID, o...  8.18 us
  transfers between devices with their start and end apart: 6, of which 3 were waited for; matrix products, arithmetic and copies ran while one was open for 0% of the time, Pallas kernels for 8%

profile of v8, /device:TPU:225, one launch (start us, length us, event | category | flops | bytes accessed | tf_op | source)
XLA Modules:
  0.0 156.6 jit_solution(15396529930222657882)
XLA Ops:
  0.6 0.8 shard_map.121
  1.4 20.1 %all_to_all.30 = bf16[4,136,128]{2,1,0:T(8,128)(2,1)S(1)} all-to-all(bf16[4,136,128]{2,1,0:T(8,128)(2,1)S(1)} %shard_map.121), channel_id=1, replica_groups=mesh['zl'=4,'core'=2,'zh'=4,'y'=4,'x'=4] {'zh'}, dimensions={0} | all-to-all | bytes 278528 | tf_op jit(solution)/shard_map/all_to_all | solution.py:451
  21.6 11.4 %all_to_all.31 = bf16[4,4,136,128]{3,2,1,0:T(8,128)(2,1)S(1)} all-to-all(bf16[4,4,136,128]{3,2,1,0:T(8,128)(2,1)S(1)} %broadcast_in_dim.8), channel_id=1, replica_groups={{0,1,2,3},{4,5,6,7},{8,9,10,11},{12,13,14,15},{64,68,72,76},{65,69,73,7..., dimensions={0} | all-to-all | bytes 1114112 | tf_op jit(solution)/shard_map/all_to_all | solution.py:476
  33.3 19.9 %all_to_all.32 = bf16[4,4,4,136,128]{4,3,2,1,0:T(8,128)(2,1)S(1)} all-to-all(bf16[4,4,4,136,128]{4,3,2,1,0:T(8,128)(2,1)S(1)} %broadcast_in_dim.9), channel_id=1, replica_groups={{0,4,8,12},{1,5,9,13},{2,6,10,14},{3,7,11,15},{64,65,66,67},{68,69,70,7..., dimensions={0} | all-to-all | bytes 4456448 | tf_op jit(solution)/shard_map/all_to_all | solution.py:476
  53.2 5.8 %collective-permute-start.2 = (bf16[16,4,136,128]{3,2,1,0:T(8,128)(2,1)S(1)}, bf16[16,4,136,128]{3,2,1,0:T(8,128)(2,1)}, u32[]{:S(2)}, u32[]{:S(2)}) collective-permute-start(bf16[16,4,136,128]{3,2,1,0:T(8,128)(2,1)S(1)} %bitcast.10), channel_id=1, source_target_pairs={{0,64},{64,0},{1,65},{65,1},{2,66},{66,2},{3,67},{67,3},{4,68},{68... | collective-permute-start | bytes 6684680 | tf_op jit(solution)/shard_map/ppermute | solution.py:487
  59.0 8.2 %collective-permute-start.1 = (bf16[32,1024]{1,0:T(8,128)(2,1)S(1)}, bf16[32,1024]{1,0:T(8,128)(2,1)S(1)}, u32[]{:S(2)}, u32[]{:S(2)}) collective-permute-start(bf16[32,1024]{1,0:T(8,128)(2,1)S(1)} %get-tuple-element.56), channel_id=1, source_target_pairs={{1,2},{2,1},{3,4},{4,3},{5,6},{6,5},{7,8},{8,7},{9,10},{10,9},{11,... | collective-permute-start | bytes 196616 | tf_op jit(solution)/shard_map/ppermute | solution.py:456
  67.2 1.9 %collective-permute-start = (bf16[32,1024]{1,0:T(8,128)(2,1)S(1)}, bf16[32,1024]{1,0:T(8,128)(2,1)S(1)}, u32[]{:S(2)}, u32[]{:S(2)}) collective-permute-start(bf16[32,1024]{1,0:T(8,128)(2,1)S(1)} %get-tuple-element.57), channel_id=1, source_target_pairs={{0,1},{1,0},{2,3},{3,2},{4,5},{5,4},{6,7},{7,6},{8,9},{9,8},{10,11... | collective-permute-start | bytes 196616 | tf_op jit(solution)/shard_map/ppermute | solution.py:453
  69.9 2.0 %shard_map.120 = (bf16[128,1024]{1,0:T(8,128)(2,1)}, f32[128,192]{1,0:T(8,128)}) custom-call(bf16[128,1024]{1,0:T(8,128)(2,1)} %bitcast.13, f32[1,1024]{1,0:T(1,128)} %bitcast.17, s32[128,8]{1,0:T(8,128)} %broadcast_subtract_fusion.rel), custom_call_target="tpu_custom_call" | custom-call | flops 4000000 | bytes 1000000 | tf_op jit(solution)/shard_map/pallas_call | solution.py:64
  71.9 0.8 collective-permute-done.1.across
  72.7 1.7 %shard_map.122 = (bf16[32,1024]{1,0:T(8,128)(2,1)S(1)}, bf16[32,1024]{1,0:T(8,128)(2,1)S(1)}, bf16[192,768]{1,0:T(8,128)(2,1)S(1)}) custom-call(bf16[32,1024]{1,0:T(8,128)(2,1)S(1)} %collective-permute-done.inside, bf16[32,1024]{1,0:T(8,128)(2,1)S(1)} %collective-permute-done.1.across, f32[1,1024]{1,0:T(1,128)} %bitcast.18, ...), custom_call_target="tpu_custom_call" | custom-call | flops 300000000 | bytes 4000000 | tf_op jit(solution)/shard_map/pallas_call | solution.py:64
  74.4 6.5 %shard_map.123 = (bf16[2,16,4,96,128]{4,3,2,1,0:T(8,128)(2,1)}, bf16[2,16,4,32,128]{4,3,2,1,0:T(8,128)(2,1)}, bf16[128,512]{1,0:T(8,128)(2,1)}, bf16[192,1024]{1...) custom-call(bf16[32,1024]{1,0:T(8,128)(2,1)S(1)} %get-tuple-element., ...), custom_call_target="tpu_custom_call" | custom-call | flops 2000000000 | bytes 10000000 | tf_op jit(solution)/shard_map/pallas_call | solution.py:64
  80.9 16.8 %all_to_all.33.every = bf16[8,128,128]{2,1,0:T(8,128)(2,1)S(1)} all-to-all(bf16[8,128,128]{2,1,0:T(8,128)(2,1)S(1)} %get-tuple-element.35), channel_id=1, replica_groups=mesh['zl'=4,'core'=2,'zh'=4,'y'=4,'x'=4] {'zl','core'}, dimensions={0} | all-to-all | bytes 524288 | tf_op jit(solution)/shard_map/all_to_all | solution.py:521
  97.7 1.2 shard_map.124
  98.9 13.0 %all_to_all.34.parts = bf16[16,4,24,128]{3,2,1,0:T(8,128)(2,1)S(1)} all-to-all(bf16[16,4,24,128]{3,2,1,0:T(8,128)(2,1)} %get-tuple-element.51), channel_id=1, replica_groups=mesh['zl'=4,'core'=2,'zh'=4,'y'=4,'x'=4] {'y','x'}, dimensions={0} | all-to-all | bytes 786432 | tf_op jit(solution)/shard_map/all_to_all | solution.py:533
  111.9 0.7 shard_map.127
  112.6 11.7 %all-to-all-start.5 = ((bf16[32,24,128]{2,1,0:T(8,128)(2,1)}), bf16[32,24,128]{2,1,0:T(8,128)(2,1)S(1)}, u32[]{:S(2)}, u32[]{:S(2)}) async-start(bf16[32,24,128]{2,1,0:T(8,128)(2,1)} %bitcast.16), calls=%async_computation.5 | async-start | bytes 393216 | tf_op jit(solution)/shard_map/all_to_all | solution.py:562
  124.3 5.4 %shard_map.125 = (bf16[128,512]{1,0:T(8,128)(2,1)}, f32[128,1024]{1,0:T(8,128)}, bf16[32,1024]{1,0:T(8,128)(2,1)}, bf16[32,1024]{1,0:T(8,128)(2,1)}) custom-call(bf16[128,128]{1,0:T(8,128)(2,1)} %get-tuple-element.39.gf_in.gf, bf16[1024,128]{1,0:T(8,128)(2,1)} %get-tuple-element.40.whead_in.whead, bf16[2,16,4,32,128]{4,3,2,1,0:T(8,128)(2,1)} %get-tuple-element.42.raw_in, ...), custom_call_target="tpu_custom_call" | custom-call | flops 1000000000 | bytes 4000000 | tf_op jit(solution)/shard_map/pallas_call | solution.py:64
  129.7 2.2 %collective-permute-start.3 = (bf16[32,1024]{1,0:T(8,128)(2,1)}, bf16[32,1024]{1,0:T(8,128)(2,1)S(1)}, u32[]{:S(2)}, u32[]{:S(2)}) collective-permute-start(bf16[32,1024]{1,0:T(8,128)(2,1)} %get-tuple-element.48), channel_id=1, source_target_pairs={{0,1},{1,0},{2,3},{3,2},{4,5},{5,4},{6,7},{7,6},{8,9},{9,8},{10,11... | collective-permute-start | bytes 196616 | tf_op jit(solution)/shard_map/ppermute | solution.py:552
  131.9 3.0 %collective-permute-start.4 = (bf16[32,1024]{1,0:T(8,128)(2,1)}, bf16[32,1024]{1,0:T(8,128)(2,1)S(1)}, u32[]{:S(2)}, u32[]{:S(2)}) collective-permute-start(bf16[32,1024]{1,0:T(8,128)(2,1)} %get-tuple-element.49), channel_id=1, source_target_pairs={{1,2},{2,1},{3,4},{4,3},{5,6},{6,5},{7,8},{8,7},{9,10},{10,9},{11,... | collective-permute-start | bytes 196616 | tf_op jit(solution)/shard_map/ppermute | solution.py:553
  135.3 15.1 %collective-permute-done.4.across = bf16[32,1024]{1,0:T(8,128)(2,1)S(1)} collective-permute-done((bf16[32,1024]{1,0:T(8,128)(2,1)}, bf16[32,1024]{1,0:T(8,128)(2,1)S(1)}, u32[]{:S(2)}, u32[]{:S(2)}) %collective-permute-start.4) | collective-permute-done | bytes 65568 | tf_op jit(solution)/shard_map/ppermute | solution.py:553
  150.3 3.7 %shard_map.126 = (f32[128,1024]{1,0:T(8,128)}, bf16[128,1024]{1,0:T(8,128)(2,1)}, bf16[1024,128]{1,0:T(8,128)(2,1)S(1)}) custom-call(bf16[128,1024]{1,0:T(8,128)(2,1)} %bitcast.15, f32[1,1024]{1,0:T(1,128)} %bitcast.19, bf16[128,128]{1,0:T(8,128)(2,1)} %get-tuple-element.39.gf_in.gf, bf16[1024,128]{1,0:T(8,128)(2,1)} %get-tuple-element.40.whead_in.whead, ...), custom_call_target="tpu_custom_call" | custom-call | flops 1000000000 | bytes 4000000 | tf_op jit(solution)/shard_map/pallas_call | solution.py:64
  154.1 0.7 copy-done.1
  154.8 0.9 copy-done.2
  155.7 0.9 shard_map.128
  (19 shorter events, 1.4 us)
Async XLA Ops:
  33.3 25.7 %copy-start.4 = (bf16[1,128,1024]{2,1,0:T(8,128)(2,1)S(1)}, bf16[1,128,1024]{2,1,0:T(8,128)(2,1)}, u32[]{:S(2)}) copy-start(bf16[1,128,1024]{2,1,0:T(8,128)(2,1)} %param.9) | copy-start | bytes 786436
  33.3 35.9 %copy-start.5 = (s32[128,8]{0,1:T(8,128)S(1)}, s32[128,8]{0,1:T(8,128)}, u32[]{:S(2)}) copy-start(s32[128,8]{0,1:T(8,128)} %param.16) | copy-start | bytes 12292
  53.2 21.2 %collective-permute-start.2 = (bf16[16,4,136,128]{3,2,1,0:T(8,128)(2,1)S(1)}, bf16[16,4,136,128]{3,2,1,0:T(8,128)(2,1)}, u32[]{:S(2)}, u32[]{:S(2)}) collective-permute-start(bf16[16,4,136,128]{3,2,1,0:T(8,128)(2,1)S(1)} %bitcast.10), channel_id=1, source_target_pairs={{0,64},{64,0},{1,65},{65,1},{2,66},{66,2},{3,67},{67,3},{4,68},{68... | collective-permute-start | bytes 6684680 | tf_op jit(solution)/shard_map/ppermute | solution.py:487
  59.0 13.7 %collective-permute-start.1 = (bf16[32,1024]{1,0:T(8,128)(2,1)S(1)}, bf16[32,1024]{1,0:T(8,128)(2,1)S(1)}, u32[]{:S(2)}, u32[]{:S(2)}) collective-permute-start(bf16[32,1024]{1,0:T(8,128)(2,1)S(1)} %get-tuple-element.56), channel_id=1, source_target_pairs={{1,2},{2,1},{3,4},{4,3},{5,6},{6,5},{7,8},{8,7},{9,10},{10,9},{11,... | collective-permute-start | bytes 196616 | tf_op jit(solution)/shard_map/ppermute | solution.py:456
  67.2 5.5 %collective-permute-start = (bf16[32,1024]{1,0:T(8,128)(2,1)S(1)}, bf16[32,1024]{1,0:T(8,128)(2,1)S(1)}, u32[]{:S(2)}, u32[]{:S(2)}) collective-permute-start(bf16[32,1024]{1,0:T(8,128)(2,1)S(1)} %get-tuple-element.57), channel_id=1, source_target_pairs={{0,1},{1,0},{2,3},{3,2},{4,5},{5,4},{6,7},{7,6},{8,9},{9,8},{10,11... | collective-permute-start | bytes 196616 | tf_op jit(solution)/shard_map/ppermute | solution.py:453
  74.4 23.4 %copy-start.3 = (f32[128,128]{1,0:T(8,128)S(1)}, f32[128,128]{1,0:T(8,128)}, u32[]{:S(2)}) copy-start(f32[128,128]{1,0:T(8,128)} %observed.1) | copy-start | bytes 196612
  111.9 38.4 %copy-start = (bf16[2,16,4,96,128]{4,3,2,1,0:T(8,128)(2,1)S(1)}, bf16[2,16,4,96,128]{4,3,2,1,0:T(8,128)(2,1)}, u32[]{:S(2)}) copy-start(bf16[2,16,4,96,128]{4,3,2,1,0:T(8,128)(2,1)} %get-tuple-element.41.raw) | copy-start | bytes 9437188
  112.6 42.1 %all-to-all-start.5 = ((bf16[32,24,128]{2,1,0:T(8,128)(2,1)}), bf16[32,24,128]{2,1,0:T(8,128)(2,1)S(1)}, u32[]{:S(2)}, u32[]{:S(2)}) async-start(bf16[32,24,128]{2,1,0:T(8,128)(2,1)} %bitcast.16), calls=%async_computation.5 | async-start | bytes 393216 | tf_op jit(solution)/shard_map/all_to_all | solution.py:562
  129.7 5.5 %collective-permute-start.3 = (bf16[32,1024]{1,0:T(8,128)(2,1)}, bf16[32,1024]{1,0:T(8,128)(2,1)S(1)}, u32[]{:S(2)}, u32[]{:S(2)}) collective-permute-start(bf16[32,1024]{1,0:T(8,128)(2,1)} %get-tuple-element.48), channel_id=1, source_target_pairs={{0,1},{1,0},{2,3},{3,2},{4,5},{5,4},{6,7},{7,6},{8,9},{9,8},{10,11... | collective-permute-start | bytes 196616 | tf_op jit(solution)/shard_map/ppermute | solution.py:552
  131.9 18.4 %collective-permute-start.4 = (bf16[32,1024]{1,0:T(8,128)(2,1)}, bf16[32,1024]{1,0:T(8,128)(2,1)S(1)}, u32[]{:S(2)}, u32[]{:S(2)}) collective-permute-start(bf16[32,1024]{1,0:T(8,128)(2,1)} %get-tuple-element.49), channel_id=1, source_target_pairs={{1,2},{2,1},{3,4},{4,3},{5,6},{6,5},{7,8},{8,7},{9,10},{10,9},{11,... | collective-permute-start | bytes 196616 | tf_op jit(solution)/shard_map/ppermute | solution.py:553
  154.1 0.7 copy-start.1
  154.8 1.0 copy-start.2

commit v9 on v7

--- a/solution.py
+++ b/solution.py
@@ -417,14 +417,17 @@
         spread[i] = total
 
 
-def weights_body(scaling, parts, whead, mixing, head):
-    flat_head = whead[...]
+def weights_body(scaling, parts, whead_in, mixing, head, whead, sems):
+    (arriving,) = fetched(((whead_in, whead),), sems)
+    arriving.start()
     rb = head.shape[0]
     total = added(parts) * scaling
     head[...] = total[:rb]
     factor = total[rb:]
     high = factor.astype(BF)
     low = (factor - high.astype(F32)).astype(BF)
+    arriving.wait()
+    flat_head = whead[...]
     mixing[...] = nt(high, flat_head) + nt(low, flat_head)
 
 
@@ -588,7 +591,8 @@
         functools.partial(weights_body, scaling),
         [((HD // devices, D), F32), ((D // devices, NVAR), F32)],
         (parts, whead),
-        "VA>AA",
+        "VH>AA",
+        scratch=(pltpu.VMEM((D, NVAR), BF), pltpu.SemaphoreType.DMA((1,))),
         cost=(1e8, 1e6),
         limit=8,
     )

time: 172 us -> 172 us (level)
  no operation moved by 1% of the time
where the time goes in v9:
time: 172 us; the launch traced here: 171 us
  blocking collectives  102 us (59%)
  Pallas kernels  24.4 us (14%)
  starting transfers between devices  23.4 us (14%)
  waiting for transfers between devices  19.2 us (11%)
    all_to_all x2, blocking collectives, widened(): lax.all_to_all(jnp.broadcast_to(block[None], (n, *block.shape)), ('core',...  30.5 us
    all_to_all x1, blocking collectives, shards(): column = lax.all_to_all(column, 'zh', 0, 0, tiled=True)  29.9 us
    pallas_call x10, Pallas kernels, call(): pl.pallas_call(body, out_shape=tuple(shapes), in_specs=[SPECS[at] for at...  24.4 us
    all_to_all x1, blocking collectives, shards(): column = lax.all_to_all(partial, 'zh', 0, 0, tiled=True)  17.5 us
    ppermute x1, waiting for transfers between devices, shards(): across = lax.ppermute(across, GRID, outer)  12.8 us
    all_to_all x1, blocking collectives, shards(): plane = lax.all_to_all(wg, PLANE, 0, 0, tiled=True)  12.3 us
    all_to_all x1, blocking collectives, shards(): every = lax.all_to_all(fore, MEMBER, 0, 0, tiled=True)  12.1 us
    ppermute x1, starting transfers between devices, shards(): lax.ppermute(jnp.where(even, inputs[:HALO], inputs[PTS - HALO:]), GRID, o...  7.71 us
  transfers between devices with their start and end apart: 6, of which 2 were waited for; matrix products, arithmetic and copies ran while one was open for 0% of the time, Pallas kernels for 7%

profile of v9, /device:TPU:30, one launch (start us, length us, event | category | flops | bytes accessed | tf_op | source)
XLA Modules:
  0.0 171.3 jit_solution(13441875058087231082)
XLA Ops:
  0.6 0.8 shard_map.121
  1.4 29.9 %all_to_all.35 = bf16[4,136,128]{2,1,0:T(8,128)(2,1)S(1)} all-to-all(bf16[4,136,128]{2,1,0:T(8,128)(2,1)S(1)} %shard_map.121), channel_id=1, replica_groups=mesh['zl'=4,'core'=2,'zh'=4,'y'=4,'x'=4] {'zh'}, dimensions={0} | all-to-all | bytes 278528 | tf_op jit(solution)/shard_map/all_to_all | solution.py:456
  31.4 10.8 %all_to_all.36 = bf16[4,4,136,128]{3,2,1,0:T(8,128)(2,1)S(1)} all-to-all(bf16[4,4,136,128]{3,2,1,0:T(8,128)(2,1)S(1)} %broadcast_in_dim.8), channel_id=1, replica_groups={{0,1,2,3},{4,5,6,7},{8,9,10,11},{12,13,14,15},{64,68,72,76},{65,69,73,7..., dimensions={0} | all-to-all | bytes 1114112 | tf_op jit(solution)/shard_map/all_to_all | solution.py:481
  42.5 19.8 %all_to_all.37 = bf16[4,4,4,136,128]{4,3,2,1,0:T(8,128)(2,1)S(1)} all-to-all(bf16[4,4,4,136,128]{4,3,2,1,0:T(8,128)(2,1)S(1)} %broadcast_in_dim.9), channel_id=1, replica_groups={{0,4,8,12},{1,5,9,13},{2,6,10,14},{3,7,11,15},{64,65,66,67},{68,69,70,7..., dimensions={0} | all-to-all | bytes 4456448 | tf_op jit(solution)/shard_map/all_to_all | solution.py:481
  62.3 1.9 %collective-permute-start.2 = (bf16[16,4,136,128]{3,2,1,0:T(8,128)(2,1)S(1)}, bf16[16,4,136,128]{3,2,1,0:T(8,128)(2,1)}, u32[]{:S(2)}, u32[]{:S(2)}) collective-permute-start(bf16[16,4,136,128]{3,2,1,0:T(8,128)(2,1)S(1)} %bitcast.9), channel_id=1, source_target_pairs={{0,64},{64,0},{1,65},{65,1},{2,66},{66,2},{3,67},{67,3},{4,68},{68... | collective-permute-start | bytes 6684680 | tf_op jit(solution)/shard_map/ppermute | solution.py:492
  64.2 7.7 %collective-permute-start.1 = (bf16[32,1024]{1,0:T(8,128)(2,1)S(1)}, bf16[32,1024]{1,0:T(8,128)(2,1)S(1)}, u32[]{:S(2)}, u32[]{:S(2)}) collective-permute-start(bf16[32,1024]{1,0:T(8,128)(2,1)S(1)} %get-tuple-element.54), channel_id=1, source_target_pairs={{1,2},{2,1},{3,4},{4,3},{5,6},{6,5},{7,8},{8,7},{9,10},{10,9},{11,... | collective-permute-start | bytes 196616 | tf_op jit(solution)/shard_map/ppermute | solution.py:461
  71.9 1.9 %collective-permute-start = (bf16[32,1024]{1,0:T(8,128)(2,1)S(1)}, bf16[32,1024]{1,0:T(8,128)(2,1)S(1)}, u32[]{:S(2)}, u32[]{:S(2)}) collective-permute-start(bf16[32,1024]{1,0:T(8,128)(2,1)S(1)} %get-tuple-element.55), channel_id=1, source_target_pairs={{0,1},{1,0},{2,3},{3,2},{4,5},{5,4},{6,7},{7,6},{8,9},{9,8},{10,11... | collective-permute-start | bytes 196616 | tf_op jit(solution)/shard_map/ppermute | solution.py:458
  74.0 0.6 broadcast_subtract_fusion.rel
  74.6 2.0 %shard_map.120 = (bf16[128,1024]{1,0:T(8,128)(2,1)}, f32[128,192]{1,0:T(8,128)}) custom-call(bf16[128,1024]{1,0:T(8,128)(2,1)} %bitcast.12, f32[1,1024]{1,0:T(1,128)} %bitcast.15, s32[128,8]{1,0:T(8,128)} %broadcast_subtract_fusion.rel), custom_call_target="tpu_custom_call" | custom-call | flops 4000000 | bytes 1000000 | tf_op jit(solution)/shard_map/pallas_call | solution.py:63
  76.6 6.3 %collective-permute-done.1.across = bf16[32,1024]{1,0:T(8,128)(2,1)S(1)} collective-permute-done((bf16[32,1024]{1,0:T(8,128)(2,1)S(1)}, bf16[32,1024]{1,0:T(8,128)(2,1)S(1)}, u32[]{:S(2)}, u32[]{:S(2)}) %collective-permute-start.1) | collective-permute-done | bytes 65568 | tf_op jit(solution)/shard_map/ppermute | solution.py:461
  82.9 1.7 shard_map.122
  84.7 6.5 %shard_map.123 = (bf16[2,16,4,96,128]{4,3,2,1,0:T(8,128)(2,1)}, bf16[2,16,4,32,128]{4,3,2,1,0:T(8,128)(2,1)}, bf16[128,512]{1,0:T(8,128)(2,1)}, bf16[192,1024]{1...) custom-call(bf16[32,1024]{1,0:T(8,128)(2,1)S(1)} %get-tuple-element., ...), custom_call_target="tpu_custom_call" | custom-call | flops 2000000000 | bytes 10000000 | tf_op jit(solution)/shard_map/pallas_call | solution.py:63
  91.2 12.1 %all_to_all.38.every = bf16[8,128,128]{2,1,0:T(8,128)(2,1)S(1)} all-to-all(bf16[8,128,128]{2,1,0:T(8,128)(2,1)S(1)} %get-tuple-element.34), channel_id=1, replica_groups=mesh['zl'=4,'core'=2,'zh'=4,'y'=4,'x'=4] {'zl','core'}, dimensions={0} | all-to-all | bytes 524288 | tf_op jit(solution)/shard_map/all_to_all | solution.py:526
  103.3 1.2 shard_map.124
  104.5 12.3 %all_to_all.39.parts = bf16[16,4,24,128]{3,2,1,0:T(8,128)(2,1)S(1)} all-to-all(bf16[16,4,24,128]{3,2,1,0:T(8,128)(2,1)} %get-tuple-element.50), channel_id=1, replica_groups=mesh['zl'=4,'core'=2,'zh'=4,'y'=4,'x'=4] {'y','x'}, dimensions={0} | all-to-all | bytes 786432 | tf_op jit(solution)/shard_map/all_to_all | solution.py:538
  116.8 0.7 shard_map.127
  117.4 17.5 %all_to_all.40.parts = bf16[4,24,128]{2,1,0:T(8,128)(2,1)S(1)} all-to-all(bf16[4,24,128]{2,1,0:T(8,128)(2,1)} %shard_map.127), channel_id=1, replica_groups=mesh['zl'=4,'core'=2,'zh'=4,'y'=4,'x'=4] {'zh'}, dimensions={0} | all-to-all | bytes 49152 | tf_op jit(solution)/shard_map/all_to_all | solution.py:567
  135.5 3.3 %all-to-all-start.6 = ((bf16[8,24,128]{2,1,0:T(8,128)(2,1)}), bf16[8,24,128]{2,1,0:T(8,128)(2,1)S(1)}, u32[]{:S(2)}, u32[]{:S(2)}) async-start(bf16[8,24,128]{2,1,0:T(8,128)(2,1)} %shard_map.128), calls=%async_computation.6 | async-start | bytes 98304 | tf_op jit(solution)/shard_map/all_to_all | solution.py:576
  138.9 5.4 %shard_map.125 = (bf16[128,512]{1,0:T(8,128)(2,1)}, f32[128,1024]{1,0:T(8,128)}, bf16[32,1024]{1,0:T(8,128)(2,1)}, bf16[32,1024]{1,0:T(8,128)(2,1)}) custom-call(bf16[128,128]{1,0:T(8,128)(2,1)} %get-tuple-element.38.gf_in.gf, bf16[1024,128]{1,0:T(8,128)(2,1)} %get-tuple-element.39.whead_in.whead, bf16[2,16,4,32,128]{4,3,2,1,0:T(8,128)(2,1)} %get-tuple-element.41.raw_in, ...), custom_call_target="tpu_custom_call" | custom-call | flops 1000000000 | bytes 4000000 | tf_op jit(solution)/shard_map/pallas_call | solution.py:63
  144.3 2.7 %collective-permute-start.3 = (bf16[32,1024]{1,0:T(8,128)(2,1)}, bf16[32,1024]{1,0:T(8,128)(2,1)S(1)}, u32[]{:S(2)}, u32[]{:S(2)}) collective-permute-start(bf16[32,1024]{1,0:T(8,128)(2,1)} %get-tuple-element.47), channel_id=1, source_target_pairs={{0,1},{1,0},{2,3},{3,2},{4,5},{5,4},{6,7},{7,6},{8,9},{9,8},{10,11... | collective-permute-start | bytes 196616 | tf_op jit(solution)/shard_map/ppermute | solution.py:557
  147.0 5.9 %collective-permute-start.4 = (bf16[32,1024]{1,0:T(8,128)(2,1)}, bf16[32,1024]{1,0:T(8,128)(2,1)S(1)}, u32[]{:S(2)}, u32[]{:S(2)}) collective-permute-start(bf16[32,1024]{1,0:T(8,128)(2,1)} %get-tuple-element.48), channel_id=1, source_target_pairs={{1,2},{2,1},{3,4},{4,3},{5,6},{6,5},{7,8},{8,7},{9,10},{10,9},{11,... | collective-permute-start | bytes 196616 | tf_op jit(solution)/shard_map/ppermute | solution.py:558
  152.9 12.8 %collective-permute-done.4.across = bf16[32,1024]{1,0:T(8,128)(2,1)S(1)} collective-permute-done((bf16[32,1024]{1,0:T(8,128)(2,1)}, bf16[32,1024]{1,0:T(8,128)(2,1)S(1)}, u32[]{:S(2)}, u32[]{:S(2)}) %collective-permute-start.4) | collective-permute-done | bytes 65568 | tf_op jit(solution)/shard_map/ppermute | solution.py:558
  165.7 3.7 %shard_map.126 = (f32[128,1024]{1,0:T(8,128)}, bf16[128,1024]{1,0:T(8,128)(2,1)}) custom-call(bf16[128,1024]{1,0:T(8,128)(2,1)} %bitcast.14, f32[1,1024]{1,0:T(1,128)} %bitcast.17, bf16[128,128]{1,0:T(8,128)(2,1)} %get-tuple-element.38.gf_in.gf, bf16[1024,128]{1,0:T(8,128)(2,1)} %get-tuple-element.39.whead_in.whead, ...), custom_call_target="tpu_custom_call" | custom-call | flops 1000000000 | bytes 4000000 | tf_op jit(solution)/shard_map/pallas_call | solution.py:63
  169.5 1.8 %shard_map.129 = (f32[8,1024]{1,0:T(8,128)}, f32[16,128]{1,0:T(8,128)}) custom-call(bf16[8,24,128]{2,1,0:T(8,128)(2,1)S(1)} %all-to-all-done.6.parts, bf16[1024,128]{1,0:T(8,128)(2,1)} %get-tuple-element.39.whead_in.whead), custom_call_target="tpu_custom_call" | custom-call | flops 100000000 | bytes 1000000 | tf_op jit(solution)/shard_map/pallas_call | solution.py:63
  (17 shorter events, 1.1 us)
Async XLA Ops:
  42.5 21.7 %copy-start.2 = (bf16[1,128,1024]{2,1,0:T(8,128)(2,1)S(1)}, bf16[1,128,1024]{2,1,0:T(8,128)(2,1)}, u32[]{:S(2)}) copy-start(bf16[1,128,1024]{2,1,0:T(8,128)(2,1)} %param.9) | copy-start | bytes 786436
  42.5 31.4 %copy-start.3 = (s32[128,8]{0,1:T(8,128)S(1)}, s32[128,8]{0,1:T(8,128)}, u32[]{:S(2)}) copy-start(s32[128,8]{0,1:T(8,128)} %param.16) | copy-start | bytes 12292
  62.3 22.4 %collective-permute-start.2 = (bf16[16,4,136,128]{3,2,1,0:T(8,128)(2,1)S(1)}, bf16[16,4,136,128]{3,2,1,0:T(8,128)(2,1)}, u32[]{:S(2)}, u32[]{:S(2)}) collective-permute-start(bf16[16,4,136,128]{3,2,1,0:T(8,128)(2,1)S(1)} %bitcast.9), channel_id=1, source_target_pairs={{0,64},{64,0},{1,65},{65,1},{2,66},{66,2},{3,67},{67,3},{4,68},{68... | collective-permute-start | bytes 6684680 | tf_op jit(solution)/shard_map/ppermute | solution.py:492
  64.2 18.7 %collective-permute-start.1 = (bf16[32,1024]{1,0:T(8,128)(2,1)S(1)}, bf16[32,1024]{1,0:T(8,128)(2,1)S(1)}, u32[]{:S(2)}, u32[]{:S(2)}) collective-permute-start(bf16[32,1024]{1,0:T(8,128)(2,1)S(1)} %get-tuple-element.54), channel_id=1, source_target_pairs={{1,2},{2,1},{3,4},{4,3},{5,6},{6,5},{7,8},{8,7},{9,10},{10,9},{11,... | collective-permute-start | bytes 196616 | tf_op jit(solution)/shard_map/ppermute | solution.py:461
  71.9 11.0 %collective-permute-start = (bf16[32,1024]{1,0:T(8,128)(2,1)S(1)}, bf16[32,1024]{1,0:T(8,128)(2,1)S(1)}, u32[]{:S(2)}, u32[]{:S(2)}) collective-permute-start(bf16[32,1024]{1,0:T(8,128)(2,1)S(1)} %get-tuple-element.55), channel_id=1, source_target_pairs={{0,1},{1,0},{2,3},{3,2},{4,5},{5,4},{6,7},{7,6},{8,9},{9,8},{10,11... | collective-permute-start | bytes 196616 | tf_op jit(solution)/shard_map/ppermute | solution.py:458
  84.7 18.7 %copy-start.1 = (f32[128,128]{1,0:T(8,128)S(1)}, f32[128,128]{1,0:T(8,128)}, u32[]{:S(2)}) copy-start(f32[128,128]{1,0:T(8,128)} %observed.1) | copy-start | bytes 196612
  116.8 49.0 %copy-start = (bf16[2,16,4,96,128]{4,3,2,1,0:T(8,128)(2,1)S(1)}, bf16[2,16,4,96,128]{4,3,2,1,0:T(8,128)(2,1)}, u32[]{:S(2)}) copy-start(bf16[2,16,4,96,128]{4,3,2,1,0:T(8,128)(2,1)} %get-tuple-element.40.raw) | copy-start | bytes 9437188
  135.5 33.9 %all-to-all-start.6 = ((bf16[8,24,128]{2,1,0:T(8,128)(2,1)}), bf16[8,24,128]{2,1,0:T(8,128)(2,1)S(1)}, u32[]{:S(2)}, u32[]{:S(2)}) async-start(bf16[8,24,128]{2,1,0:T(8,128)(2,1)} %shard_map.128), calls=%async_computation.6 | async-start | bytes 98304 | tf_op jit(solution)/shard_map/all_to_all | solution.py:576
  144.3 8.6 %collective-permute-start.3 = (bf16[32,1024]{1,0:T(8,128)(2,1)}, bf16[32,1024]{1,0:T(8,128)(2,1)S(1)}, u32[]{:S(2)}, u32[]{:S(2)}) collective-permute-start(bf16[32,1024]{1,0:T(8,128)(2,1)} %get-tuple-element.47), channel_id=1, source_target_pairs={{0,1},{1,0},{2,3},{3,2},{4,5},{5,4},{6,7},{7,6},{8,9},{9,8},{10,11... | collective-permute-start | bytes 196616 | tf_op jit(solution)/shard_map/ppermute | solution.py:557
  147.0 18.7 %collective-permute-start.4 = (bf16[32,1024]{1,0:T(8,128)(2,1)}, bf16[32,1024]{1,0:T(8,128)(2,1)S(1)}, u32[]{:S(2)}, u32[]{:S(2)}) collective-permute-start(bf16[32,1024]{1,0:T(8,128)(2,1)} %get-tuple-element.48), channel_id=1, source_target_pairs={{1,2},{2,1},{3,4},{4,3},{5,6},{6,5},{7,8},{8,7},{9,10},{10,9},{11,... | collective-permute-start | bytes 196616 | tf_op jit(solution)/shard_map/ppermute | solution.py:558

commit v10 on v9

--- a/solution.py
+++ b/solution.py
@@ -467,7 +467,7 @@
         taps_body,
         [((PTS, D), BF), ((PTS, EXT), F32)],
         (inputs, scale, rel),
-        "AAA>AA",
+        "VAA>VV",
         cost=(4e6, 1e6),
         limit=8,
     )
@@ -494,7 +494,7 @@
         functools.partial(early_body, ny, nx, rs),
         [((HALO, D), BF), ((HALO, D), BF), ((EXT, 6 * LANE), BF)],
         (inside, across, scale, normed, own),
-        "VVAAV>VVV",
+        "VVAVV>VVV",
         cost=(3e8, 4e6),
         limit=8,
     )
@@ -513,7 +513,7 @@
             ((PTS, NVAR), F32),
         ],
         (ahead, normed, behind, part, inputs, count, own, other),
-        "VAVVAAVV>HHHHHAVVVV",
+        "VVVVVVVV>HHHHHAVVVV",
         scratch=(
             pltpu.VMEM((EXT, 3 * HD), BF),
             pltpu.VMEM((HEADS, PTS, EXT), BF),

time: 172 us -> 172 us (level)
  no operation moved by 1% of the time
where the time goes in v10:
time: 172 us; the launch traced here: 171 us
  blocking collectives  102 us (59%)
  starting transfers between devices  23.5 us (14%)
  Pallas kernels  23.2 us (13%)
  waiting for transfers between devices  20 us (12%)
    all_to_all x2, blocking collectives, widened(): lax.all_to_all(jnp.broadcast_to(block[None], (n, *block.shape)), ('core',...  30.5 us
    all_to_all x1, blocking collectives, shards(): column = lax.all_to_all(column, 'zh', 0, 0, tiled=True)  29.9 us
    pallas_call x10, Pallas kernels, call(): pl.pallas_call(body, out_shape=tuple(shapes), in_specs=[SPECS[at] for at...  23.2 us
    all_to_all x1, blocking collectives, shards(): column = lax.all_to_all(partial, 'zh', 0, 0, tiled=True)  17.5 us
    ppermute x1, waiting for transfers between devices, shards(): across = lax.ppermute(across, GRID, outer)  12.8 us
    all_to_all x1, blocking collectives, shards(): plane = lax.all_to_all(wg, PLANE, 0, 0, tiled=True)  12.3 us
    all_to_all x1, blocking collectives, shards(): every = lax.all_to_all(fore, MEMBER, 0, 0, tiled=True)  12.1 us
    ppermute x1, starting transfers between devices, shards(): lax.ppermute(jnp.where(even, inputs[:HALO], inputs[PTS - HALO:]), GRID, o...  7.71 us
  transfers between devices with their start and end apart: 6, of which 2 were waited for; matrix products, arithmetic and copies ran while one was open for 0% of the time, Pallas kernels for 7%

profile of v10, /device:TPU:30, one launch (start us, length us, event | category | flops | bytes accessed | tf_op | source)
XLA Modules:
  0.0 170.9 jit_solution(15442766715325372004)
XLA Ops:
  0.6 0.8 shard_map.121
  1.4 29.9 %all_to_all.35 = bf16[4,136,128]{2,1,0:T(8,128)(2,1)S(1)} all-to-all(bf16[4,136,128]{2,1,0:T(8,128)(2,1)S(1)} %shard_map.121), channel_id=1, replica_groups=mesh['zl'=4,'core'=2,'zh'=4,'y'=4,'x'=4] {'zh'}, dimensions={0} | all-to-all | bytes 278528 | tf_op jit(solution)/shard_map/all_to_all | solution.py:456
  31.4 10.8 %all_to_all.36 = bf16[4,4,136,128]{3,2,1,0:T(8,128)(2,1)S(1)} all-to-all(bf16[4,4,136,128]{3,2,1,0:T(8,128)(2,1)S(1)} %broadcast_in_dim.8), channel_id=1, replica_groups={{0,1,2,3},{4,5,6,7},{8,9,10,11},{12,13,14,15},{64,68,72,76},{65,69,73,7..., dimensions={0} | all-to-all | bytes 1114112 | tf_op jit(solution)/shard_map/all_to_all | solution.py:481
  42.5 19.8 %all_to_all.37 = bf16[4,4,4,136,128]{4,3,2,1,0:T(8,128)(2,1)S(1)} all-to-all(bf16[4,4,4,136,128]{4,3,2,1,0:T(8,128)(2,1)S(1)} %broadcast_in_dim.9), channel_id=1, replica_groups={{0,4,8,12},{1,5,9,13},{2,6,10,14},{3,7,11,15},{64,65,66,67},{68,69,70,7..., dimensions={0} | all-to-all | bytes 4456448 | tf_op jit(solution)/shard_map/all_to_all | solution.py:481
  62.3 1.9 %collective-permute-start.2 = (bf16[16,4,136,128]{3,2,1,0:T(8,128)(2,1)S(1)}, bf16[16,4,136,128]{3,2,1,0:T(8,128)(2,1)}, u32[]{:S(2)}, u32[]{:S(2)}) collective-permute-start(bf16[16,4,136,128]{3,2,1,0:T(8,128)(2,1)S(1)} %bitcast.9), channel_id=1, source_target_pairs={{0,64},{64,0},{1,65},{65,1},{2,66},{66,2},{3,67},{67,3},{4,68},{68... | collective-permute-start | bytes 6684680 | tf_op jit(solution)/shard_map/ppermute | solution.py:492
  64.2 7.7 %collective-permute-start.1 = (bf16[32,1024]{1,0:T(8,128)(2,1)S(1)}, bf16[32,1024]{1,0:T(8,128)(2,1)S(1)}, u32[]{:S(2)}, u32[]{:S(2)}) collective-permute-start(bf16[32,1024]{1,0:T(8,128)(2,1)S(1)} %get-tuple-element.54), channel_id=1, source_target_pairs={{1,2},{2,1},{3,4},{4,3},{5,6},{6,5},{7,8},{8,7},{9,10},{10,9},{11,... | collective-permute-start | bytes 196616 | tf_op jit(solution)/shard_map/ppermute | solution.py:461
  71.9 1.9 %collective-permute-start = (bf16[32,1024]{1,0:T(8,128)(2,1)S(1)}, bf16[32,1024]{1,0:T(8,128)(2,1)S(1)}, u32[]{:S(2)}, u32[]{:S(2)}) collective-permute-start(bf16[32,1024]{1,0:T(8,128)(2,1)S(1)} %get-tuple-element.55), channel_id=1, source_target_pairs={{0,1},{1,0},{2,3},{3,2},{4,5},{5,4},{6,7},{7,6},{8,9},{9,8},{10,11... | collective-permute-start | bytes 196616 | tf_op jit(solution)/shard_map/ppermute | solution.py:458
  74.0 0.6 broadcast_subtract_fusion.rel
  74.6 1.2 shard_map.120
  75.8 7.1 %collective-permute-done.1.across = bf16[32,1024]{1,0:T(8,128)(2,1)S(1)} collective-permute-done((bf16[32,1024]{1,0:T(8,128)(2,1)S(1)}, bf16[32,1024]{1,0:T(8,128)(2,1)S(1)}, u32[]{:S(2)}, u32[]{:S(2)}) %collective-permute-start.1) | collective-permute-done | bytes 65568 | tf_op jit(solution)/shard_map/ppermute | solution.py:461
  82.9 1.4 shard_map.122
  84.4 6.4 %shard_map.123 = (bf16[2,16,4,96,128]{4,3,2,1,0:T(8,128)(2,1)}, bf16[2,16,4,32,128]{4,3,2,1,0:T(8,128)(2,1)}, bf16[128,512]{1,0:T(8,128)(2,1)}, bf16[192,1024]{1...) custom-call(bf16[32,1024]{1,0:T(8,128)(2,1)S(1)} %get-tuple-element., ...), custom_call_target="tpu_custom_call" | custom-call | flops 2000000000 | bytes 10000000 | tf_op jit(solution)/shard_map/pallas_call | solution.py:63
  90.8 12.1 %all_to_all.38.every = bf16[8,128,128]{2,1,0:T(8,128)(2,1)S(1)} all-to-all(bf16[8,128,128]{2,1,0:T(8,128)(2,1)S(1)} %get-tuple-element.34), channel_id=1, replica_groups=mesh['zl'=4,'core'=2,'zh'=4,'y'=4,'x'=4] {'zl','core'}, dimensions={0} | all-to-all | bytes 524288 | tf_op jit(solution)/shard_map/all_to_all | solution.py:526
  102.9 1.2 shard_map.124
  104.1 12.3 %all_to_all.39.parts = bf16[16,4,24,128]{3,2,1,0:T(8,128)(2,1)S(1)} all-to-all(bf16[16,4,24,128]{3,2,1,0:T(8,128)(2,1)} %get-tuple-element.50), channel_id=1, replica_groups=mesh['zl'=4,'core'=2,'zh'=4,'y'=4,'x'=4] {'y','x'}, dimensions={0} | all-to-all | bytes 786432 | tf_op jit(solution)/shard_map/all_to_all | solution.py:538
  116.3 0.7 shard_map.127
  117.0 17.5 %all_to_all.40.parts = bf16[4,24,128]{2,1,0:T(8,128)(2,1)S(1)} all-to-all(bf16[4,24,128]{2,1,0:T(8,128)(2,1)} %shard_map.127), channel_id=1, replica_groups=mesh['zl'=4,'core'=2,'zh'=4,'y'=4,'x'=4] {'zh'}, dimensions={0} | all-to-all | bytes 49152 | tf_op jit(solution)/shard_map/all_to_all | solution.py:567
  135.1 3.3 %all-to-all-start.6 = ((bf16[8,24,128]{2,1,0:T(8,128)(2,1)}), bf16[8,24,128]{2,1,0:T(8,128)(2,1)S(1)}, u32[]{:S(2)}, u32[]{:S(2)}) async-start(bf16[8,24,128]{2,1,0:T(8,128)(2,1)} %shard_map.128), calls=%async_computation.6 | async-start | bytes 98304 | tf_op jit(solution)/shard_map/all_to_all | solution.py:576
  138.5 5.4 %shard_map.125 = (bf16[128,512]{1,0:T(8,128)(2,1)}, f32[128,1024]{1,0:T(8,128)}, bf16[32,1024]{1,0:T(8,128)(2,1)}, bf16[32,1024]{1,0:T(8,128)(2,1)}) custom-call(bf16[128,128]{1,0:T(8,128)(2,1)} %get-tuple-element.38.gf_in.gf, bf16[1024,128]{1,0:T(8,128)(2,1)} %get-tuple-element.39.whead_in.whead, bf16[2,16,4,32,128]{4,3,2,1,0:T(8,128)(2,1)} %get-tuple-element.41.raw_in, ...), custom_call_target="tpu_custom_call" | custom-call | flops 1000000000 | bytes 4000000 | tf_op jit(solution)/shard_map/pallas_call | solution.py:63
  143.9 2.7 %collective-permute-start.3 = (bf16[32,1024]{1,0:T(8,128)(2,1)}, bf16[32,1024]{1,0:T(8,128)(2,1)S(1)}, u32[]{:S(2)}, u32[]{:S(2)}) collective-permute-start(bf16[32,1024]{1,0:T(8,128)(2,1)} %get-tuple-element.47), channel_id=1, source_target_pairs={{0,1},{1,0},{2,3},{3,2},{4,5},{5,4},{6,7},{7,6},{8,9},{9,8},{10,11... | collective-permute-start | bytes 196616 | tf_op jit(solution)/shard_map/ppermute | solution.py:557
  146.6 5.9 %collective-permute-start.4 = (bf16[32,1024]{1,0:T(8,128)(2,1)}, bf16[32,1024]{1,0:T(8,128)(2,1)S(1)}, u32[]{:S(2)}, u32[]{:S(2)}) collective-permute-start(bf16[32,1024]{1,0:T(8,128)(2,1)} %get-tuple-element.48), channel_id=1, source_target_pairs={{1,2},{2,1},{3,4},{4,3},{5,6},{6,5},{7,8},{8,7},{9,10},{10,9},{11,... | collective-permute-start | bytes 196616 | tf_op jit(solution)/shard_map/ppermute | solution.py:558
  152.5 12.8 %collective-permute-done.4.across = bf16[32,1024]{1,0:T(8,128)(2,1)S(1)} collective-permute-done((bf16[32,1024]{1,0:T(8,128)(2,1)}, bf16[32,1024]{1,0:T(8,128)(2,1)S(1)}, u32[]{:S(2)}, u32[]{:S(2)}) %collective-permute-start.4) | collective-permute-done | bytes 65568 | tf_op jit(solution)/shard_map/ppermute | solution.py:558
  165.3 3.7 %shard_map.126 = (f32[128,1024]{1,0:T(8,128)}, bf16[128,1024]{1,0:T(8,128)(2,1)}) custom-call(bf16[128,1024]{1,0:T(8,128)(2,1)} %bitcast.12, f32[1,1024]{1,0:T(1,128)} %bitcast.17, bf16[128,128]{1,0:T(8,128)(2,1)} %get-tuple-element.38.gf_in.gf, bf16[1024,128]{1,0:T(8,128)(2,1)} %get-tuple-element.39.whead_in.whead, ...), custom_call_target="tpu_custom_call" | custom-call | flops 1000000000 | bytes 4000000 | tf_op jit(solution)/shard_map/pallas_call | solution.py:63
  169.0 1.8 %shard_map.129 = (f32[8,1024]{1,0:T(8,128)}, f32[16,128]{1,0:T(8,128)}) custom-call(bf16[8,24,128]{2,1,0:T(8,128)(2,1)S(1)} %all-to-all-done.6.parts, bf16[1024,128]{1,0:T(8,128)(2,1)} %get-tuple-element.39.whead_in.whead), custom_call_target="tpu_custom_call" | custom-call | flops 100000000 | bytes 1000000 | tf_op jit(solution)/shard_map/pallas_call | solution.py:63
  (17 shorter events, 1.1 us)
Async XLA Ops:
  42.5 21.7 %copy-start.1 = (bf16[1,128,1024]{2,1,0:T(8,128)(2,1)S(1)}, bf16[1,128,1024]{2,1,0:T(8,128)(2,1)}, u32[]{:S(2)}) copy-start(bf16[1,128,1024]{2,1,0:T(8,128)(2,1)} %param.9) | copy-start | bytes 786436
  42.5 31.4 %copy-start.3 = (s32[128,8]{0,1:T(8,128)S(1)}, s32[128,8]{0,1:T(8,128)}, u32[]{:S(2)}) copy-start(s32[128,8]{0,1:T(8,128)} %param.16) | copy-start | bytes 12292
  62.3 22.1 %collective-permute-start.2 = (bf16[16,4,136,128]{3,2,1,0:T(8,128)(2,1)S(1)}, bf16[16,4,136,128]{3,2,1,0:T(8,128)(2,1)}, u32[]{:S(2)}, u32[]{:S(2)}) collective-permute-start(bf16[16,4,136,128]{3,2,1,0:T(8,128)(2,1)S(1)} %bitcast.9), channel_id=1, source_target_pairs={{0,64},{64,0},{1,65},{65,1},{2,66},{66,2},{3,67},{67,3},{4,68},{68... | collective-permute-start | bytes 6684680 | tf_op jit(solution)/shard_map/ppermute | solution.py:492
  64.2 18.7 %collective-permute-start.1 = (bf16[32,1024]{1,0:T(8,128)(2,1)S(1)}, bf16[32,1024]{1,0:T(8,128)(2,1)S(1)}, u32[]{:S(2)}, u32[]{:S(2)}) collective-permute-start(bf16[32,1024]{1,0:T(8,128)(2,1)S(1)} %get-tuple-element.54), channel_id=1, source_target_pairs={{1,2},{2,1},{3,4},{4,3},{5,6},{6,5},{7,8},{8,7},{9,10},{10,9},{11,... | collective-permute-start | bytes 196616 | tf_op jit(solution)/shard_map/ppermute | solution.py:461
  71.9 11.0 %collective-permute-start = (bf16[32,1024]{1,0:T(8,128)(2,1)S(1)}, bf16[32,1024]{1,0:T(8,128)(2,1)S(1)}, u32[]{:S(2)}, u32[]{:S(2)}) collective-permute-start(bf16[32,1024]{1,0:T(8,128)(2,1)S(1)} %get-tuple-element.55), channel_id=1, source_target_pairs={{0,1},{1,0},{2,3},{3,2},{4,5},{5,4},{6,7},{7,6},{8,9},{9,8},{10,11... | collective-permute-start | bytes 196616 | tf_op jit(solution)/shard_map/ppermute | solution.py:458
  84.4 18.5 %copy-start.2 = (f32[128,128]{1,0:T(8,128)S(1)}, f32[128,128]{1,0:T(8,128)}, u32[]{:S(2)}) copy-start(f32[128,128]{1,0:T(8,128)} %observed.1) | copy-start | bytes 196612
  116.3 49.0 %copy-start = (bf16[2,16,4,96,128]{4,3,2,1,0:T(8,128)(2,1)S(1)}, bf16[2,16,4,96,128]{4,3,2,1,0:T(8,128)(2,1)}, u32[]{:S(2)}) copy-start(bf16[2,16,4,96,128]{4,3,2,1,0:T(8,128)(2,1)} %get-tuple-element.40.raw) | copy-start | bytes 9437188
  135.1 33.9 %all-to-all-start.6 = ((bf16[8,24,128]{2,1,0:T(8,128)(2,1)}), bf16[8,24,128]{2,1,0:T(8,128)(2,1)S(1)}, u32[]{:S(2)}, u32[]{:S(2)}) async-start(bf16[8,24,128]{2,1,0:T(8,128)(2,1)} %shard_map.128), calls=%async_computation.6 | async-start | bytes 98304 | tf_op jit(solution)/shard_map/all_to_all | solution.py:576
  143.9 8.6 %collective-permute-start.3 = (bf16[32,1024]{1,0:T(8,128)(2,1)}, bf16[32,1024]{1,0:T(8,128)(2,1)S(1)}, u32[]{:S(2)}, u32[]{:S(2)}) collective-permute-start(bf16[32,1024]{1,0:T(8,128)(2,1)} %get-tuple-element.47), channel_id=1, source_target_pairs={{0,1},{1,0},{2,3},{3,2},{4,5},{5,4},{6,7},{7,6},{8,9},{9,8},{10,11... | collective-permute-start | bytes 196616 | tf_op jit(solution)/shard_map/ppermute | solution.py:557
  146.6 18.7 %collective-permute-start.4 = (bf16[32,1024]{1,0:T(8,128)(2,1)}, bf16[32,1024]{1,0:T(8,128)(2,1)S(1)}, u32[]{:S(2)}, u32[]{:S(2)}) collective-permute-start(bf16[32,1024]{1,0:T(8,128)(2,1)} %get-tuple-element.48), channel_id=1, source_target_pairs={{1,2},{2,1},{3,4},{4,3},{5,6},{6,5},{7,8},{8,7},{9,10},{10,9},{11,... | collective-permute-start | bytes 196616 | tf_op jit(solution)/shard_map/ppermute | solution.py:558
